TPU v7x, 128 devices: a whole 4x4x4 slice. The times are simulated.
128 devices in a mesh: path: 8 (over y, core), fsdp: 16 (over z, x).
Axes of the slice: x: 4, y: 4, z: 4, core: 2. Of those that a mesh axis runs over, the one named last changes fastest.
Arguments:
- input_activation_matrix: bfloat16 [8, 3072, 2048], P('path', 'fsdp'), may hold values from -6 to 6
- output_sensitivity: bfloat16 [8, 3072, 2048], P('path', 'fsdp'), may hold values from -12 to 12
- trajectory_initial_parameters: bfloat16 [8, 8, 1024, 4096], P('path', None, 'fsdp'), may hold values from -6 to 6
- trajectory_gradient_average: bfloat16 [8, 8, 1024, 4096], P('path', None, 'fsdp'), may hold values from -0.19921875 to 0.19921875
- trajectory_squared_average: bfloat16 [8, 8, 1024, 4096], P('path', None, 'fsdp'), may hold values from 0.0009994507 to 0.099609375
- common_expert_parameters: float32 [8, 2, 1024, 4096], P('path', None, 'fsdp'), may hold values from -6 to 6
- outer_inertia: float32 [8, 2, 1024, 4096], P('path', None, 'fsdp'), may hold values from -0.4 to 0.4
- trajectory_membership: int32 [8, 8], replicated, may hold values from 0 to 1
- punctual_flags: int32 [8], replicated, may hold values 0 or 1
Outputs:
- refreshed_experts: float32 [8, 2, 1024, 4096], P('path', None, 'fsdp')
- refreshed_inertia: float32 [8, 2, 1024, 4096], P('path', None, 'fsdp')
- returned: bfloat16 [8, 8, 1024, 4096], P('path', None, 'fsdp')
All inputs are finite; a program needn't handle non-finite values.
Results may differ from a plain program's by a relative error of at most 0.0024.
Values may be sent and summed in bfloat16 or wider, within the bound.
No kernel may reach another device: no remote copies, remote signals or barrier semaphores. Data moves between devices by JAX's collectives and lax.ppermute only.
A program may use at most 320 MiB of HBM per device.

v0:
```python
import functools

import jax
import jax.numpy as jnp
from jax import lax
from jax.experimental import pallas as pl
from jax.experimental.pallas import tpu as pltpu
from jax.sharding import PartitionSpec as P

UNIT = 1024
SETS = 8
STEP = 1000


BETA_ONE = 0.9
BETA_TWO = 0.999
ADAM_EPS = 1e-08
INNER_RATE = 0.05
DECAY = 0.1
GLOBAL_LEARNING = 0.7
INERTIA_FACTOR = 0.9

ZS, XS, YS = 4, 4, 4
GELU_C = 0.7978845608028654
GELU_A = 0.044715
NT = (((1,), (1,)), ((), ()))
F32 = jnp.float32
BF16 = jnp.bfloat16
COLS = 512
CHUNK = 256
LIMIT = 46 << 20


def plane_hop(da, db):
    pairs = []
    for p in range(2 * YS):
        dz, dx = (da, db) if p % 2 == 0 else (db, da)
        for z in range(ZS):
            for x in range(XS):
                to = ((z + dz) % ZS) * XS + (x + dx) % XS
                pairs.append((p * ZS * XS + z * XS + x, p * ZS * XS + to))
    return pairs


def path_hop(hop, flip):
    return [
        (i, ((i // 2 + (hop if i % 2 == 0 else -hop)) % YS) * 2 + ((i % 2) ^ flip))
        for i in range(2 * YS)
    ]


def on_path(a, hop, flip=0):
    return lax.ppermute(a, "path", path_hop(hop, flip))


def after(a, *others):
    return lax.optimization_barrier((a, *others))[0]


def gather_tokens(own, compute):
    def send(a, to, *others):
        if others:
            a = after(a, *others)
        return lax.ppermute(a, ("path", "fsdp"), plane_hop(*to))

    half = own.shape[0] // 2
    got = {(0, 0): own}
    got[0, -1], got[0, 1] = send(own, (0, 1)), send(own, (0, -1))
    got[-1, 0], got[1, 0] = send(own, (1, 0)), send(own, (-1, 0))
    low = send(got[0, -1][:half], (0, 1))
    high = send(got[0, 1][half:], (0, -1))
    got[-1, -1] = send(got[0, -1], (1, 0), got[0, 1])
    got[1, -1] = send(got[0, -1], (-1, 0), got[0, 1])
    got[0, 2] = jnp.concatenate([low, high], 0)
    hold = {3: compute(0, got)}
    ups = [(-1, 0), (-1, -1), (-1, 1), (-1, 2), (2, 0), (2, -1)]
    downs = [(1, 0), (1, -1), (1, 1), (1, 2), (2, 1), (2, 2)]
    for j in range(2, 6):
        a, b = ups[j]
        c, d = downs[j]
        wait = [got[ups[j - 2]], got[downs[j - 2]]]
        if j == 2:
            wait += [low, high]
        if j == 4:
            hold[4] = compute(1, got)
        if j in hold:
            wait.append(hold[j])
        got[a, b] = send(got[0 if a == -1 else -1, b], (1, 0), *wait)
        got[c, d] = send(got[0 if c == 1 else 1, d], (-1, 0), *wait)
    compute(2, got)
    compute(3, got)
    return got


def hidden_both(xg, w, act_t, dpre_t, features, hidden_scale):
    in_scale = features ** (-0.5)
    tokens = xg.shape[0]
    size = CHUNK if tokens % CHUNK == 0 else tokens

    def chunk(t, carry):
        rows = pl.ds(pl.multiple_of(t * size, size), size)
        pre = (
            lax.dot_general(w[:, :features], xg[rows, :features], NT, preferred_element_type=F32)
            * in_scale
        )
        back = (
            lax.dot_general(w[:, features:], xg[rows, features:], NT, preferred_element_type=F32)
            * hidden_scale
        )
        sq = pre * pre
        t_ = jnp.tanh(GELU_C * pre * (1.0 + GELU_A * sq))
        cdf = 0.5 * (1.0 + t_)
        slope = cdf + (0.5 * GELU_C) * pre * (1.0 - t_ * t_) * (1.0 + (3.0 * GELU_A) * sq)
        act_t[:, rows] = (pre * cdf).astype(BF16)
        dpre_t[:, rows] = (back * slope).astype(BF16)
        return carry

    lax.fori_loop(0, tokens // size, chunk, 0)


def fetch(refs, dst, sem, cols=slice(None)):
    copies, at = [], 0
    for k, p in enumerate(refs):
        rows = pl.ds(at, p.shape[0])
        copies.append(pltpu.make_async_copy(p.at[:, cols], dst.at[rows, :], sem.at[k]))
        at += p.shape[0]
    for c in copies:
        c.start()
    for c in copies:
        c.wait()


def grads_kernel(n, first, features, hidden_scale, *refs):
    w, acc = refs[n], None if first else refs[n + 1]
    out, xg, act_t, dpre_t, sem = refs[-5:]
    fetch(refs[:n], xg, sem)
    hidden_both(xg, w, act_t, dpre_t, features, hidden_scale)
    for left, base in ((dpre_t, 0), (act_t, features)):

        def columns(j, carry, left=left, base=base):
            cols = pl.ds(pl.multiple_of(base + j * COLS, COLS), COLS)
            term = jnp.dot(left[...], xg[:, cols], preferred_element_type=F32)
            out[:, cols] = term if first else acc[:, cols] + term
            return carry

        lax.fori_loop(0, features // COLS, columns, 0)


ANY = pl.BlockSpec(memory_space=pl.ANY)
HBM = pl.BlockSpec(memory_space=pltpu.HBM)
VMEM = pl.BlockSpec(memory_space=pltpu.VMEM)


def resident(a):
    return pltpu.with_memory_space_constraint(a, pltpu.VMEM)


def accumulate(pieces, w, acc, hidden_scale):
    n = len(pieces)
    units, width = w.shape
    features = width // 2
    tokens = sum(p.shape[0] for p in pieces)
    first = acc is None
    return pl.pallas_call(
        functools.partial(grads_kernel, n, first, features, hidden_scale),
        in_specs=[HBM] * n + [VMEM] * (1 if first else 2),
        out_specs=VMEM,
        out_shape=pltpu.VMEM((units, width), F32),
        scratch_shapes=[
            pltpu.VMEM((tokens, width), BF16),
            pltpu.VMEM((units, tokens), BF16),
            pltpu.VMEM((units, tokens), BF16),
            pltpu.SemaphoreType.DMA((n,)),
        ],
        input_output_aliases={} if first else {n + 1: 0},
        compiler_params=pltpu.CompilerParams(vmem_limit_bytes=LIMIT),
        cost_estimate=pl.CostEstimate(
            flops=8 * tokens * units * features,
            bytes_accessed=tokens * width * 2,
            transcendentals=units * tokens,
        ),
        name="grads",
    )(*pieces, w, *(() if first else (acc,)))


def adam(total, scale, first, second, start):
    corr_one = 1.0 - BETA_ONE**STEP
    corr_two = 1.0 - BETA_TWO**STEP
    raw = total * scale
    first_new = (INNER_RATE * BETA_ONE / corr_one) * first.astype(F32) + (
        INNER_RATE * (1.0 - BETA_ONE) / corr_one
    ) * raw
    second_new = (BETA_TWO / corr_two) * second.astype(F32) + (
        (1.0 - BETA_TWO) / corr_two
    ) * (raw * raw)
    root = second_new * lax.rsqrt(second_new)
    return (first_new / (root + ADAM_EPS) + (INNER_RATE * DECAY) * start.astype(F32)).astype(BF16)


def pseudo_kernel(n, lead, features, hidden_scale, *refs):
    where, pieces = refs[0], refs[1 : 1 + n]
    if lead:
        w, acc, m, v, keep, swap, act_t, total, dpre_t, right, sem = refs[1 + n :]
        fetch(pieces, right, sem)
        hidden_both(right, w, act_t, dpre_t, features, hidden_scale)
        left, base, scale = dpre_t, 0, features ** (-0.5)
    else:
        left, w, acc, m, v, keep, swap, total, right, sem = refs[1 + n :]
        base, scale = features, hidden_scale
        fetch(pieces, right, sem, pl.ds(base, features))
    y, core = where[0], where[1]
    rows = w.shape[0] // SETS

    def columns(j, carry):
        here = pl.ds(pl.multiple_of(j * COLS, COLS), COLS)
        cols = pl.ds(pl.multiple_of(base + j * COLS, COLS), COLS)
        total[...] = acc[:, cols] + jnp.dot(left[...], right[:, here], preferred_element_type=F32)

        def ring(d, carry):
            for out, parity in ((keep, core), (swap, 1 - core)):
                chip = lax.rem(y + jnp.where(parity == 0, d, YS - d), YS)
                at = pl.ds(pl.multiple_of((2 * chip + parity) * rows, rows), rows)
                out[d, :, here] = adam(total[at, :], scale, m[at, cols], v[at, cols], w[at, cols])
            return carry

        return lax.fori_loop(0, YS, ring, carry)

    lax.fori_loop(0, features // COLS, columns, 0)


def last_pseudo(lead, where, pieces, act, w, acc, m, v, hidden_scale):
    n = len(pieces)
    units, width = w.shape
    features = width // 2
    tokens = sum(p.shape[0] for p in pieces)
    hid = (units, tokens)
    out_shape = [pltpu.VMEM((YS, units // SETS, features), BF16)] * 2
    scratch = [pltpu.VMEM((units, COLS), F32)]
    if lead:
        out_shape.append(pltpu.VMEM(hid, BF16))
        scratch += [pltpu.VMEM(hid, BF16), pltpu.VMEM((tokens, width), BF16)]
    else:
        scratch += [pltpu.VMEM((tokens, features), BF16)]
    tail = (() if lead else (act,)) + (w, acc, m, v)
    return pl.pallas_call(
        functools.partial(pseudo_kernel, n, lead, features, hidden_scale),
        in_specs=[pl.BlockSpec(memory_space=pltpu.SMEM)] + [HBM] * n + [VMEM] * len(tail),
        out_specs=[VMEM] * len(out_shape),
        scratch_shapes=scratch + [pltpu.SemaphoreType.DMA((n,))],
        out_shape=out_shape,
        compiler_params=pltpu.CompilerParams(vmem_limit_bytes=LIMIT),
        cost_estimate=pl.CostEstimate(
            flops=(6 if lead else 2) * tokens * units * features,
            bytes_accessed=units * features * 12 + tokens * width * 2,
            transcendentals=units * tokens,
        ),
        name="pseudo_in" if lead else "pseudo_out",
    )(where, *pieces, *tail)


def assemble_kernel(halves, *refs):
    info = refs[0]
    out, sem = refs[-2:]
    ins = refs[1:-2]
    y, core = info[0], info[1]
    per = len(ins) // halves
    span = out.shape[2] // halves
    copies = []

    def copy(src, s, lo, n):
        dst = out.at[s, :, pl.ds(lo, n)]
        c = pltpu.make_async_copy(src, dst, sem.at[len(copies)])
        c.start()
        copies.append(c)

    def home(d, parity):
        return 2 * lax.rem(y + jnp.where(parity == 0, d, YS - d), YS) + parity

    for h in range(halves):
        own, nxt, far_l, far_r, prv, other = ins[h * per : (h + 1) * per]
        at = h * span
        copy(own.at[info[2]], home(0, core), at, span)
        copy(nxt.at[info[3]], home(1, core), at, span)
        copy(far_l.at[info[4]], home(2, core), at, span // 2)
        copy(far_r.at[info[4]], home(2, core), at + span // 2, span // 2)
        copy(prv.at[info[5]], home(3, core), at, span)
        for d in range(YS):
            copy(other.at[d], home(d, 1 - core), at, span)
    for c in copies:
        c.wait()


def assemble(info, pieces, rows, width):
    halves = len(pieces)
    flat = [a for p in pieces for a in p]
    return pl.pallas_call(
        functools.partial(assemble_kernel, halves),
        grid_spec=pltpu.PrefetchScalarGridSpec(
            num_scalar_prefetch=1,
            grid=(1,),
            in_specs=[pl.BlockSpec(memory_space=pltpu.VMEM)] * len(flat),
            out_specs=ANY,
            scratch_shapes=[pltpu.SemaphoreType.DMA((9 * halves,))],
        ),
        out_shape=jax.ShapeDtypeStruct((SETS, rows, width), BF16),
        name="assemble",
    )(info, *flat)


def per_device(
    input_activation_matrix,
    output_sensitivity,
    trajectory_initial_parameters,
    trajectory_gradient_average,
    trajectory_squared_average,
    common_expert_parameters,
    outer_inertia,
    trajectory_membership,
    punctual_flags,
):
    set_count, rows, width = trajectory_initial_parameters.shape[1:]
    units = set_count * rows
    features = width // 2
    hidden_scale = (SETS * UNIT) ** (-0.5)
    w = trajectory_initial_parameters[0].reshape(units, width)
    m = trajectory_gradient_average[0].reshape(units, width)
    v = trajectory_squared_average[0].reshape(units, width)

    me = lax.axis_index("path")
    y, core = me // 2, me % 2
    choices = common_expert_parameters.shape[1]
    eligible = jnp.arange(choices, dtype=jnp.int32)
    chosen = jnp.where(
        (trajectory_membership[:, :, None] == eligible[None, None, :])
        & (punctual_flags[:, None, None] == 1),
        1.0,
        0.0,
    ).astype(F32)
    steps = jnp.arange(YS, dtype=jnp.int32)
    ring_sets = 2 * ((y + jnp.where(core == 0, steps, YS - steps)) % YS) + core
    mine = chosen[me][ring_sets]
    mates = chosen[me ^ 1][ring_sets]
    tally = jnp.sum(chosen[:, me], axis=0)
    share = jnp.maximum(tally, 1.0)[:, None, None]
    own_pick = trajectory_membership[me][ring_sets]
    mate_pick = trajectory_membership[me ^ 1][ring_sets]
    where = jnp.stack([y, core]).astype(jnp.int32)

    calls = (
        ((0, 0), (0, -1), (0, 1), (0, 2)),
        ((-1, 0), (1, 0), (-1, -1), (1, -1)),
        ((-1, 1), (1, 1), (-1, 2), (1, 2)),
        ((2, 0), (2, 1)),
    )
    small = (where, mine, mates, share, own_pick, mate_pick)
    w, where, mine, mates, share, own_pick, mate_pick = lax.optimization_barrier((w, *small))
    w, m, v = resident(w), resident(m), resident(v)
    acc = None

    def compute(k, got):
        nonlocal acc
        acc = accumulate([got[b] for b in calls[k]], w, acc, hidden_scale)
        return acc

    own = jnp.concatenate([input_activation_matrix[0], output_sensitivity[0]], 1)
    got = gather_tokens(own, compute)
    rest = [got[2, -1], got[2, 2]]
    keep_in, swap_in, act = last_pseudo(True, where, rest, None, w, acc, m, v, hidden_scale)
    keep_out, swap_out = last_pseudo(False, where, rest, act, w, acc, m, v, hidden_scale)

    common = common_expert_parameters[0]
    inertia = outer_inertia[0]
    mid = features // 2

    def refreshed(average, common, inertia):
        new_inertia = INERTIA_FACTOR * inertia + average
        return common - GLOBAL_LEARNING * (average + INERTIA_FACTOR * new_inertia), new_inertia

    totals, pieces = [], []
    mate = None
    for h, (keep, swap) in enumerate(((keep_in, swap_in), (keep_out, swap_out))):
        mate = on_path(swap if mate is None else after(swap, mate), 0, 1)

        def both(d, lo=0, hi=features, keep=keep, mate=mate):
            a = keep[d, :, lo:hi].astype(F32)[None]
            b = mate[d, :, lo:hi].astype(F32)[None]
            return mine[d][:, None, None] * a + mates[d][:, None, None] * b

        from_prv = on_path(both(2, 0, mid).astype(BF16), 1)
        from_nxt = on_path(both(2, mid, features).astype(BF16), -1)
        up = jnp.concatenate([both(1, 0, mid) + from_prv.astype(F32), both(1, mid, features)], -1)
        down = jnp.concatenate([both(3, 0, mid), both(3, mid, features) + from_nxt.astype(F32)], -1)
        part_up = on_path(up.astype(BF16), 1)
        part_down = on_path(down.astype(BF16), -1)
        total = both(0) + part_up.astype(F32) + part_down.astype(F32)
        totals.append(total)
        cols = slice(h * features, (h + 1) * features)
        experts, _ = refreshed(total / share, common[..., cols], inertia[..., cols])
        updated = experts.astype(BF16)
        prv, nxt = on_path(updated, 1), on_path(updated, -1)
        far_l = on_path(prv[..., :mid], 1)
        far_r = on_path(nxt[..., mid:], -1)
        far = jnp.concatenate([far_l, far_r], -1)
        chosen_for_mate = jnp.stack(
            [
                jnp.where(mate_pick[d] == 1, a[1], a[0])
                for d, a in enumerate((updated, nxt, far, prv))
            ]
        )
        other = on_path(chosen_for_mate, 0, 1)
        pieces.append((updated, nxt, far_l, far_r, prv, other))

    average = jnp.concatenate(totals, -1) / share
    new_experts, new_inertia = refreshed(average, common, inertia)
    info = jnp.concatenate([where, own_pick]).astype(jnp.int32)
    returned = assemble(info, pieces, rows, width)
    return (new_experts[None], new_inertia[None], returned[None])


def solution(mesh):
    placed = (
        P("path", "fsdp", None),
        P("path", "fsdp", None),
        P("path", None, "fsdp", None),
        P("path", None, "fsdp", None),
        P("path", None, "fsdp", None),
        P("path", None, "fsdp", None),
        P("path", None, "fsdp", None),
        P(),
        P(),
    )
    return jax.shard_map(
        per_device,
        mesh=mesh,
        in_specs=placed,
        out_specs=(
            P("path", None, "fsdp", None),
            P("path", None, "fsdp", None),
            P("path", None, "fsdp", None),
        ),
        check_vma=False,
    )
```

profile of v0, /device:TPU:1, one launch (start us, length us, event | category | flops | bytes accessed | tf_op | source)
XLA Modules:
  0.0 273.4 jit_solution(4704848670319312703)
XLA Ops:
  2.1 4.7 %collective-permute-start.1 = (bf16[192,4096]{1,0:T(8,128)(2,1)S(1)}, bf16[192,4096]{1,0:T(8,128)(2,1)}, u32[]{:S(2)}, u32[]{:S(2)}) collective-permute-start(bf16[192,4096]{1,0:T(8,128)(2,1)S(1)} %pad_maximum_fusion.refs_0_), channel_id=1, source_target_pairs={{0,3},{1,0},{2,1},{3,2},{4,7},{5,4},{6,5},{7,6},{8,11},{9,8},{10,9... | collective-permute-start | bytes 4718600 | tf_op jit(solution)/shard_map/ppermute | solution.py:64
  9.6 27.5 %collective-permute-done.1.refs_2_ = bf16[192,4096]{1,0:T(8,128)(2,1)} collective-permute-done((bf16[192,4096]{1,0:T(8,128)(2,1)S(1)}, bf16[192,4096]{1,0:T(8,128)(2,1)}, u32[]{:S(2)}, u32[]{:S(2)}) %collective-permute-start.1) | collective-permute-done | bytes 1572896 | tf_op jit(solution)/shard_map/ppermute | solution.py:64
  39.1 3.5 %collective-permute-start.4 = (bf16[96,4096]{1,0:T(8,128)(2,1)}, bf16[96,4096]{1,0:T(8,128)(2,1)}, u32[]{:S(2)}, u32[]{:S(2)}) collective-permute-start(bf16[96,4096]{1,0:T(8,128)(2,1)} %slice.297), channel_id=1, source_target_pairs={{0,3},{1,0},{2,1},{3,2},{4,7},{5,4},{6,5},{7,6},{8,11},{9,8},{10,9... | collective-permute-start | bytes 2359304 | tf_op jit(solution)/shard_map/ppermute | solution.py:64
  51.9 11.4 %collective-permute-done.3 = bf16[96,4096]{1,0:T(8,128)(2,1)} collective-permute-done((bf16[96,4096]{1,0:T(8,128)(2,1)}, bf16[96,4096]{1,0:T(8,128)(2,1)}, u32[]{:S(2)}, u32[]{:S(2)}) %collective-permute-start.3) | collective-permute-done | bytes 786464 | tf_op jit(solution)/shard_map/ppermute | solution.py:64
  63.3 5.4 %collective-permute-start.12 = (bf16[192,4096]{1,0:T(8,128)(2,1)}, bf16[192,4096]{1,0:T(8,128)(2,1)S(1)}, u32[]{:S(2)}, u32[]{:S(2)}) collective-permute-start(bf16[192,4096]{1,0:T(8,128)(2,1)} %collective-permute-done.1.refs_2_), channel_id=1, source_target_pairs={{0,4},{1,5},{2,6},{3,7},{4,8},{5,9},{6,10},{7,11},{8,12},{9,13},{1... | collective-permute-start | bytes 4718600 | tf_op jit(solution)/shard_map/ppermute | solution.py:64
  75.0 12.1 %grads.4.refs_5_ = f32[512,4096]{1,0:T(8,128)S(1)} custom-call(bf16[192,4096]{1,0:T(8,128)(2,1)} %copy-done.16, bf16[192,4096]{1,0:T(8,128)(2,1)} %collective-permute-done.refs_1_, bf16[192,4096]{1,0:T(8,128)(2,1)} %collective-permute-done.1.refs_2_, bf16[192,4096]{1,0:T(8,128)(2,1)} %constant_dynamic-update-slice_fusion.refs_3_, bf16[512,4096]{1,0:T(8,128)(2,1)S(1)} %bitcast.159), custom_call_target="tpu_custom_call" | custom-call | flops 6442450944 | bytes 6291456 | tf_op jit(solution)/shard_map/grads/pallas_call | solution.py:164
  89.9 12.5 %grads.5.refs_5_ = f32[512,4096]{1,0:T(8,128)S(1)} custom-call(bf16[192,4096]{1,0:T(8,128)(2,1)} %collective-permute-done.10.refs_0_, bf16[192,4096]{1,0:T(8,128)(2,1)} %copy-done.17, bf16[192,4096]{1,0:T(8,128)(2,1)} %collective-permute-done.2.refs_2_, bf16[192,4096]{1,0:T(8,128)(2,1)} %collective-permute-done.5.refs_3_, ...), custom_call_target="tpu_custom_call", output_to_operand_aliasing={{}: (5, {})} | custom-call | flops 6442450944 | bytes 6291456 | tf_op jit(solution)/shard_map/grads/pallas_call | solution.py:164
  104.0 5.1 %collective-permute-done.6.refs_2_ = bf16[192,4096]{1,0:T(8,128)(2,1)S(1)} collective-permute-done((bf16[192,4096]{1,0:T(8,128)(2,1)}, bf16[192,4096]{1,0:T(8,128)(2,1)S(1)}, u32[]{:S(2)}, u32[]{:S(2)}) %collective-permute-start.6) | collective-permute-done | bytes 1572896 | tf_op jit(solution)/shard_map/ppermute | solution.py:64
  111.7 12.5 %grads.6.refs_3_ = f32[512,4096]{1,0:T(8,128)S(1)} custom-call(bf16[192,4096]{1,0:T(8,128)(2,1)} %copy-done.18, bf16[192,4096]{1,0:T(8,128)(2,1)} %collective-permute-done.13.refs_1_, bf16[192,4096]{1,0:T(8,128)(2,1)} %copy-done.19, bf16[192,4096]{1,0:T(8,128)(2,1)} %collective-permute-done.7.refs_3_, ...), custom_call_target="tpu_custom_call", output_to_operand_aliasing={{}: (5, {})} | custom-call | flops 6442450944 | bytes 6291456 | tf_op jit(solution)/shard_map/grads/pallas_call | solution.py:164
  126.6 8.2 %grads.7.refs_4_.refs_5_ = f32[512,4096]{1,0:T(8,128)S(1)} custom-call(bf16[192,4096]{1,0:T(8,128)(2,1)} %collective-permute-done.14.refs_0_, bf16[192,4096]{1,0:T(8,128)(2,1)} %copy-done.15, bf16[512,4096]{1,0:T(8,128)(2,1)S(1)} %bitcast.162, f32[512,4096]{1,0:T(8,128)S(1)} %grads.6.refs_3_), custom_call_target="tpu_custom_call", output_to_operand_aliasing={{}: (3, {})} | custom-call | flops 3221225472 | bytes 3145728 | tf_op jit(solution)/shard_map/grads/pallas_call | solution.py:164
  134.8 3.3 %copy-done = f32[512,4096]{1,0:T(8,128)} copy-done((f32[512,4096]{1,0:T(8,128)}, f32[512,4096]{1,0:T(8,128)S(1)}, u32[]{:S(2)}) %copy-start) | copy-done | bytes 8388632
  138.1 4.0 %collective-permute-done.9.refs_2_ = bf16[192,4096]{1,0:T(8,128)(2,1)S(1)} collective-permute-done((bf16[192,4096]{1,0:T(8,128)(2,1)}, bf16[192,4096]{1,0:T(8,128)(2,1)S(1)}, u32[]{:S(2)}, u32[]{:S(2)}) %collective-permute-start.9) | collective-permute-done | bytes 1572896 | tf_op jit(solution)/shard_map/ppermute | solution.py:64
  148.4 12.4 %pseudo_in.1 = (bf16[4,64,2048]{2,1,0:T(8,128)(2,1)S(1)}, bf16[4,64,2048]{2,1,0:T(8,128)(2,1)S(1)}, bf16[512,384]{1,0:T(8,128)(2,1)S(1)}) custom-call(s32[2]{0:T(128)} %pad_add_fusion.refs_0_, bf16[192,4096]{1,0:T(8,128)(2,1)} %copy-done.8, bf16[192,4096]{1,0:T(8,128)(2,1)} %copy-done.7, bf16[512,4096]{1,0:T(8,128)(2,1)S(1)} %bitcast.163, ...), custom_call_target="tpu_custom_call" | custom-call | flops 2415919104 | bytes 15728640 | tf_op jit(solution)/shard_map/pseudo_in/pallas_call | solution.py:245
  161.5 5.2 %collective-permute-start.16 = (bf16[4,64,2048]{2,1,0:T(8,128)(2,1)S(1)}, bf16[4,64,2048]{2,1,0:T(8,128)(2,1)S(1)}, u32[]{:S(2)}, u32[]{:S(2)}) collective-permute-start(bf16[4,64,2048]{2,1,0:T(8,128)(2,1)S(1)} %get-tuple-element.35), channel_id=1, source_target_pairs={{0,16},{16,0},{32,48},{48,32},{64,80},{80,64},{96,112},{112,96},{1... | collective-permute-start | bytes 3145736 | tf_op jit(solution)/shard_map/ppermute | solution.py:53
  166.7 9.5 %pseudo_out.1 = (bf16[4,64,2048]{2,1,0:T(8,128)(2,1)S(1)}, bf16[4,64,2048]{2,1,0:T(8,128)(2,1)S(1)}) custom-call(s32[2]{0:T(128)} %pad_add_fusion.refs_0_, bf16[192,4096]{1,0:T(8,128)(2,1)} %copy-done.8, bf16[192,4096]{1,0:T(8,128)(2,1)} %copy-done.7, bf16[512,384]{1,0:T(8,128)(2,1)} %copy-done.4, bf16[512,4096]{1,0:T(8,128)(2,1)S(1)} %bitcast.164, ...), custom_call_target="tpu_custom_call" | custom-call | flops 805306368 | bytes 15728640 | tf_op jit(solution)/shard_map/pseudo_out/pallas_call | solution.py:245
  187.3 5.4 %collective-permute-done.22 = bf16[2,64,1024]{2,1,0:T(8,128)(2,1)S(1)} collective-permute-done((bf16[2,64,1024]{2,1,0:T(8,128)(2,1)S(1)}, bf16[2,64,1024]{2,1,0:T(8,128)(2,1)S(1)}, u32[]{:S(2)}, u32[]{:S(2)}) %collective-permute-start.22) | collective-permute-done | bytes 262176 | tf_op jit(solution)/shard_map/ppermute | solution.py:53
  193.2 3.5 %collective-permute-start.18 = (bf16[2,64,2048]{2,1,0:T(8,128)(2,1)S(1)}, bf16[2,64,2048]{2,1,0:T(8,128)(2,1)S(1)}, u32[]{:S(2)}, u32[]{:S(2)}) collective-permute-start(bf16[2,64,2048]{2,1,0:T(8,128)(2,1)S(1)} %pad_maximum_fusion.3), channel_id=1, source_target_pairs={{0,32},{16,112},{32,64},{48,16},{64,96},{80,48},{96,0},{112,80},{1... | collective-permute-start | bytes 1572872 | tf_op jit(solution)/shard_map/ppermute | solution.py:53
  200.8 3.5 %collective-permute-done.18 = bf16[2,64,2048]{2,1,0:T(8,128)(2,1)S(1)} collective-permute-done((bf16[2,64,2048]{2,1,0:T(8,128)(2,1)S(1)}, bf16[2,64,2048]{2,1,0:T(8,128)(2,1)S(1)}, u32[]{:S(2)}, u32[]{:S(2)}) %collective-permute-start.18) | collective-permute-done | bytes 524320 | tf_op jit(solution)/shard_map/ppermute | solution.py:53
  204.3 8.4 %collective-permute-done.20 = bf16[2,64,2048]{2,1,0:T(8,128)(2,1)S(1)} collective-permute-done((bf16[2,64,2048]{2,1,0:T(8,128)(2,1)S(1)}, bf16[2,64,2048]{2,1,0:T(8,128)(2,1)S(1)}, u32[]{:S(2)}, u32[]{:S(2)}) %collective-permute-start.20) | collective-permute-done | bytes 524320 | tf_op jit(solution)/shard_map/ppermute | solution.py:53
  215.6 7.7 %collective-permute-done.25 = bf16[2,64,2048]{2,1,0:T(8,128)(2,1)S(1)} collective-permute-done((bf16[2,64,2048]{2,1,0:T(8,128)(2,1)S(1)}, bf16[2,64,2048]{2,1,0:T(8,128)(2,1)S(1)}, u32[]{:S(2)}, u32[]{:S(2)}) %collective-permute-start.25) | collective-permute-done | bytes 524320 | tf_op jit(solution)/shard_map/ppermute | solution.py:53
  227.5 10.1 %collective-permute-done.32.refs_11_ = bf16[2,64,2048]{2,1,0:T(8,128)(2,1)S(1)} collective-permute-done((bf16[2,64,2048]{2,1,0:T(8,128)(2,1)S(1)}, bf16[2,64,2048]{2,1,0:T(8,128)(2,1)S(1)}, u32[]{:S(2)}, u32[]{:S(2)}) %collective-permute-start.32) | collective-permute-done | bytes 524320 | tf_op jit(solution)/shard_map/ppermute | solution.py:53
  240.0 8.8 %collective-permute-done.27.refs_5_ = bf16[2,64,2048]{2,1,0:T(8,128)(2,1)S(1)} collective-permute-done((bf16[2,64,2048]{2,1,0:T(8,128)(2,1)S(1)}, bf16[2,64,2048]{2,1,0:T(8,128)(2,1)S(1)}, u32[]{:S(2)}, u32[]{:S(2)}) %collective-permute-start.27) | collective-permute-done | bytes 524320 | tf_op jit(solution)/shard_map/ppermute | solution.py:53
  251.4 3.0 %collective-permute-done.33.refs_9_ = bf16[2,64,1024]{2,1,0:T(8,128)(2,1)S(1)} collective-permute-done((bf16[2,64,1024]{2,1,0:T(8,128)(2,1)S(1)}, bf16[2,64,1024]{2,1,0:T(8,128)(2,1)S(1)}, u32[]{:S(2)}, u32[]{:S(2)}) %collective-permute-start.33) | collective-permute-done | bytes 262176 | tf_op jit(solution)/shard_map/ppermute | solution.py:53
  267.6 5.6 %assemble.1 = bf16[8,64,4096]{2,1,0:T(8,128)(2,1)} custom-call(s32[6]{0:T(128)} %pad_add_fusion.1.refs_0_, bf16[2,64,2048]{2,1,0:T(8,128)(2,1)} %copy-done.10, bf16[2,64,2048]{2,1,0:T(8,128)(2,1)} %copy-done.14, bf16[2,64,1024]{2,1,0:T(8,128)(2,1)} %copy-done.24, bf16[2,64,1024]{2,1,0:T(8,128)(2,1)} %copy-done.25, bf16[2,64,2048]{2,1,0:T(8,128)(2,1)} %copy-done.13, ...), custom_call_target="tpu_custom_call" | custom-call | tf_op jit(solution)/shard_map/assemble/pallas_call | solution.py:296
  (169 shorter events, 76.0 us)
Async XLA Ops:
  2.1 34.9 %collective-permute-start.1 = (bf16[192,4096]{1,0:T(8,128)(2,1)S(1)}, bf16[192,4096]{1,0:T(8,128)(2,1)}, u32[]{:S(2)}, u32[]{:S(2)}) collective-permute-start(bf16[192,4096]{1,0:T(8,128)(2,1)S(1)} %pad_maximum_fusion.refs_0_), channel_id=1, source_target_pairs={{0,3},{1,0},{2,1},{3,2},{4,7},{5,4},{6,5},{7,6},{8,11},{9,8},{10,9... | collective-permute-start | bytes 4718600 | tf_op jit(solution)/shard_map/ppermute | solution.py:64
  6.8 36.8 %collective-permute-start = (bf16[192,4096]{1,0:T(8,128)(2,1)S(1)}, bf16[192,4096]{1,0:T(8,128)(2,1)}, u32[]{:S(2)}, u32[]{:S(2)}) collective-permute-start(bf16[192,4096]{1,0:T(8,128)(2,1)S(1)} %pad_maximum_fusion.refs_0_), channel_id=1, source_target_pairs={{0,1},{1,2},{2,3},{3,0},{4,5},{5,6},{6,7},{7,4},{8,9},{9,10},{10,1... | collective-permute-start | bytes 4718600 | tf_op jit(solution)/shard_map/ppermute | solution.py:64
  6.8 41.1 %collective-permute-start.10 = (bf16[192,4096]{1,0:T(8,128)(2,1)S(1)}, bf16[192,4096]{1,0:T(8,128)(2,1)}, u32[]{:S(2)}, u32[]{:S(2)}) collective-permute-start(bf16[192,4096]{1,0:T(8,128)(2,1)S(1)} %pad_maximum_fusion.refs_0_), channel_id=1, source_target_pairs={{0,4},{1,5},{2,6},{3,7},{4,8},{5,9},{6,10},{7,11},{8,12},{9,13},{1... | collective-permute-start | bytes 4718600 | tf_op jit(solution)/shard_map/ppermute | solution.py:64
  8.0 43.8 %collective-permute-start.11 = (bf16[192,4096]{1,0:T(8,128)(2,1)S(1)}, bf16[192,4096]{1,0:T(8,128)(2,1)S(1)}, u32[]{:S(2)}, u32[]{:S(2)}) collective-permute-start(bf16[192,4096]{1,0:T(8,128)(2,1)S(1)} %pad_maximum_fusion.refs_0_), channel_id=1, source_target_pairs={{0,12},{1,13},{2,14},{3,15},{4,0},{5,1},{6,2},{7,3},{8,4},{9,5},{1... | collective-permute-start | bytes 4718600 | tf_op jit(solution)/shard_map/ppermute | solution.py:64
  45.7 17.7 %collective-permute-start.3 = (bf16[96,4096]{1,0:T(8,128)(2,1)}, bf16[96,4096]{1,0:T(8,128)(2,1)}, u32[]{:S(2)}, u32[]{:S(2)}) collective-permute-start(bf16[96,4096]{1,0:T(8,128)(2,1)} %slice.296), channel_id=1, source_target_pairs={{0,1},{1,2},{2,3},{3,0},{4,5},{5,6},{6,7},{7,4},{8,9},{9,10},{10,1... | collective-permute-start | bytes 2359304 | tf_op jit(solution)/shard_map/ppermute | solution.py:64
  45.9 41.2 %collective-permute-start.2 = (bf16[192,4096]{1,0:T(8,128)(2,1)}, bf16[192,4096]{1,0:T(8,128)(2,1)}, u32[]{:S(2)}, u32[]{:S(2)}) collective-permute-start(bf16[192,4096]{1,0:T(8,128)(2,1)} %collective-permute-done.refs_1_), channel_id=1, source_target_pairs={{0,4},{1,5},{2,6},{3,7},{4,8},{5,9},{6,10},{7,11},{8,12},{9,13},{1... | collective-permute-start | bytes 4718600 | tf_op jit(solution)/shard_map/ppermute | solution.py:64
  48.0 39.2 %collective-permute-start.5 = (bf16[192,4096]{1,0:T(8,128)(2,1)}, bf16[192,4096]{1,0:T(8,128)(2,1)}, u32[]{:S(2)}, u32[]{:S(2)}) collective-permute-start(bf16[192,4096]{1,0:T(8,128)(2,1)} %collective-permute-done.refs_1_), channel_id=1, source_target_pairs={{0,12},{1,13},{2,14},{3,15},{4,0},{5,1},{6,2},{7,3},{8,4},{9,5},{1... | collective-permute-start | bytes 4718600 | tf_op jit(solution)/shard_map/ppermute | solution.py:64
  63.3 39.1 %collective-permute-start.12 = (bf16[192,4096]{1,0:T(8,128)(2,1)}, bf16[192,4096]{1,0:T(8,128)(2,1)S(1)}, u32[]{:S(2)}, u32[]{:S(2)}) collective-permute-start(bf16[192,4096]{1,0:T(8,128)(2,1)} %collective-permute-done.1.refs_2_), channel_id=1, source_target_pairs={{0,4},{1,5},{2,6},{3,7},{4,8},{5,9},{6,10},{7,11},{8,12},{9,13},{1... | collective-permute-start | bytes 4718600 | tf_op jit(solution)/shard_map/ppermute | solution.py:64
  68.7 33.8 %collective-permute-start.13 = (bf16[192,4096]{1,0:T(8,128)(2,1)}, bf16[192,4096]{1,0:T(8,128)(2,1)}, u32[]{:S(2)}, u32[]{:S(2)}) collective-permute-start(bf16[192,4096]{1,0:T(8,128)(2,1)} %collective-permute-done.1.refs_2_), channel_id=1, source_target_pairs={{0,12},{1,13},{2,14},{3,15},{4,0},{5,1},{6,2},{7,3},{8,4},{9,5},{1... | collective-permute-start | bytes 4718600 | tf_op jit(solution)/shard_map/ppermute | solution.py:64
  87.2 21.9 %collective-permute-start.6 = (bf16[192,4096]{1,0:T(8,128)(2,1)}, bf16[192,4096]{1,0:T(8,128)(2,1)S(1)}, u32[]{:S(2)}, u32[]{:S(2)}) collective-permute-start(bf16[192,4096]{1,0:T(8,128)(2,1)} %constant_dynamic-update-slice_fusion.refs_3_), channel_id=1, source_target_pairs={{0,4},{1,5},{2,6},{3,7},{4,8},{5,9},{6,10},{7,11},{8,12},{9,13},{1... | collective-permute-start | bytes 4718600 | tf_op jit(solution)/shard_map/ppermute | solution.py:64
  88.7 21.6 %collective-permute-start.7 = (bf16[192,4096]{1,0:T(8,128)(2,1)}, bf16[192,4096]{1,0:T(8,128)(2,1)}, u32[]{:S(2)}, u32[]{:S(2)}) collective-permute-start(bf16[192,4096]{1,0:T(8,128)(2,1)} %constant_dynamic-update-slice_fusion.refs_3_), channel_id=1, source_target_pairs={{0,12},{1,13},{2,14},{3,15},{4,0},{5,1},{6,2},{7,3},{8,4},{9,5},{1... | collective-permute-start | bytes 4718600 | tf_op jit(solution)/shard_map/ppermute | solution.py:64
  102.5 22.9 %collective-permute-start.15 = (bf16[192,4096]{1,0:T(8,128)(2,1)}, bf16[192,4096]{1,0:T(8,128)(2,1)S(1)}, u32[]{:S(2)}, u32[]{:S(2)}) collective-permute-start(bf16[192,4096]{1,0:T(8,128)(2,1)} %collective-permute-done.13.refs_1_), channel_id=1, source_target_pairs={{0,12},{1,13},{2,14},{3,15},{4,0},{5,1},{6,2},{7,3},{8,4},{9,5},{1... | collective-permute-start | bytes 4718600 | tf_op jit(solution)/shard_map/ppermute | solution.py:64
  102.6 23.5 %collective-permute-start.14 = (bf16[192,4096]{1,0:T(8,128)(2,1)}, bf16[192,4096]{1,0:T(8,128)(2,1)}, u32[]{:S(2)}, u32[]{:S(2)}) collective-permute-start(bf16[192,4096]{1,0:T(8,128)(2,1)} %collective-permute-done.10.refs_0_), channel_id=1, source_target_pairs={{0,4},{1,5},{2,6},{3,7},{4,8},{5,9},{6,10},{7,11},{8,12},{9,13},{1... | collective-permute-start | bytes 4718600 | tf_op jit(solution)/shard_map/ppermute | solution.py:64
  110.3 31.9 %collective-permute-start.9 = (bf16[192,4096]{1,0:T(8,128)(2,1)}, bf16[192,4096]{1,0:T(8,128)(2,1)S(1)}, u32[]{:S(2)}, u32[]{:S(2)}) collective-permute-start(bf16[192,4096]{1,0:T(8,128)(2,1)} %collective-permute-done.7.refs_3_), channel_id=1, source_target_pairs={{0,12},{1,13},{2,14},{3,15},{4,0},{5,1},{6,2},{7,3},{8,4},{9,5},{1... | collective-permute-start | bytes 4718600 | tf_op jit(solution)/shard_map/ppermute | solution.py:64
  110.9 31.9 %collective-permute-start.8 = (bf16[192,4096]{1,0:T(8,128)(2,1)}, bf16[192,4096]{1,0:T(8,128)(2,1)S(1)}, u32[]{:S(2)}, u32[]{:S(2)}) collective-permute-start(bf16[192,4096]{1,0:T(8,128)(2,1)} %collective-permute-done.2.refs_2_), channel_id=1, source_target_pairs={{0,4},{1,5},{2,6},{3,7},{4,8},{5,9},{6,10},{7,11},{8,12},{9,13},{1... | collective-permute-start | bytes 4718600 | tf_op jit(solution)/shard_map/ppermute | solution.py:64
  161.5 14.7 %collective-permute-start.16 = (bf16[4,64,2048]{2,1,0:T(8,128)(2,1)S(1)}, bf16[4,64,2048]{2,1,0:T(8,128)(2,1)S(1)}, u32[]{:S(2)}, u32[]{:S(2)}) collective-permute-start(bf16[4,64,2048]{2,1,0:T(8,128)(2,1)S(1)} %get-tuple-element.35), channel_id=1, source_target_pairs={{0,16},{16,0},{32,48},{48,32},{64,80},{80,64},{96,112},{112,96},{1... | collective-permute-start | bytes 3145736 | tf_op jit(solution)/shard_map/ppermute | solution.py:53
  197.6 15.1 %collective-permute-start.20 = (bf16[2,64,2048]{2,1,0:T(8,128)(2,1)S(1)}, bf16[2,64,2048]{2,1,0:T(8,128)(2,1)S(1)}, u32[]{:S(2)}, u32[]{:S(2)}) collective-permute-start(bf16[2,64,2048]{2,1,0:T(8,128)(2,1)S(1)} %pad_maximum_fusion.4), channel_id=1, source_target_pairs={{0,96},{16,48},{32,0},{48,80},{64,32},{80,112},{96,64},{112,16},{1... | collective-permute-start | bytes 1572872 | tf_op jit(solution)/shard_map/ppermute | solution.py:53
  197.7 17.8 %collective-permute-start.23 = (bf16[2,64,2048]{2,1,0:T(8,128)(2,1)S(1)}, bf16[2,64,2048]{2,1,0:T(8,128)(2,1)S(1)}, u32[]{:S(2)}, u32[]{:S(2)}) collective-permute-start(bf16[2,64,2048]{2,1,0:T(8,128)(2,1)S(1)} %pad_maximum_fusion.5), channel_id=1, source_target_pairs={{0,32},{16,112},{32,64},{48,16},{64,96},{80,48},{96,0},{112,80},{1... | collective-permute-start | bytes 1572872 | tf_op jit(solution)/shard_map/ppermute | solution.py:53
  200.7 22.6 %collective-permute-start.25 = (bf16[2,64,2048]{2,1,0:T(8,128)(2,1)S(1)}, bf16[2,64,2048]{2,1,0:T(8,128)(2,1)S(1)}, u32[]{:S(2)}, u32[]{:S(2)}) collective-permute-start(bf16[2,64,2048]{2,1,0:T(8,128)(2,1)S(1)} %pad_maximum_fusion.6), channel_id=1, source_target_pairs={{0,96},{16,48},{32,0},{48,80},{64,32},{80,112},{96,64},{112,16},{1... | collective-permute-start | bytes 1572872 | tf_op jit(solution)/shard_map/ppermute | solution.py:53
  224.5 14.5 %collective-permute-start.31 = (bf16[2,64,2048]{2,1,0:T(8,128)(2,1)S(1)}, bf16[2,64,2048]{2,1,0:T(8,128)(2,1)S(1)}, u32[]{:S(2)}, u32[]{:S(2)}) collective-permute-start(bf16[2,64,2048]{2,1,0:T(8,128)(2,1)S(1)} %get-tuple-element.45.refs_7_), channel_id=1, source_target_pairs={{0,96},{16,48},{32,0},{48,80},{64,32},{80,112},{96,64},{112,16},{1... | collective-permute-start | bytes 1572872 | tf_op jit(solution)/shard_map/ppermute | solution.py:53
  226.0 22.8 %collective-permute-start.27 = (bf16[2,64,2048]{2,1,0:T(8,128)(2,1)S(1)}, bf16[2,64,2048]{2,1,0:T(8,128)(2,1)S(1)}, u32[]{:S(2)}, u32[]{:S(2)}) collective-permute-start(bf16[2,64,2048]{2,1,0:T(8,128)(2,1)S(1)} %get-tuple-element.46.refs_1_), channel_id=1, source_target_pairs={{0,32},{16,112},{32,64},{48,16},{64,96},{80,48},{96,0},{112,80},{1... | collective-permute-start | bytes 1572872 | tf_op jit(solution)/shard_map/ppermute | solution.py:53
  227.3 23.0 %collective-permute-start.26 = (bf16[2,64,2048]{2,1,0:T(8,128)(2,1)S(1)}, bf16[2,64,2048]{2,1,0:T(8,128)(2,1)S(1)}, u32[]{:S(2)}, u32[]{:S(2)}) collective-permute-start(bf16[2,64,2048]{2,1,0:T(8,128)(2,1)S(1)} %get-tuple-element.46.refs_1_), channel_id=1, source_target_pairs={{0,96},{16,48},{32,0},{48,80},{64,32},{80,112},{96,64},{112,16},{1... | collective-permute-start | bytes 1572872 | tf_op jit(solution)/shard_map/ppermute | solution.py:53
  237.6 16.8 %collective-permute-start.33 = (bf16[2,64,1024]{2,1,0:T(8,128)(2,1)S(1)}, bf16[2,64,1024]{2,1,0:T(8,128)(2,1)S(1)}, u32[]{:S(2)}, u32[]{:S(2)}) collective-permute-start(bf16[2,64,1024]{2,1,0:T(8,128)(2,1)S(1)} %slice.326), channel_id=1, source_target_pairs={{0,32},{16,112},{32,64},{48,16},{64,96},{80,48},{96,0},{112,80},{1... | collective-permute-start | bytes 786440 | tf_op jit(solution)/shard_map/ppermute | solution.py:53
  239.1 16.8 %collective-permute-start.34 = (bf16[2,64,1024]{2,1,0:T(8,128)(2,1)S(1)}, bf16[2,64,1024]{2,1,0:T(8,128)(2,1)S(1)}, u32[]{:S(2)}, u32[]{:S(2)}) collective-permute-start(bf16[2,64,1024]{2,1,0:T(8,128)(2,1)S(1)} %slice.327), channel_id=1, source_target_pairs={{0,96},{16,48},{32,0},{48,80},{64,32},{80,112},{96,64},{112,16},{1... | collective-permute-start | bytes 786440 | tf_op jit(solution)/shard_map/ppermute | solution.py:53
  (41 other events, 403.3 us)
where the time goes:
time: 274 us; the launch traced here: 273 us
  waiting for transfers between devices  110 us (40%)
  Pallas kernels  72.9 us (27%)
  starting transfers between devices  49.1 us (18%)
  local copies, waits for them, and re-layouts  27.8 us (10%)
  other arithmetic  9.37 us (3%)
  between operations  4.05 us (1%)
    ppermute x20, waiting for transfers between devices, on_path(): return lax.ppermute(a, 'path', path_hop(hop, flip))  58.8 us
    ppermute x16, waiting for transfers between devices, send(): return lax.ppermute(a, ('path', 'fsdp'), plane_hop(*to))  51.5 us
    pallas_call x4, Pallas kernels, accumulate(): pl.pallas_call(functools.partial(grads_kernel, n, first, features, hidden...  45.4 us
    ppermute x16, starting transfers between devices, send(): return lax.ppermute(a, ('path', 'fsdp'), plane_hop(*to))  24.7 us
    ppermute x20, starting transfers between devices, on_path(): return lax.ppermute(a, 'path', path_hop(hop, flip))  24.4 us
    pallas_call x2, Pallas kernels, last_pseudo(): pl.pallas_call(functools.partial(pseudo_kernel, n, lead, features, hidden...  21.8 us
    unnamed x61, local copies, waits for them, and re-layouts  18.2 us
    pallas_call x1, Pallas kernels, assemble(): pl.pallas_call(functools.partial(assemble_kernel, halves), grid_spec=pltp...  5.62 us
  transfers between devices with their start and end apart: 36, of which 23 were waited for; matrix products, arithmetic and copies ran while one was open for 7% of the time, Pallas kernels for 20%

commit v1 on v0

--- a/solution.py
+++ b/solution.py
@@ -28,7 +28,7 @@
 BF16 = jnp.bfloat16
 COLS = 512
 CHUNK = 256
-LIMIT = 46 << 20
+LIMIT = 30 << 20
 
 
 def plane_hop(da, db):
@@ -57,21 +57,24 @@
     return lax.optimization_barrier((a, *others))[0]
 
 
-def gather_tokens(own, compute):
+def gather_tokens(x, g, compute):
     def send(a, to, *others):
         if others:
             a = after(a, *others)
         return lax.ppermute(a, ("path", "fsdp"), plane_hop(*to))
 
-    half = own.shape[0] // 2
-    got = {(0, 0): own}
-    got[0, -1], got[0, 1] = send(own, (0, 1)), send(own, (0, -1))
-    got[-1, 0], got[1, 0] = send(own, (1, 0)), send(own, (-1, 0))
-    low = send(got[0, -1][:half], (0, 1))
-    high = send(got[0, 1][half:], (0, -1))
-    got[-1, -1] = send(got[0, -1], (1, 0), got[0, 1])
-    got[1, -1] = send(got[0, -1], (-1, 0), got[0, 1])
-    got[0, 2] = jnp.concatenate([low, high], 0)
+    def join(x, g):
+        return jnp.concatenate([x, g], 1)
+
+    x_prv, g_nxt = send(x, (0, 1)), send(g, (0, -1))
+    x_nxt, g_prv = send(x, (0, -1)), send(g, (0, 1))
+    x_far, g_far = send(x_prv, (0, 1)), send(g_nxt, (0, -1))
+    own = join(x, g)
+    got = {(0, 0): own, (0, -1): join(x_prv, g_prv), (0, 1): join(x_nxt, g_nxt)}
+    got[0, 2] = join(x_far, g_far)
+    got[-1, 0], got[1, 0] = send(own, (1, 0)), send(own, (-1, 0), x_prv)
+    got[-1, -1] = send(got[0, -1], (1, 0), x_far, g_far)
+    got[1, -1] = send(got[0, -1], (-1, 0), x_far, g_far)
     hold = {3: compute(0, got)}
     ups = [(-1, 0), (-1, -1), (-1, 1), (-1, 2), (2, 0), (2, -1)]
     downs = [(1, 0), (1, -1), (1, 1), (1, 2), (2, 1), (2, 2)]
@@ -79,8 +82,6 @@
         a, b = ups[j]
         c, d = downs[j]
         wait = [got[ups[j - 2]], got[downs[j - 2]]]
-        if j == 2:
-            wait += [low, high]
         if j == 4:
             hold[4] = compute(1, got)
         if j in hold:
@@ -197,22 +198,26 @@
     return (first_new / (root + ADAM_EPS) + (INNER_RATE * DECAY) * start.astype(F32)).astype(BF16)
 
 
-def pseudo_kernel(n, lead, features, hidden_scale, *refs):
+def pseudo_kernel(n, part, features, hidden_scale, *refs):
     where, pieces = refs[0], refs[1 : 1 + n]
-    if lead:
+    span = features if part == 0 else features // 2
+    base, to = ((0, 0), (features, 0), (features + span, span))[part]
+    if part == 0:
         w, acc, m, v, keep, swap, act_t, total, dpre_t, right, sem = refs[1 + n :]
         fetch(pieces, right, sem)
         hidden_both(right, w, act_t, dpre_t, features, hidden_scale)
-        left, base, scale = dpre_t, 0, features ** (-0.5)
+        left, scale = dpre_t, features ** (-0.5)
     else:
-        left, w, acc, m, v, keep, swap, total, right, sem = refs[1 + n :]
-        base, scale = features, hidden_scale
-        fetch(pieces, right, sem, pl.ds(base, features))
+        left, w, acc, m, v = refs[1 + n : 6 + n]
+        keep, swap, total, right, sem = refs[-5:]
+        scale = hidden_scale
+        fetch(pieces, right, sem, pl.ds(base, span))
     y, core = where[0], where[1]
     rows = w.shape[0] // SETS
 
     def columns(j, carry):
         here = pl.ds(pl.multiple_of(j * COLS, COLS), COLS)
+        put = pl.ds(pl.multiple_of(to + j * COLS, COLS), COLS)
         cols = pl.ds(pl.multiple_of(base + j * COLS, COLS), COLS)
         total[...] = acc[:, cols] + jnp.dot(left[...], right[:, here], preferred_element_type=F32)
 
@@ -220,91 +225,101 @@
             for out, parity in ((keep, core), (swap, 1 - core)):
                 chip = lax.rem(y + jnp.where(parity == 0, d, YS - d), YS)
                 at = pl.ds(pl.multiple_of((2 * chip + parity) * rows, rows), rows)
-                out[d, :, here] = adam(total[at, :], scale, m[at, cols], v[at, cols], w[at, cols])
+                out[d, :, put] = adam(total[at, :], scale, m[at, cols], v[at, cols], w[at, cols])
             return carry
 
         return lax.fori_loop(0, YS, ring, carry)
 
-    lax.fori_loop(0, features // COLS, columns, 0)
-
-
-def last_pseudo(lead, where, pieces, act, w, acc, m, v, hidden_scale):
+    lax.fori_loop(0, span // COLS, columns, 0)
+
+
+def last_pseudo(part, where, pieces, act, w, acc, m, v, begun, hidden_scale):
     n = len(pieces)
     units, width = w.shape
     features = width // 2
+    span = features if part == 0 else features // 2
     tokens = sum(p.shape[0] for p in pieces)
     hid = (units, tokens)
     out_shape = [pltpu.VMEM((YS, units // SETS, features), BF16)] * 2
     scratch = [pltpu.VMEM((units, COLS), F32)]
-    if lead:
+    if part == 0:
         out_shape.append(pltpu.VMEM(hid, BF16))
         scratch += [pltpu.VMEM(hid, BF16), pltpu.VMEM((tokens, width), BF16)]
     else:
-        scratch += [pltpu.VMEM((tokens, features), BF16)]
-    tail = (() if lead else (act,)) + (w, acc, m, v)
+        scratch += [pltpu.VMEM((tokens, span), BF16)]
+    tail = (() if part == 0 else (act,)) + (w, acc, m, v) + begun
     return pl.pallas_call(
-        functools.partial(pseudo_kernel, n, lead, features, hidden_scale),
+        functools.partial(pseudo_kernel, n, part, features, hidden_scale),
         in_specs=[pl.BlockSpec(memory_space=pltpu.SMEM)] + [HBM] * n + [VMEM] * len(tail),
         out_specs=[VMEM] * len(out_shape),
         scratch_shapes=scratch + [pltpu.SemaphoreType.DMA((n,))],
         out_shape=out_shape,
+        input_output_aliases={n + 6: 0, n + 7: 1} if begun else {},
         compiler_params=pltpu.CompilerParams(vmem_limit_bytes=LIMIT),
         cost_estimate=pl.CostEstimate(
-            flops=(6 if lead else 2) * tokens * units * features,
-            bytes_accessed=units * features * 12 + tokens * width * 2,
+            flops=(6 * features if part == 0 else 2 * span) * tokens * units,
+            bytes_accessed=units * span * 12 + tokens * width * 2,
             transcendentals=units * tokens,
         ),
-        name="pseudo_in" if lead else "pseudo_out",
+        name="pseudo_%d" % part,
     )(where, *pieces, *tail)
 
 
-def assemble_kernel(halves, *refs):
-    info = refs[0]
-    out, sem = refs[-2:]
-    ins = refs[1:-2]
-    y, core = info[0], info[1]
+def home(info, d, parity):
+    return 2 * lax.rem(info[0] + jnp.where(parity == 0, d, YS - d), YS) + parity
+
+
+def own_kernel(halves, *refs):
+    info, ins, out, sem = refs[0], refs[1:-2], refs[-2], refs[-1]
     per = len(ins) // halves
     span = out.shape[2] // halves
     copies = []
 
-    def copy(src, s, lo, n):
-        dst = out.at[s, :, pl.ds(lo, n)]
-        c = pltpu.make_async_copy(src, dst, sem.at[len(copies)])
-        c.start()
-        copies.append(c)
-
-    def home(d, parity):
-        return 2 * lax.rem(y + jnp.where(parity == 0, d, YS - d), YS) + parity
+    def copy(src, d, lo, n):
+        dst = out.at[home(info, d, info[1]), :, pl.ds(lo, n)]
+        copies.append(pltpu.make_async_copy(src.at[info[2 + d]], dst, sem.at[len(copies)]))
+        copies[-1].start()
 
     for h in range(halves):
-        own, nxt, far_l, far_r, prv, other = ins[h * per : (h + 1) * per]
+        own, nxt, far_l, far_r, prv = ins[h * per : (h + 1) * per]
         at = h * span
-        copy(own.at[info[2]], home(0, core), at, span)
-        copy(nxt.at[info[3]], home(1, core), at, span)
-        copy(far_l.at[info[4]], home(2, core), at, span // 2)
-        copy(far_r.at[info[4]], home(2, core), at + span // 2, span // 2)
-        copy(prv.at[info[5]], home(3, core), at, span)
-        for d in range(YS):
-            copy(other.at[d], home(d, 1 - core), at, span)
+        copy(own, 0, at, span)
+        copy(nxt, 1, at, span)
+        copy(far_l, 2, at, span // 2)
+        copy(far_r, 2, at + span // 2, span // 2)
+        copy(prv, 3, at, span)
     for c in copies:
         c.wait()
 
 
-def assemble(info, pieces, rows, width):
-    halves = len(pieces)
-    flat = [a for p in pieces for a in p]
+def other_kernel(halves, *refs):
+    info, ins, out, sem = refs[0], refs[1 : 1 + halves], refs[-2], refs[-1]
+    span = out.shape[2] // halves
+    copies = []
+    for h in range(halves):
+        for d in range(YS):
+            dst = out.at[home(info, d, 1 - info[1]), :, pl.ds(h * span, span)]
+            copies.append(pltpu.make_async_copy(ins[h].at[d], dst, sem.at[h * YS + d]))
+            copies[-1].start()
+    for c in copies:
+        c.wait()
+
+
+def assemble(kernel, info, pieces, begun, halves, rows, width):
     return pl.pallas_call(
-        functools.partial(assemble_kernel, halves),
-        grid_spec=pltpu.PrefetchScalarGridSpec(
-            num_scalar_prefetch=1,
-            grid=(1,),
-            in_specs=[pl.BlockSpec(memory_space=pltpu.VMEM)] * len(flat),
-            out_specs=ANY,
-            scratch_shapes=[pltpu.SemaphoreType.DMA((9 * halves,))],
+        functools.partial(kernel, halves),
+        in_specs=[pl.BlockSpec(memory_space=pltpu.SMEM)]
+        + [VMEM] * len(pieces)
+        + [HBM] * len(begun),
+        out_specs=HBM,
+        out_shape=jax.ShapeDtypeStruct((SETS, rows, width), BF16),
+        scratch_shapes=[pltpu.SemaphoreType.DMA((5 * halves,))],
+        input_output_aliases={1 + len(pieces): 0} if begun else {},
+        cost_estimate=pl.CostEstimate(
+            flops=0, bytes_accessed=SETS * rows * width * 2, transcendentals=0
         ),
-        out_shape=jax.ShapeDtypeStruct((SETS, rows, width), BF16),
-        name="assemble",
-    )(info, *flat)
+        name=kernel.__name__,
+    )(info, *pieces, *begun)
 
 
 def per_device(
@@ -362,11 +377,8 @@
         acc = accumulate([got[b] for b in calls[k]], w, acc, hidden_scale)
         return acc
 
-    own = jnp.concatenate([input_activation_matrix[0], output_sensitivity[0]], 1)
-    got = gather_tokens(own, compute)
+    got = gather_tokens(input_activation_matrix[0], output_sensitivity[0], compute)
     rest = [got[2, -1], got[2, 2]]
-    keep_in, swap_in, act = last_pseudo(True, where, rest, None, w, acc, m, v, hidden_scale)
-    keep_out, swap_out = last_pseudo(False, where, rest, act, w, acc, m, v, hidden_scale)
 
     common = common_expert_parameters[0]
     inertia = outer_inertia[0]
@@ -376,44 +388,70 @@
         new_inertia = INERTIA_FACTOR * inertia + average
         return common - GLOBAL_LEARNING * (average + INERTIA_FACTOR * new_inertia), new_inertia
 
-    totals, pieces = [], []
-    mate = None
-    for h, (keep, swap) in enumerate(((keep_in, swap_in), (keep_out, swap_out))):
-        mate = on_path(swap if mate is None else after(swap, mate), 0, 1)
-
-        def both(d, lo=0, hi=features, keep=keep, mate=mate):
-            a = keep[d, :, lo:hi].astype(F32)[None]
-            b = mate[d, :, lo:hi].astype(F32)[None]
-            return mine[d][:, None, None] * a + mates[d][:, None, None] * b
-
-        from_prv = on_path(both(2, 0, mid).astype(BF16), 1)
-        from_nxt = on_path(both(2, mid, features).astype(BF16), -1)
-        up = jnp.concatenate([both(1, 0, mid) + from_prv.astype(F32), both(1, mid, features)], -1)
-        down = jnp.concatenate([both(3, 0, mid), both(3, mid, features) + from_nxt.astype(F32)], -1)
-        part_up = on_path(up.astype(BF16), 1)
-        part_down = on_path(down.astype(BF16), -1)
-        total = both(0) + part_up.astype(F32) + part_down.astype(F32)
-        totals.append(total)
+    def merged(d, pair, lo=0, hi=features):
+        keep, mate = (a[d, :, lo:hi].astype(F32)[None] for a in pair)
+        return mine[d][:, None, None] * keep + mates[d][:, None, None] * mate
+
+    def far_parts(pair):
+        return merged(2, pair, 0, mid).astype(BF16), merged(2, pair, mid).astype(BF16)
+
+    def far_sums(left, right):
+        return on_path(left, 1), on_path(right, -1)
+
+    def near_parts(pair, from_prv, from_nxt):
+        up = [merged(1, pair, 0, mid) + from_prv.astype(F32), merged(1, pair, mid)]
+        down = [merged(3, pair, 0, mid), merged(3, pair, mid) + from_nxt.astype(F32)]
+        return [jnp.concatenate(p, -1).astype(BF16) for p in (up, down)]
+
+    def near_sums(up, down):
+        return on_path(up, 1), on_path(down, -1)
+
+    def total_of(pair, parts):
+        return merged(0, pair) + parts[0].astype(F32) + parts[1].astype(F32)
+
+    def update(h, total):
         cols = slice(h * features, (h + 1) * features)
-        experts, _ = refreshed(total / share, common[..., cols], inertia[..., cols])
-        updated = experts.astype(BF16)
-        prv, nxt = on_path(updated, 1), on_path(updated, -1)
-        far_l = on_path(prv[..., :mid], 1)
-        far_r = on_path(nxt[..., mid:], -1)
+        return refreshed(total / share, common[..., cols], inertia[..., cols])[0].astype(BF16)
+
+    def near_modules(updated):
+        return on_path(updated, 1), on_path(updated, -1)
+
+    def spread(updated, prv, nxt):
+        far_l, far_r = on_path(prv[..., :mid], 1), on_path(nxt[..., mid:], -1)
         far = jnp.concatenate([far_l, far_r], -1)
-        chosen_for_mate = jnp.stack(
-            [
-                jnp.where(mate_pick[d] == 1, a[1], a[0])
-                for d, a in enumerate((updated, nxt, far, prv))
-            ]
-        )
-        other = on_path(chosen_for_mate, 0, 1)
-        pieces.append((updated, nxt, far_l, far_r, prv, other))
-
-    average = jnp.concatenate(totals, -1) / share
+        picked = [
+            jnp.where(mate_pick[d] == 1, a[1], a[0]) for d, a in enumerate((updated, nxt, far, prv))
+        ]
+        return (updated, nxt, far_l, far_r, prv), on_path(jnp.stack(picked), 0, 1)
+
+    acc = resident(acc)
+    keep_0, swap_0, act = last_pseudo(0, where, rest, None, w, acc, m, v, (), hidden_scale)
+    pair_0 = (keep_0, on_path(swap_0, 0, 1))
+    act = resident(act)
+    begun = last_pseudo(1, where, rest, act, w, acc, m, v, (), hidden_scale)
+    pair_0 = (keep_0, after(pair_0[1], *begun))
+    ends_0 = far_parts(pair_0)
+    held = after(where, *ends_0)
+    begun = tuple(resident(a) for a in begun)
+    keep_1, swap_1 = last_pseudo(2, held, rest, act, w, acc, m, v, begun, hidden_scale)
+    sums_0 = far_sums(*ends_0)
+    pair_1 = (keep_1, on_path(after(swap_1, *sums_0), 0, 1))
+    parts_0 = near_sums(*near_parts(pair_0, *sums_0))
+    total_0 = total_of(pair_0, parts_0)
+    sums_1 = far_sums(*far_parts(pair_1))
+    updated_0 = update(0, total_0)
+    near_0 = near_modules(updated_0)
+    ends_1 = (after(a, *parts_0) for a in near_parts(pair_1, *sums_1))
+    total_1 = total_of(pair_1, near_sums(*ends_1))
+    updated_1 = update(1, after(total_1, *near_0))
+    seen_0, other_0 = spread(updated_0, *near_0)
+    seen_1, other_1 = spread(updated_1, *near_modules(updated_1))
+
+    average = jnp.concatenate([total_0, total_1], -1) / share
     new_experts, new_inertia = refreshed(average, common, inertia)
     info = jnp.concatenate([where, own_pick]).astype(jnp.int32)
-    returned = assemble(info, pieces, rows, width)
+    returned = assemble(own_kernel, info, seen_0 + seen_1, (), 2, rows, width)
+    returned = assemble(other_kernel, info, (other_0, other_1), (returned,), 2, rows, width)
     return (new_experts[None], new_inertia[None], returned[None])
 
 

time: 274 us -> 283 us (1.033)
  waiting for transfers between devices: 110 us -> 141 us
  local copies, waits for them, and re-layouts: 27.8 us -> 9.35 us
  Pallas kernels: 72.9 us -> 62 us
  starting transfers between devices: 49.1 us -> 55.8 us
    ppermute x16 -> x18, waiting for transfers between devices: 51.5 us -> 72.6 us  [send(): return lax.ppermute(a, ('path', 'fsdp'), plane_hop(*to))]
    unnamed x61 -> x43, local copies, waits for them, and re-layouts: 18.2 us -> 4.69 us
    ppermute x20, waiting for transfers between devices: 58.8 us -> 67.9 us  [on_path(): return lax.ppermute(a, 'path', path_hop(hop, flip))]
    ppermute x16 -> x18, starting transfers between devices: 24.7 us -> 33 us  [send(): return lax.ppermute(a, ('path', 'fsdp'), plane_hop(*to))]
    pallas_call x4, Pallas kernels: 45.4 us -> 38.6 us  [accumulate(): pl.pallas_call(functools.partial(grads_kernel, n, first, features, hidden...]
    slice x7 -> x5, local copies, waits for them, and re-layouts: 4.88 us -> 0.72 us  [the longest x1 0.65 us: spread(): mate_pick[d] == 1]
    pallas_call x3 -> x5, Pallas kernels: 27.4 us -> 23.4 us  [the longest x3 16.9 us: last_pseudo(): pl.pallas_call(functools.partial(pseudo_kernel, n, part, features, hidden...]
  transfers between devices with their start and end apart: 36 -> 38, of which waited for: 23 -> 22; matrix products, arithmetic and copies ran while one was open for 7% -> 6% of each run, Pallas kernels for 20% -> 18%
where the time goes in v1:
time: 283 us
  waiting for transfers between devices  141 us (50%)
  Pallas kernels  62 us (22%)
  starting transfers between devices  55.8 us (20%)
  other arithmetic  10.9 us (4%)
  local copies, waits for them, and re-layouts  9.35 us (3%)
  between operations  4.02 us (1%)
    ppermute x18, waiting for transfers between devices, send(): return lax.ppermute(a, ('path', 'fsdp'), plane_hop(*to))  72.6 us
    ppermute x20, waiting for transfers between devices, on_path(): return lax.ppermute(a, 'path', path_hop(hop, flip))  67.9 us
    pallas_call x4, Pallas kernels, accumulate(): pl.pallas_call(functools.partial(grads_kernel, n, first, features, hidden...  38.6 us
    ppermute x18, starting transfers between devices, send(): return lax.ppermute(a, ('path', 'fsdp'), plane_hop(*to))  33 us
    ppermute x20, starting transfers between devices, on_path(): return lax.ppermute(a, 'path', path_hop(hop, flip))  22.9 us
    pallas_call x3, Pallas kernels, last_pseudo(): pl.pallas_call(functools.partial(pseudo_kernel, n, part, features, hidden...  16.9 us
    pallas_call x2, Pallas kernels, assemble(): pl.pallas_call(functools.partial(kernel, halves), in_specs=[pl.BlockSpec(...  6.51 us
  transfers between devices with their start and end apart: 38, of which 22 were waited for; matrix products, arithmetic and copies ran while one was open for 6% of the time, Pallas kernels for 18%

profile of v1, /device:TPU:1, one launch (start us, length us, event | category | flops | bytes accessed | tf_op | source)
XLA Modules:
  0.0 282.6 jit_solution(1501642655460907031)
XLA Ops:
  0.6 4.7 %collective-permute-start.3 = (bf16[192,2048]{1,0:T(8,128)(2,1)}, bf16[192,2048]{1,0:T(8,128)(2,1)S(1)}, u32[]{:S(2)}, u32[]{:S(2)}) collective-permute-start(bf16[192,2048]{1,0:T(8,128)(2,1)} %bitcast.163), channel_id=1, source_target_pairs={{0,3},{1,0},{2,1},{3,2},{4,7},{5,4},{6,5},{7,6},{8,11},{9,8},{10,9... | collective-permute-start | bytes 2359304 | tf_op jit(solution)/shard_map/ppermute | solution.py:64
  13.7 23.9 %collective-permute-done = bf16[192,2048]{1,0:T(8,128)(2,1)} collective-permute-done((bf16[192,2048]{1,0:T(8,128)(2,1)}, bf16[192,2048]{1,0:T(8,128)(2,1)}, u32[]{:S(2)}, u32[]{:S(2)}) %collective-permute-start) | collective-permute-done | bytes 786464 | tf_op jit(solution)/shard_map/ppermute | solution.py:64
  46.0 5.6 %collective-permute-done.2 = bf16[192,2048]{1,0:T(8,128)(2,1)S(1)} collective-permute-done((bf16[192,2048]{1,0:T(8,128)(2,1)}, bf16[192,2048]{1,0:T(8,128)(2,1)S(1)}, u32[]{:S(2)}, u32[]{:S(2)}) %collective-permute-start.2) | collective-permute-done | bytes 786464 | tf_op jit(solution)/shard_map/ppermute | solution.py:64
  51.6 4.8 %collective-permute-start.5 = (bf16[192,4096]{1,0:T(8,128)(2,1)S(1)}, bf16[192,4096]{1,0:T(8,128)(2,1)S(1)}, u32[]{:S(2)}, u32[]{:S(2)}) collective-permute-start(bf16[192,4096]{1,0:T(8,128)(2,1)S(1)} %constant_dynamic-update-slice_fusion.refs_1_), channel_id=1, source_target_pairs={{0,4},{1,5},{2,6},{3,7},{4,8},{5,9},{6,10},{7,11},{8,12},{9,13},{1... | collective-permute-start | bytes 4718600 | tf_op jit(solution)/shard_map/ppermute | solution.py:64
  57.8 11.2 %collective-permute-done.13.refs_1_ = bf16[192,4096]{1,0:T(8,128)(2,1)S(1)} collective-permute-done((bf16[192,4096]{1,0:T(8,128)(2,1)S(1)}, bf16[192,4096]{1,0:T(8,128)(2,1)S(1)}, u32[]{:S(2)}, u32[]{:S(2)}) %collective-permute-start.13) | collective-permute-done | bytes 1572896 | tf_op jit(solution)/shard_map/ppermute | solution.py:64
  72.4 9.7 %grads.4.refs_5_ = f32[512,4096]{1,0:T(8,128)S(1)} custom-call(bf16[192,4096]{1,0:T(8,128)(2,1)S(1)} %pad_maximum_fusion.refs_0_, bf16[192,4096]{1,0:T(8,128)(2,1)S(1)} %constant_dynamic-update-slice_fusion.refs_1_, bf16[192,4096]{1,0:T(8,128)(2,1)S(1)} %constant_dynamic-update-slice_fusion.4.refs_2_, ...), custom_call_target="tpu_custom_call" | custom-call | flops 6442450944 | bytes 6291456 | tf_op jit(solution)/shard_map/grads/pallas_call | solution.py:165
  82.1 3.7 %collective-permute-done.6.refs_3_ = bf16[192,4096]{1,0:T(8,128)(2,1)S(1)} collective-permute-done((bf16[192,4096]{1,0:T(8,128)(2,1)S(1)}, bf16[192,4096]{1,0:T(8,128)(2,1)S(1)}, u32[]{:S(2)}, u32[]{:S(2)}) %collective-permute-start.6) | collective-permute-done | bytes 1572896 | tf_op jit(solution)/shard_map/ppermute | solution.py:64
  89.2 11.1 %grads.5.refs_5_ = f32[512,4096]{1,0:T(8,128)S(1)} custom-call(bf16[192,4096]{1,0:T(8,128)(2,1)} %collective-permute-done.12.refs_0_, bf16[192,4096]{1,0:T(8,128)(2,1)S(1)} %collective-permute-done.13.refs_1_, bf16[192,4096]{1,0:T(8,128)(2,1)S(1)} %collective-permute-done.5.refs_2_, ...), custom_call_target="tpu_custom_call", output_to_operand_aliasing={{}: (5, {})} | custom-call | flops 6442450944 | bytes 6291456 | tf_op jit(solution)/shard_map/grads/pallas_call | solution.py:165
  107.4 12.1 %collective-permute-done.9.refs_3_ = bf16[192,4096]{1,0:T(8,128)(2,1)S(1)} collective-permute-done((bf16[192,4096]{1,0:T(8,128)(2,1)S(1)}, bf16[192,4096]{1,0:T(8,128)(2,1)S(1)}, u32[]{:S(2)}, u32[]{:S(2)}) %collective-permute-start.9) | collective-permute-done | bytes 1572896 | tf_op jit(solution)/shard_map/ppermute | solution.py:64
  122.9 11.2 %grads.6.refs_3_ = f32[512,4096]{1,0:T(8,128)S(1)} custom-call(bf16[192,4096]{1,0:T(8,128)(2,1)S(1)} %collective-permute-done.14.refs_0_, bf16[192,4096]{1,0:T(8,128)(2,1)} %collective-permute-done.15.refs_1_, bf16[192,4096]{1,0:T(8,128)(2,1)S(1)} %collective-permute-done.8.refs_2_, ...), custom_call_target="tpu_custom_call", output_to_operand_aliasing={{}: (5, {})} | custom-call | flops 6442450944 | bytes 6291456 | tf_op jit(solution)/shard_map/grads/pallas_call | solution.py:165
  136.5 6.6 %grads.7.refs_4_.refs_5_ = f32[512,4096]{1,0:T(8,128)S(1)} custom-call(bf16[192,4096]{1,0:T(8,128)(2,1)S(1)} %collective-permute-done.16.refs_0_, bf16[192,4096]{1,0:T(8,128)(2,1)S(1)} %collective-permute-done.17.refs_1_, bf16[512,4096]{1,0:T(8,128)(2,1)S(1)} %bitcast.147, f32[512,4096]{1,0:T(8,128)S(1)} %grads.6.refs_3_), custom_call_target="tpu_custom_call", output_to_operand_aliasing={{}: (3, {})} | custom-call | flops 3221225472 | bytes 3145728 | tf_op jit(solution)/shard_map/grads/pallas_call | solution.py:165
  143.0 10.2 %collective-permute-done.11.refs_2_ = bf16[192,4096]{1,0:T(8,128)(2,1)S(1)} collective-permute-done((bf16[192,4096]{1,0:T(8,128)(2,1)S(1)}, bf16[192,4096]{1,0:T(8,128)(2,1)S(1)}, u32[]{:S(2)}, u32[]{:S(2)}) %collective-permute-start.11) | collective-permute-done | bytes 1572896 | tf_op jit(solution)/shard_map/ppermute | solution.py:64
  154.4 9.1 %pseudo_0.1 = (bf16[4,64,2048]{2,1,0:T(8,128)(2,1)S(1)}, bf16[4,64,2048]{2,1,0:T(8,128)(2,1)S(1)}, bf16[512,384]{1,0:T(8,128)(2,1)S(1)}) custom-call(s32[2]{0:T(128)S(1)} %pad_add_fusion.refs_0_, bf16[192,4096]{1,0:T(8,128)(2,1)S(1)} %collective-permute-done.10.refs_1_, bf16[192,4096]{1,0:T(8,128)(2,1)} %copy-done.3, bf16[512,4096]{1,0:T(8,128)(2,1)S(1)} %bitcast.148, ...), custom_call_target="tpu_custom_call" | custom-call | flops 2415919104 | bytes 15728640 | tf_op jit(solution)/shard_map/pseudo_0/pallas_call | solution.py:251
  164.0 3.9 %pseudo_1.1 = (bf16[4,64,2048]{2,1,0:T(8,128)(2,1)S(1)}, bf16[4,64,2048]{2,1,0:T(8,128)(2,1)S(1)}) custom-call(s32[2]{0:T(128)S(1)} %pad_add_fusion.refs_0_, bf16[192,4096]{1,0:T(8,128)(2,1)S(1)} %collective-permute-done.10.refs_1_, bf16[192,4096]{1,0:T(8,128)(2,1)} %copy-done.3, bf16[512,384]{1,0:T(8,128)(2,1)S(1)} %get-tuple-element.45.refs_3_, ...), custom_call_target="tpu_custom_call" | custom-call | flops 402653184 | bytes 9437184 | tf_op jit(solution)/shard_map/pseudo_1/pallas_call | solution.py:251
  171.2 3.9 %pseudo_2.1 = (bf16[4,64,2048]{2,1,0:T(8,128)(2,1)S(1)}, bf16[4,64,2048]{2,1,0:T(8,128)(2,1)S(1)}) custom-call(s32[2]{0:T(128)S(1)} %pad_add_fusion.refs_0_, bf16[192,4096]{1,0:T(8,128)(2,1)S(1)} %collective-permute-done.10.refs_1_, bf16[192,4096]{1,0:T(8,128)(2,1)} %copy-done.3, ...), custom_call_target="tpu_custom_call", output_to_operand_aliasing={{0}: (8, {}), {1}: (9, {})} | custom-call | flops 402653184 | bytes 9437184 | tf_op jit(solution)/shard_map/pseudo_2/pallas_call | solution.py:251
  185.0 4.8 %collective-permute-done.24 = bf16[2,64,1024]{2,1,0:T(8,128)(2,1)S(1)} collective-permute-done((bf16[2,64,1024]{2,1,0:T(8,128)(2,1)S(1)}, bf16[2,64,1024]{2,1,0:T(8,128)(2,1)S(1)}, u32[]{:S(2)}, u32[]{:S(2)}) %collective-permute-start.24) | collective-permute-done | bytes 262176 | tf_op jit(solution)/shard_map/ppermute | solution.py:53
  190.2 3.5 %collective-permute-start.20 = (bf16[2,64,2048]{2,1,0:T(8,128)(2,1)S(1)}, bf16[2,64,2048]{2,1,0:T(8,128)(2,1)S(1)}, u32[]{:S(2)}, u32[]{:S(2)}) collective-permute-start(bf16[2,64,2048]{2,1,0:T(8,128)(2,1)S(1)} %pad_maximum_fusion.3), channel_id=1, source_target_pairs={{0,32},{16,112},{32,64},{48,16},{64,96},{80,48},{96,0},{112,80},{1... | collective-permute-start | bytes 1572872 | tf_op jit(solution)/shard_map/ppermute | solution.py:53
  194.6 8.4 %collective-permute-done.20 = bf16[2,64,2048]{2,1,0:T(8,128)(2,1)S(1)} collective-permute-done((bf16[2,64,2048]{2,1,0:T(8,128)(2,1)S(1)}, bf16[2,64,2048]{2,1,0:T(8,128)(2,1)S(1)}, u32[]{:S(2)}, u32[]{:S(2)}) %collective-permute-start.20) | collective-permute-done | bytes 524320 | tf_op jit(solution)/shard_map/ppermute | solution.py:53
  203.0 3.7 %collective-permute-done.22 = bf16[2,64,2048]{2,1,0:T(8,128)(2,1)S(1)} collective-permute-done((bf16[2,64,2048]{2,1,0:T(8,128)(2,1)S(1)}, bf16[2,64,2048]{2,1,0:T(8,128)(2,1)S(1)}, u32[]{:S(2)}, u32[]{:S(2)}) %collective-permute-start.22) | collective-permute-done | bytes 524320 | tf_op jit(solution)/shard_map/ppermute | solution.py:53
  208.3 12.1 %collective-permute-done.25 = bf16[2,64,2048]{2,1,0:T(8,128)(2,1)S(1)} collective-permute-done((bf16[2,64,2048]{2,1,0:T(8,128)(2,1)S(1)}, bf16[2,64,2048]{2,1,0:T(8,128)(2,1)S(1)}, u32[]{:S(2)}, u32[]{:S(2)}) %collective-permute-start.25) | collective-permute-done | bytes 524320 | tf_op jit(solution)/shard_map/ppermute | solution.py:53
  225.9 8.8 %collective-permute-done.28.refs_2_ = bf16[2,64,2048]{2,1,0:T(8,128)(2,1)S(1)} collective-permute-done((bf16[2,64,2048]{2,1,0:T(8,128)(2,1)S(1)}, bf16[2,64,2048]{2,1,0:T(8,128)(2,1)S(1)}, u32[]{:S(2)}, u32[]{:S(2)}) %collective-permute-start.28) | collective-permute-done | bytes 524320 | tf_op jit(solution)/shard_map/ppermute | solution.py:53
  243.7 13.0 %collective-permute-done.30.refs_3_ = bf16[2,64,1024]{2,1,0:T(8,128)(2,1)S(1)} collective-permute-done((bf16[2,64,1024]{2,1,0:T(8,128)(2,1)S(1)}, bf16[2,64,1024]{2,1,0:T(8,128)(2,1)S(1)}, u32[]{:S(2)}, u32[]{:S(2)}) %collective-permute-start.30) | collective-permute-done | bytes 262176 | tf_op jit(solution)/shard_map/ppermute | solution.py:53
  263.3 4.7 %collective-permute-done.35.refs_8_ = bf16[2,64,1024]{2,1,0:T(8,128)(2,1)S(1)} collective-permute-done((bf16[2,64,1024]{2,1,0:T(8,128)(2,1)S(1)}, bf16[2,64,1024]{2,1,0:T(8,128)(2,1)S(1)}, u32[]{:S(2)}, u32[]{:S(2)}) %collective-permute-start.35) | collective-permute-done | bytes 262176 | tf_op jit(solution)/shard_map/ppermute | solution.py:53
  274.9 3.6 %own_kernel.1.refs_3_ = bf16[8,64,4096]{2,1,0:T(8,128)(2,1)} custom-call(s32[6]{0:T(128)} %pad_add_fusion.1.refs_0_, bf16[2,64,2048]{2,1,0:T(8,128)(2,1)} %copy-done.6, bf16[2,64,2048]{2,1,0:T(8,128)(2,1)} %copy-done.8, bf16[2,64,1024]{2,1,0:T(8,128)(2,1)} %copy-done.12, bf16[2,64,1024]{2,1,0:T(8,128)(2,1)} %copy-done.13, bf16[2,64,2048]{2,1,0:T(8,128)(2,1)} %copy-done.9, ...), custom_call_target="tpu_custom_call" | custom-call | bytes 4194304 | tf_op jit(solution)/shard_map/own_kernel/pallas_call | solution.py:309
  (161 shorter events, 84.5 us)
Async XLA Ops:
  0.6 36.9 %collective-permute-start.3 = (bf16[192,2048]{1,0:T(8,128)(2,1)}, bf16[192,2048]{1,0:T(8,128)(2,1)S(1)}, u32[]{:S(2)}, u32[]{:S(2)}) collective-permute-start(bf16[192,2048]{1,0:T(8,128)(2,1)} %bitcast.163), channel_id=1, source_target_pairs={{0,3},{1,0},{2,1},{3,2},{4,7},{5,4},{6,5},{7,6},{8,11},{9,8},{10,9... | collective-permute-start | bytes 2359304 | tf_op jit(solution)/shard_map/ppermute | solution.py:64
  5.3 35.0 %collective-permute-start.1 = (bf16[192,2048]{1,0:T(8,128)(2,1)}, bf16[192,2048]{1,0:T(8,128)(2,1)}, u32[]{:S(2)}, u32[]{:S(2)}) collective-permute-start(bf16[192,2048]{1,0:T(8,128)(2,1)} %bitcast.164), channel_id=1, source_target_pairs={{0,1},{1,2},{2,3},{3,0},{4,5},{5,6},{6,7},{7,4},{8,9},{9,10},{10,1... | collective-permute-start | bytes 2359304 | tf_op jit(solution)/shard_map/ppermute | solution.py:64
  5.3 32.3 %collective-permute-start = (bf16[192,2048]{1,0:T(8,128)(2,1)}, bf16[192,2048]{1,0:T(8,128)(2,1)}, u32[]{:S(2)}, u32[]{:S(2)}) collective-permute-start(bf16[192,2048]{1,0:T(8,128)(2,1)} %bitcast.166), channel_id=1, source_target_pairs={{0,1},{1,2},{2,3},{3,0},{4,5},{5,6},{6,7},{7,4},{8,9},{9,10},{10,1... | collective-permute-start | bytes 2359304 | tf_op jit(solution)/shard_map/ppermute | solution.py:64
  5.3 51.0 %collective-permute-start.7 = (bf16[192,2048]{1,0:T(8,128)(2,1)}, bf16[192,2048]{1,0:T(8,128)(2,1)}, u32[]{:S(2)}, u32[]{:S(2)}) collective-permute-start(bf16[192,2048]{1,0:T(8,128)(2,1)} %bitcast.167), channel_id=1, source_target_pairs={{0,3},{1,0},{2,1},{3,2},{4,7},{5,4},{6,5},{7,6},{8,11},{9,8},{10,9... | collective-permute-start | bytes 2359304 | tf_op jit(solution)/shard_map/ppermute | solution.py:64
  9.5 48.2 %collective-permute-start.12 = (bf16[192,4096]{1,0:T(8,128)(2,1)S(1)}, bf16[192,4096]{1,0:T(8,128)(2,1)}, u32[]{:S(2)}, u32[]{:S(2)}) collective-permute-start(bf16[192,4096]{1,0:T(8,128)(2,1)S(1)} %pad_maximum_fusion.refs_0_), channel_id=1, source_target_pairs={{0,4},{1,5},{2,6},{3,7},{4,8},{5,9},{6,10},{7,11},{8,12},{9,13},{1... | collective-permute-start | bytes 4718600 | tf_op jit(solution)/shard_map/ppermute | solution.py:64
  37.6 14.0 %collective-permute-start.2 = (bf16[192,2048]{1,0:T(8,128)(2,1)}, bf16[192,2048]{1,0:T(8,128)(2,1)S(1)}, u32[]{:S(2)}, u32[]{:S(2)}) collective-permute-start(bf16[192,2048]{1,0:T(8,128)(2,1)} %collective-permute-done), channel_id=1, source_target_pairs={{0,1},{1,2},{2,3},{3,0},{4,5},{5,6},{6,7},{7,4},{8,9},{9,10},{10,1... | collective-permute-start | bytes 2359304 | tf_op jit(solution)/shard_map/ppermute | solution.py:64
  37.6 14.0 %collective-permute-start.4 = (bf16[192,2048]{1,0:T(8,128)(2,1)S(1)}, bf16[192,2048]{1,0:T(8,128)(2,1)S(1)}, u32[]{:S(2)}, u32[]{:S(2)}) collective-permute-start(bf16[192,2048]{1,0:T(8,128)(2,1)S(1)} %collective-permute-done.3), channel_id=1, source_target_pairs={{0,3},{1,0},{2,1},{3,2},{4,7},{5,4},{6,5},{7,6},{8,11},{9,8},{10,9... | collective-permute-start | bytes 2359304 | tf_op jit(solution)/shard_map/ppermute | solution.py:64
  40.3 28.7 %collective-permute-start.13 = (bf16[192,4096]{1,0:T(8,128)(2,1)S(1)}, bf16[192,4096]{1,0:T(8,128)(2,1)S(1)}, u32[]{:S(2)}, u32[]{:S(2)}) collective-permute-start(bf16[192,4096]{1,0:T(8,128)(2,1)S(1)} %pad_maximum_fusion.refs_0_), channel_id=1, source_target_pairs={{0,12},{1,13},{2,14},{3,15},{4,0},{5,1},{6,2},{7,3},{8,4},{9,5},{1... | collective-permute-start | bytes 4718600 | tf_op jit(solution)/shard_map/ppermute | solution.py:64
  51.6 30.6 %collective-permute-start.5 = (bf16[192,4096]{1,0:T(8,128)(2,1)S(1)}, bf16[192,4096]{1,0:T(8,128)(2,1)S(1)}, u32[]{:S(2)}, u32[]{:S(2)}) collective-permute-start(bf16[192,4096]{1,0:T(8,128)(2,1)S(1)} %constant_dynamic-update-slice_fusion.refs_1_), channel_id=1, source_target_pairs={{0,4},{1,5},{2,6},{3,7},{4,8},{5,9},{6,10},{7,11},{8,12},{9,13},{1... | collective-permute-start | bytes 4718600 | tf_op jit(solution)/shard_map/ppermute | solution.py:64
  56.3 29.5 %collective-permute-start.6 = (bf16[192,4096]{1,0:T(8,128)(2,1)S(1)}, bf16[192,4096]{1,0:T(8,128)(2,1)S(1)}, u32[]{:S(2)}, u32[]{:S(2)}) collective-permute-start(bf16[192,4096]{1,0:T(8,128)(2,1)S(1)} %constant_dynamic-update-slice_fusion.refs_1_), channel_id=1, source_target_pairs={{0,12},{1,13},{2,14},{3,15},{4,0},{5,1},{6,2},{7,3},{8,4},{9,5},{1... | collective-permute-start | bytes 4718600 | tf_op jit(solution)/shard_map/ppermute | solution.py:64
  69.0 31.4 %collective-permute-start.14 = (bf16[192,4096]{1,0:T(8,128)(2,1)S(1)}, bf16[192,4096]{1,0:T(8,128)(2,1)S(1)}, u32[]{:S(2)}, u32[]{:S(2)}) collective-permute-start(bf16[192,4096]{1,0:T(8,128)(2,1)S(1)} %constant_dynamic-update-slice_fusion.4.refs_2_), channel_id=1, source_target_pairs={{0,4},{1,5},{2,6},{3,7},{4,8},{5,9},{6,10},{7,11},{8,12},{9,13},{1... | collective-permute-start | bytes 4718600 | tf_op jit(solution)/shard_map/ppermute | solution.py:64
  69.0 33.7 %collective-permute-start.15 = (bf16[192,4096]{1,0:T(8,128)(2,1)S(1)}, bf16[192,4096]{1,0:T(8,128)(2,1)}, u32[]{:S(2)}, u32[]{:S(2)}) collective-permute-start(bf16[192,4096]{1,0:T(8,128)(2,1)S(1)} %constant_dynamic-update-slice_fusion.4.refs_2_), channel_id=1, source_target_pairs={{0,12},{1,13},{2,14},{3,15},{4,0},{5,1},{6,2},{7,3},{8,4},{9,5},{1... | collective-permute-start | bytes 4718600 | tf_op jit(solution)/shard_map/ppermute | solution.py:64
  85.8 21.6 %collective-permute-start.8 = (bf16[192,4096]{1,0:T(8,128)(2,1)S(1)}, bf16[192,4096]{1,0:T(8,128)(2,1)S(1)}, u32[]{:S(2)}, u32[]{:S(2)}) collective-permute-start(bf16[192,4096]{1,0:T(8,128)(2,1)S(1)} %constant_dynamic-update-slice_fusion.2.refs_3_), channel_id=1, source_target_pairs={{0,4},{1,5},{2,6},{3,7},{4,8},{5,9},{6,10},{7,11},{8,12},{9,13},{1... | collective-permute-start | bytes 4718600 | tf_op jit(solution)/shard_map/ppermute | solution.py:64
  85.8 33.7 %collective-permute-start.9 = (bf16[192,4096]{1,0:T(8,128)(2,1)S(1)}, bf16[192,4096]{1,0:T(8,128)(2,1)S(1)}, u32[]{:S(2)}, u32[]{:S(2)}) collective-permute-start(bf16[192,4096]{1,0:T(8,128)(2,1)S(1)} %constant_dynamic-update-slice_fusion.2.refs_3_), channel_id=1, source_target_pairs={{0,12},{1,13},{2,14},{3,15},{4,0},{5,1},{6,2},{7,3},{8,4},{9,5},{1... | collective-permute-start | bytes 4718600 | tf_op jit(solution)/shard_map/ppermute | solution.py:64
  102.7 33.8 %collective-permute-start.17 = (bf16[192,4096]{1,0:T(8,128)(2,1)}, bf16[192,4096]{1,0:T(8,128)(2,1)S(1)}, u32[]{:S(2)}, u32[]{:S(2)}) collective-permute-start(bf16[192,4096]{1,0:T(8,128)(2,1)} %collective-permute-done.15.refs_1_), channel_id=1, source_target_pairs={{0,12},{1,13},{2,14},{3,15},{4,0},{5,1},{6,2},{7,3},{8,4},{9,5},{1... | collective-permute-start | bytes 4718600 | tf_op jit(solution)/shard_map/ppermute | solution.py:64
  106.1 30.4 %collective-permute-start.16 = (bf16[192,4096]{1,0:T(8,128)(2,1)}, bf16[192,4096]{1,0:T(8,128)(2,1)S(1)}, u32[]{:S(2)}, u32[]{:S(2)}) collective-permute-start(bf16[192,4096]{1,0:T(8,128)(2,1)} %collective-permute-done.12.refs_0_), channel_id=1, source_target_pairs={{0,4},{1,5},{2,6},{3,7},{4,8},{5,9},{6,10},{7,11},{8,12},{9,13},{1... | collective-permute-start | bytes 4718600 | tf_op jit(solution)/shard_map/ppermute | solution.py:64
  119.5 33.7 %collective-permute-start.11 = (bf16[192,4096]{1,0:T(8,128)(2,1)S(1)}, bf16[192,4096]{1,0:T(8,128)(2,1)S(1)}, u32[]{:S(2)}, u32[]{:S(2)}) collective-permute-start(bf16[192,4096]{1,0:T(8,128)(2,1)S(1)} %collective-permute-done.9.refs_3_), channel_id=1, source_target_pairs={{0,12},{1,13},{2,14},{3,15},{4,0},{5,1},{6,2},{7,3},{8,4},{9,5},{1... | collective-permute-start | bytes 4718600 | tf_op jit(solution)/shard_map/ppermute | solution.py:64
  122.9 30.3 %collective-permute-start.10 = (bf16[192,4096]{1,0:T(8,128)(2,1)S(1)}, bf16[192,4096]{1,0:T(8,128)(2,1)S(1)}, u32[]{:S(2)}, u32[]{:S(2)}) collective-permute-start(bf16[192,4096]{1,0:T(8,128)(2,1)S(1)} %collective-permute-done.5.refs_2_), channel_id=1, source_target_pairs={{0,4},{1,5},{2,6},{3,7},{4,8},{5,9},{6,10},{7,11},{8,12},{9,13},{1... | collective-permute-start | bytes 4718600 | tf_op jit(solution)/shard_map/ppermute | solution.py:64
  222.6 14.4 %collective-permute-start.29 = (bf16[2,64,2048]{2,1,0:T(8,128)(2,1)S(1)}, bf16[2,64,2048]{2,1,0:T(8,128)(2,1)S(1)}, u32[]{:S(2)}, u32[]{:S(2)}) collective-permute-start(bf16[2,64,2048]{2,1,0:T(8,128)(2,1)S(1)} %get-tuple-element.61.refs_1_), channel_id=1, source_target_pairs={{0,32},{16,112},{32,64},{48,16},{64,96},{80,48},{96,0},{112,80},{1... | collective-permute-start | bytes 1572872 | tf_op jit(solution)/shard_map/ppermute | solution.py:53
  237.3 23.3 %collective-permute-start.34 = (bf16[2,64,2048]{2,1,0:T(8,128)(2,1)S(1)}, bf16[2,64,2048]{2,1,0:T(8,128)(2,1)S(1)}, u32[]{:S(2)}, u32[]{:S(2)}) collective-permute-start(bf16[2,64,2048]{2,1,0:T(8,128)(2,1)S(1)} %fusion.5.refs_6_), channel_id=1, source_target_pairs={{0,32},{16,112},{32,64},{48,16},{64,96},{80,48},{96,0},{112,80},{1... | collective-permute-start | bytes 1572872 | tf_op jit(solution)/shard_map/ppermute | solution.py:53
  240.7 22.5 %collective-permute-start.33 = (bf16[2,64,2048]{2,1,0:T(8,128)(2,1)S(1)}, bf16[2,64,2048]{2,1,0:T(8,128)(2,1)S(1)}, u32[]{:S(2)}, u32[]{:S(2)}) collective-permute-start(bf16[2,64,2048]{2,1,0:T(8,128)(2,1)S(1)} %fusion.5.refs_6_), channel_id=1, source_target_pairs={{0,96},{16,48},{32,0},{48,80},{64,32},{80,112},{96,64},{112,16},{1... | collective-permute-start | bytes 1572872 | tf_op jit(solution)/shard_map/ppermute | solution.py:53
  240.7 16.0 %collective-permute-start.30 = (bf16[2,64,1024]{2,1,0:T(8,128)(2,1)S(1)}, bf16[2,64,1024]{2,1,0:T(8,128)(2,1)S(1)}, u32[]{:S(2)}, u32[]{:S(2)}) collective-permute-start(bf16[2,64,1024]{2,1,0:T(8,128)(2,1)S(1)} %slice.301), channel_id=1, source_target_pairs={{0,32},{16,112},{32,64},{48,16},{64,96},{80,48},{96,0},{112,80},{1... | collective-permute-start | bytes 786440 | tf_op jit(solution)/shard_map/ppermute | solution.py:53
  243.5 16.0 %collective-permute-start.31 = (bf16[2,64,1024]{2,1,0:T(8,128)(2,1)S(1)}, bf16[2,64,1024]{2,1,0:T(8,128)(2,1)S(1)}, u32[]{:S(2)}, u32[]{:S(2)}) collective-permute-start(bf16[2,64,1024]{2,1,0:T(8,128)(2,1)S(1)} %slice.302), channel_id=1, source_target_pairs={{0,96},{16,48},{32,0},{48,80},{64,32},{80,112},{96,64},{112,16},{1... | collective-permute-start | bytes 786440 | tf_op jit(solution)/shard_map/ppermute | solution.py:53
  260.7 17.8 %collective-permute-start.32 = (bf16[4,64,2048]{2,1,0:T(8,128)(2,1)}, bf16[4,64,2048]{2,1,0:T(8,128)(2,1)}, u32[]{:S(2)}, u32[]{:S(2)}) collective-permute-start(bf16[4,64,2048]{2,1,0:T(8,128)(2,1)} %pad_maximum_fusion.1), channel_id=1, source_target_pairs={{0,16},{16,0},{32,48},{48,32},{64,80},{80,64},{96,112},{112,96},{1... | collective-permute-start | bytes 3145736 | tf_op jit(solution)/shard_map/ppermute | solution.py:53
  (33 other events, 340.8 us)

commit v2 on v1

--- a/solution.py
+++ b/solution.py
@@ -72,7 +72,8 @@
     own = join(x, g)
     got = {(0, 0): own, (0, -1): join(x_prv, g_prv), (0, 1): join(x_nxt, g_nxt)}
     got[0, 2] = join(x_far, g_far)
-    got[-1, 0], got[1, 0] = send(own, (1, 0)), send(own, (-1, 0), x_prv)
+    got[-1, 0] = send(own, (1, 0), x_prv, g_nxt)
+    got[1, 0] = send(own, (-1, 0), x_prv, g_nxt)
     got[-1, -1] = send(got[0, -1], (1, 0), x_far, g_far)
     got[1, -1] = send(got[0, -1], (-1, 0), x_far, g_far)
     hold = {3: compute(0, got)}
@@ -200,65 +201,72 @@
 
 def pseudo_kernel(n, part, features, hidden_scale, *refs):
     where, pieces = refs[0], refs[1 : 1 + n]
-    span = features if part == 0 else features // 2
-    base, to = ((0, 0), (features, 0), (features + span, span))[part]
+    base = part * features
     if part == 0:
-        w, acc, m, v, keep, swap, act_t, total, dpre_t, right, sem = refs[1 + n :]
+        w, acc, m, v, keep, swap, far_keep, far_swap, act_t = refs[1 + n : 10 + n]
+        total, dpre_t, right, sem = refs[10 + n :]
         fetch(pieces, right, sem)
         hidden_both(right, w, act_t, dpre_t, features, hidden_scale)
         left, scale = dpre_t, features ** (-0.5)
     else:
-        left, w, acc, m, v = refs[1 + n : 6 + n]
-        keep, swap, total, right, sem = refs[-5:]
+        left, w, acc, m, v, keep, swap, far_keep, far_swap, total, right, sem = refs[1 + n :]
         scale = hidden_scale
-        fetch(pieces, right, sem, pl.ds(base, span))
+        fetch(pieces, right, sem, pl.ds(base, features))
     y, core = where[0], where[1]
     rows = w.shape[0] // SETS
+    per = far_keep.shape[2] // COLS
 
     def columns(j, carry):
         here = pl.ds(pl.multiple_of(j * COLS, COLS), COLS)
-        put = pl.ds(pl.multiple_of(to + j * COLS, COLS), COLS)
         cols = pl.ds(pl.multiple_of(base + j * COLS, COLS), COLS)
         total[...] = acc[:, cols] + jnp.dot(left[...], right[:, here], preferred_element_type=F32)
 
-        def ring(d, carry):
+        def stepped(d, parity):
+            chip = lax.rem(y + jnp.where(parity == 0, d, YS - d), YS)
+            at = pl.ds(pl.multiple_of((2 * chip + parity) * rows, rows), rows)
+            return adam(total[at, :], scale, m[at, cols], v[at, cols], w[at, cols])
+
+        def ring(i, carry):
             for out, parity in ((keep, core), (swap, 1 - core)):
-                chip = lax.rem(y + jnp.where(parity == 0, d, YS - d), YS)
-                at = pl.ds(pl.multiple_of((2 * chip + parity) * rows, rows), rows)
-                out[d, :, put] = adam(total[at, :], scale, m[at, cols], v[at, cols], w[at, cols])
+                out[i, :, here] = stepped(i + i // 2, parity)
             return carry
 
-        return lax.fori_loop(0, YS, ring, carry)
-
-    lax.fori_loop(0, span // COLS, columns, 0)
-
-
-def last_pseudo(part, where, pieces, act, w, acc, m, v, begun, hidden_scale):
+        lax.fori_loop(0, YS - 1, ring, carry)
+        put = pl.ds(pl.multiple_of(lax.rem(j, per) * COLS, COLS), COLS)
+        for out, parity in ((far_keep, core), (far_swap, 1 - core)):
+            out[lax.div(j, per), :, put] = stepped(2, parity)
+        return carry
+
+    lax.fori_loop(0, features // COLS, columns, 0)
+
+
+def last_pseudo(part, where, pieces, act, w, acc, m, v, hidden_scale):
     n = len(pieces)
     units, width = w.shape
     features = width // 2
-    span = features if part == 0 else features // 2
+    rows = units // SETS
     tokens = sum(p.shape[0] for p in pieces)
     hid = (units, tokens)
-    out_shape = [pltpu.VMEM((YS, units // SETS, features), BF16)] * 2
+    near = pltpu.VMEM((YS - 1, rows, features), BF16)
+    far = pltpu.VMEM((2, rows, features // 2), BF16)
+    out_shape = [near, near, far, far]
     scratch = [pltpu.VMEM((units, COLS), F32)]
     if part == 0:
         out_shape.append(pltpu.VMEM(hid, BF16))
         scratch += [pltpu.VMEM(hid, BF16), pltpu.VMEM((tokens, width), BF16)]
     else:
-        scratch += [pltpu.VMEM((tokens, span), BF16)]
-    tail = (() if part == 0 else (act,)) + (w, acc, m, v) + begun
+        scratch += [pltpu.VMEM((tokens, features), BF16)]
+    tail = (() if part == 0 else (act,)) + (w, acc, m, v)
     return pl.pallas_call(
         functools.partial(pseudo_kernel, n, part, features, hidden_scale),
         in_specs=[pl.BlockSpec(memory_space=pltpu.SMEM)] + [HBM] * n + [VMEM] * len(tail),
         out_specs=[VMEM] * len(out_shape),
         scratch_shapes=scratch + [pltpu.SemaphoreType.DMA((n,))],
         out_shape=out_shape,
-        input_output_aliases={n + 6: 0, n + 7: 1} if begun else {},
         compiler_params=pltpu.CompilerParams(vmem_limit_bytes=LIMIT),
         cost_estimate=pl.CostEstimate(
-            flops=(6 * features if part == 0 else 2 * span) * tokens * units,
-            bytes_accessed=units * span * 12 + tokens * width * 2,
+            flops=(6 if part == 0 else 2) * features * tokens * units,
+            bytes_accessed=units * features * 12 + tokens * width * 2,
             transcendentals=units * tokens,
         ),
         name="pseudo_%d" % part,
@@ -269,51 +277,40 @@
     return 2 * lax.rem(info[0] + jnp.where(parity == 0, d, YS - d), YS) + parity
 
 
-def own_kernel(halves, *refs):
-    info, ins, out, sem = refs[0], refs[1:-2], refs[-2], refs[-1]
-    per = len(ins) // halves
-    span = out.shape[2] // halves
-    copies = []
-
-    def copy(src, d, lo, n):
-        dst = out.at[home(info, d, info[1]), :, pl.ds(lo, n)]
-        copies.append(pltpu.make_async_copy(src.at[info[2 + d]], dst, sem.at[len(copies)]))
-        copies[-1].start()
-
-    for h in range(halves):
-        own, nxt, far_l, far_r, prv = ins[h * per : (h + 1) * per]
-        at = h * span
-        copy(own, 0, at, span)
-        copy(nxt, 1, at, span)
-        copy(far_l, 2, at, span // 2)
-        copy(far_r, 2, at + span // 2, span // 2)
-        copy(prv, 3, at, span)
+def run_copies(pairs, sem):
+    copies = [pltpu.make_async_copy(a, b, sem.at[k]) for k, (a, b) in enumerate(pairs)]
+    for c in copies:
+        c.start()
     for c in copies:
         c.wait()
 
 
-def other_kernel(halves, *refs):
-    info, ins, out, sem = refs[0], refs[1 : 1 + halves], refs[-2], refs[-1]
-    span = out.shape[2] // halves
-    copies = []
-    for h in range(halves):
-        for d in range(YS):
-            dst = out.at[home(info, d, 1 - info[1]), :, pl.ds(h * span, span)]
-            copies.append(pltpu.make_async_copy(ins[h].at[d], dst, sem.at[h * YS + d]))
-            copies[-1].start()
-    for c in copies:
-        c.wait()
-
-
-def assemble(kernel, info, pieces, begun, halves, rows, width):
+def near_own_kernel(info, own, nxt, prv, out, sem):
+    run_copies(
+        [(a.at[info[2 + d]], out.at[home(info, d, info[1])]) for a, d in ((own, 0), (nxt, 1), (prv, 3))],
+        sem,
+    )
+
+
+def rest_kernel(info, near, own_l, own_r, other_l, other_r, begun, out, sem):
+    half = own_l.shape[1]
+    left, right = pl.ds(0, half), pl.ds(half, half)
+    pairs = [(near.at[i], out.at[home(info, d, 1 - info[1])]) for i, d in enumerate((0, 1, 3))]
+    for parity, l, r in ((info[1], own_l, own_r), (1 - info[1], other_l, other_r)):
+        far = home(info, 2, parity)
+        pairs += [(l, out.at[far, :, left]), (r, out.at[far, :, right])]
+    run_copies(pairs, sem)
+
+
+def assemble(kernel, info, pieces, begun, copies, rows, width):
     return pl.pallas_call(
-        functools.partial(kernel, halves),
+        kernel,
         in_specs=[pl.BlockSpec(memory_space=pltpu.SMEM)]
         + [VMEM] * len(pieces)
         + [HBM] * len(begun),
         out_specs=HBM,
         out_shape=jax.ShapeDtypeStruct((SETS, rows, width), BF16),
-        scratch_shapes=[pltpu.SemaphoreType.DMA((5 * halves,))],
+        scratch_shapes=[pltpu.SemaphoreType.DMA((copies,))],
         input_output_aliases={1 + len(pieces): 0} if begun else {},
         cost_estimate=pl.CostEstimate(
             flops=0, bytes_accessed=SETS * rows * width * 2, transcendentals=0
@@ -351,15 +348,26 @@
         1.0,
         0.0,
     ).astype(F32)
-    steps = jnp.arange(YS, dtype=jnp.int32)
-    ring_sets = 2 * ((y + jnp.where(core == 0, steps, YS - steps)) % YS) + core
-    mine = chosen[me][ring_sets]
-    mates = chosen[me ^ 1][ring_sets]
+    turn = 1 - 2 * core
+    chips = (y + turn * jnp.arange(YS, dtype=jnp.int32)) % YS
+    sets = 2 * chips + core
+    nxt_chip, prv_chip = chips[1], chips[3]
+    mate = me ^ 1
+    paths = jnp.stack(
+        [me] * 4
+        + [mate] * 4
+        + [2 * prv_chip + core, 2 * prv_chip + 1 - core]
+        + [2 * nxt_chip + core, 2 * nxt_chip + 1 - core]
+    )
+    at_sets = jnp.concatenate([sets, sets, sets[1:2], sets[1:2], sets[3:], sets[3:]])
+    weights = chosen[paths, at_sets]
+    pick_paths = jnp.concatenate([paths[:8], paths[10:], paths[8:10]])
+    pick_sets = jnp.concatenate([sets, sets, sets[3:], sets[3:], sets[1:2], sets[1:2]])
+    picks = trajectory_membership[pick_paths, pick_sets]
     tally = jnp.sum(chosen[:, me], axis=0)
     share = jnp.maximum(tally, 1.0)[:, None, None]
-    own_pick = trajectory_membership[me][ring_sets]
-    mate_pick = trajectory_membership[me ^ 1][ring_sets]
     where = jnp.stack([y, core]).astype(jnp.int32)
+    info = jnp.concatenate([where, picks[:4]]).astype(jnp.int32)
 
     calls = (
         ((0, 0), (0, -1), (0, 1), (0, 2)),
@@ -367,8 +375,9 @@
         ((-1, 1), (1, 1), (-1, 2), (1, 2)),
         ((2, 0), (2, 1)),
     )
-    small = (where, mine, mates, share, own_pick, mate_pick)
-    w, where, mine, mates, share, own_pick, mate_pick = lax.optimization_barrier((w, *small))
+    w, where, weights, picks, share, info = lax.optimization_barrier(
+        (w, where, weights, picks, share, info)
+    )
     w, m, v = resident(w), resident(m), resident(v)
     acc = None
 
@@ -384,74 +393,52 @@
     inertia = outer_inertia[0]
     mid = features // 2
 
-    def refreshed(average, common, inertia):
-        new_inertia = INERTIA_FACTOR * inertia + average
-        return common - GLOBAL_LEARNING * (average + INERTIA_FACTOR * new_inertia), new_inertia
-
-    def merged(d, pair, lo=0, hi=features):
-        keep, mate = (a[d, :, lo:hi].astype(F32)[None] for a in pair)
-        return mine[d][:, None, None] * keep + mates[d][:, None, None] * mate
-
-    def far_parts(pair):
-        return merged(2, pair, 0, mid).astype(BF16), merged(2, pair, mid).astype(BF16)
-
-    def far_sums(left, right):
-        return on_path(left, 1), on_path(right, -1)
-
-    def near_parts(pair, from_prv, from_nxt):
-        up = [merged(1, pair, 0, mid) + from_prv.astype(F32), merged(1, pair, mid)]
-        down = [merged(3, pair, 0, mid), merged(3, pair, mid) + from_nxt.astype(F32)]
-        return [jnp.concatenate(p, -1).astype(BF16) for p in (up, down)]
-
-    def near_sums(up, down):
-        return on_path(up, 1), on_path(down, -1)
-
-    def total_of(pair, parts):
-        return merged(0, pair) + parts[0].astype(F32) + parts[1].astype(F32)
-
-    def update(h, total):
-        cols = slice(h * features, (h + 1) * features)
-        return refreshed(total / share, common[..., cols], inertia[..., cols])[0].astype(BF16)
-
-    def near_modules(updated):
-        return on_path(updated, 1), on_path(updated, -1)
-
-    def spread(updated, prv, nxt):
-        far_l, far_r = on_path(prv[..., :mid], 1), on_path(nxt[..., mid:], -1)
-        far = jnp.concatenate([far_l, far_r], -1)
-        picked = [
-            jnp.where(mate_pick[d] == 1, a[1], a[0]) for d, a in enumerate((updated, nxt, far, prv))
-        ]
-        return (updated, nxt, far_l, far_r, prv), on_path(jnp.stack(picked), 0, 1)
+    def weighed(k, a):
+        return weights[k][:, None, None] * a.astype(F32)[None]
+
+    def exchange(swap, far_keep, far_swap):
+        lefts = on_path(far_keep[0], 1), on_path(far_swap[0], -1, 1)
+        rights = on_path(far_keep[1], -1), on_path(far_swap[1], 1, 1)
+        return (on_path(swap, 0, 1), *lefts, *rights)
+
+    def sums(keep, came):
+        near = came[0]
+
+        def merged(i, d, lo=0, hi=features):
+            return weighed(d, keep[i, :, lo:hi]) + weighed(4 + d, near[i, :, lo:hi])
+
+        up = [merged(1, 1, 0, mid) + weighed(8, came[1]) + weighed(9, came[2]), merged(1, 1, mid)]
+        down = [merged(2, 3, 0, mid), merged(2, 3, mid) + weighed(10, came[3]) + weighed(11, came[4])]
+        return merged(0, 0), up, down
 
     acc = resident(acc)
-    keep_0, swap_0, act = last_pseudo(0, where, rest, None, w, acc, m, v, (), hidden_scale)
-    pair_0 = (keep_0, on_path(swap_0, 0, 1))
-    act = resident(act)
-    begun = last_pseudo(1, where, rest, act, w, acc, m, v, (), hidden_scale)
-    pair_0 = (keep_0, after(pair_0[1], *begun))
-    ends_0 = far_parts(pair_0)
-    held = after(where, *ends_0)
-    begun = tuple(resident(a) for a in begun)
-    keep_1, swap_1 = last_pseudo(2, held, rest, act, w, acc, m, v, begun, hidden_scale)
-    sums_0 = far_sums(*ends_0)
-    pair_1 = (keep_1, on_path(after(swap_1, *sums_0), 0, 1))
-    parts_0 = near_sums(*near_parts(pair_0, *sums_0))
-    total_0 = total_of(pair_0, parts_0)
-    sums_1 = far_sums(*far_parts(pair_1))
-    updated_0 = update(0, total_0)
-    near_0 = near_modules(updated_0)
-    ends_1 = (after(a, *parts_0) for a in near_parts(pair_1, *sums_1))
-    total_1 = total_of(pair_1, near_sums(*ends_1))
-    updated_1 = update(1, after(total_1, *near_0))
-    seen_0, other_0 = spread(updated_0, *near_0)
-    seen_1, other_1 = spread(updated_1, *near_modules(updated_1))
-
-    average = jnp.concatenate([total_0, total_1], -1) / share
-    new_experts, new_inertia = refreshed(average, common, inertia)
-    info = jnp.concatenate([where, own_pick]).astype(jnp.int32)
-    returned = assemble(own_kernel, info, seen_0 + seen_1, (), 2, rows, width)
-    returned = assemble(other_kernel, info, (other_0, other_1), (returned,), 2, rows, width)
+    keep_0, *out_0, act = last_pseudo(0, where, rest, None, w, acc, m, v, hidden_scale)
+    came_0 = exchange(*out_0)
+    keep_1, *out_1 = last_pseudo(1, where, rest, resident(act), w, acc, m, v, hidden_scale)
+    came_1 = exchange(*lax.optimization_barrier((*out_1, *came_0))[:3])
+    here_0, up_0, down_0 = sums(keep_0, came_0)
+    here_1, up_1, down_1 = sums(keep_1, came_1)
+    part_up = on_path(jnp.concatenate([a.astype(BF16) for a in up_0 + up_1], -1), 1)
+    part_down = on_path(jnp.concatenate([a.astype(BF16) for a in down_0 + down_1], -1), -1)
+
+    total = jnp.concatenate([here_0, here_1], -1) + part_up.astype(F32) + part_down.astype(F32)
+    average = total / share
+    new_inertia = INERTIA_FACTOR * inertia + average
+    new_experts = common - GLOBAL_LEARNING * (average + INERTIA_FACTOR * new_inertia)
+    updated = new_experts.astype(BF16)
+    prv, nxt = on_path(updated, 1), on_path(updated, -1)
+
+    def picked(k, a, lo=0, hi=width):
+        return jnp.where(picks[k] == 1, a[1, :, lo:hi], a[0, :, lo:hi])
+
+    own_l = on_path(picked(8, prv, 0, features), 1)
+    other_l = on_path(picked(9, prv, 0, features), 1, 1)
+    own_r = on_path(picked(10, nxt, features), -1)
+    other_r = on_path(picked(11, nxt, features), -1, 1)
+    near = on_path(jnp.stack([picked(4, updated), picked(5, nxt), picked(7, prv)]), 0, 1)
+    returned = assemble(near_own_kernel, info, (updated, nxt, prv), (), 3, rows, width)
+    far = (own_l, own_r, other_l, other_r)
+    returned = assemble(rest_kernel, info, (near, *far), (returned,), 7, rows, width)
     return (new_experts[None], new_inertia[None], returned[None])
 
 

time: 283 us -> 250 us (0.88)
  waiting for transfers between devices: 141 us -> 116 us
  starting transfers between devices: 55.8 us -> 45.6 us
  Pallas kernels: 62 us -> 58.7 us
  between operations: 4.02 us -> 6.98 us
    ppermute x18, waiting for transfers between devices: 72.6 us -> 59.9 us  [send(): return lax.ppermute(a, ('path', 'fsdp'), plane_hop(*to))]
    ppermute x20 -> x19, waiting for transfers between devices: 67.9 us -> 55.6 us  [on_path(): return lax.ppermute(a, 'path', path_hop(hop, flip))]
    ppermute x20 -> x19, starting transfers between devices: 22.9 us -> 16.4 us  [on_path(): return lax.ppermute(a, 'path', path_hop(hop, flip))]
    concatenate x2, local copies, waits for them, and re-layouts: 0.04 us -> 5.4 us  [the longest x1 2.7 us: per_device(): jnp.concatenate([sets, sets, sets[1:2], sets[1:2], sets[3:], sets[3:]])]
    ppermute x18, starting transfers between devices: 33 us -> 29.1 us  [send(): return lax.ppermute(a, ('path', 'fsdp'), plane_hop(*to))]
    pallas_call x3 -> x2, Pallas kernels: 16.9 us -> 15.6 us  [last_pseudo(): pl.pallas_call(functools.partial(pseudo_kernel, n, part, features, hidden...]
  transfers between devices with their start and end apart: 38 -> 37, of which waited for: 22 -> 19; matrix products, arithmetic and copies ran while one was open for 6% -> 7% of each run, Pallas kernels for 18% -> 19%
where the time goes in v2:
time: 250 us; the launch traced here: 249 us
  waiting for transfers between devices  116 us (46%)
  Pallas kernels  58.7 us (23%)
  starting transfers between devices  45.6 us (18%)
  local copies, waits for them, and re-layouts  11.3 us (5%)
  other arithmetic  11.2 us (4%)
  between operations  6.98 us (3%)
    ppermute x18, waiting for transfers between devices, send(): return lax.ppermute(a, ('path', 'fsdp'), plane_hop(*to))  59.9 us
    ppermute x19, waiting for transfers between devices, on_path(): return lax.ppermute(a, 'path', path_hop(hop, flip))  55.6 us
    pallas_call x4, Pallas kernels, accumulate(): pl.pallas_call(functools.partial(grads_kernel, n, first, features, hidden...  36.8 us
    ppermute x18, starting transfers between devices, send(): return lax.ppermute(a, ('path', 'fsdp'), plane_hop(*to))  29.1 us
    ppermute x19, starting transfers between devices, on_path(): return lax.ppermute(a, 'path', path_hop(hop, flip))  16.4 us
    pallas_call x2, Pallas kernels, last_pseudo(): pl.pallas_call(functools.partial(pseudo_kernel, n, part, features, hidden...  15.6 us
    pallas_call x2, Pallas kernels, assemble(): pl.pallas_call(kernel, in_specs=[pl.BlockSpec(memory_space=pltpu.SMEM)] +...  6.25 us
  transfers between devices with their start and end apart: 37, of which 19 were waited for; matrix products, arithmetic and copies ran while one was open for 7% of the time, Pallas kernels for 19%

profile of v2, /device:TPU:1, one launch (start us, length us, event | category | flops | bytes accessed | tf_op | source)
XLA Modules:
  0.0 249.3 jit_solution(2141593217902162838)
XLA Ops:
  0.6 4.7 %collective-permute-start.3 = (bf16[192,2048]{1,0:T(8,128)(2,1)}, bf16[192,2048]{1,0:T(8,128)(2,1)S(1)}, u32[]{:S(2)}, u32[]{:S(2)}) collective-permute-start(bf16[192,2048]{1,0:T(8,128)(2,1)} %bitcast.200), channel_id=1, source_target_pairs={{0,3},{1,0},{2,1},{3,2},{4,7},{5,4},{6,5},{7,6},{8,11},{9,8},{10,9... | collective-permute-start | bytes 2359304 | tf_op jit(solution)/shard_map/ppermute | solution.py:64
  20.9 5.4 %collective-permute-done = bf16[192,2048]{1,0:T(8,128)(2,1)S(1)} collective-permute-done((bf16[192,2048]{1,0:T(8,128)(2,1)}, bf16[192,2048]{1,0:T(8,128)(2,1)S(1)}, u32[]{:S(2)}, u32[]{:S(2)}) %collective-permute-start) | collective-permute-done | bytes 786464 | tf_op jit(solution)/shard_map/ppermute | solution.py:64
  32.4 9.6 %collective-permute-done.2 = bf16[192,2048]{1,0:T(8,128)(2,1)S(1)} collective-permute-done((bf16[192,2048]{1,0:T(8,128)(2,1)S(1)}, bf16[192,2048]{1,0:T(8,128)(2,1)S(1)}, u32[]{:S(2)}, u32[]{:S(2)}) %collective-permute-start.2) | collective-permute-done | bytes 786464 | tf_op jit(solution)/shard_map/ppermute | solution.py:64
  41.9 3.3 %collective-permute-start.5 = (bf16[192,4096]{1,0:T(8,128)(2,1)S(1)}, bf16[192,4096]{1,0:T(8,128)(2,1)S(1)}, u32[]{:S(2)}, u32[]{:S(2)}) collective-permute-start(bf16[192,4096]{1,0:T(8,128)(2,1)S(1)} %constant_dynamic-update-slice_fusion.refs_1_), channel_id=1, source_target_pairs={{0,4},{1,5},{2,6},{3,7},{4,8},{5,9},{6,10},{7,11},{8,12},{9,13},{1... | collective-permute-start | bytes 4718600 | tf_op jit(solution)/shard_map/ppermute | solution.py:64
  46.8 9.7 %collective-permute-done.12.refs_0_ = bf16[192,4096]{1,0:T(8,128)(2,1)S(1)} collective-permute-done((bf16[192,4096]{1,0:T(8,128)(2,1)S(1)}, bf16[192,4096]{1,0:T(8,128)(2,1)S(1)}, u32[]{:S(2)}, u32[]{:S(2)}) %collective-permute-start.12) | collective-permute-done | bytes 1572896 | tf_op jit(solution)/shard_map/ppermute | solution.py:64
  56.5 3.0 %collective-permute-start.15 = (bf16[192,4096]{1,0:T(8,128)(2,1)S(1)}, bf16[192,4096]{1,0:T(8,128)(2,1)S(1)}, u32[]{:S(2)}, u32[]{:S(2)}) collective-permute-start(bf16[192,4096]{1,0:T(8,128)(2,1)S(1)} %constant_dynamic-update-slice_fusion.4.refs_2_), channel_id=1, source_target_pairs={{0,12},{1,13},{2,14},{3,15},{4,0},{5,1},{6,2},{7,3},{8,4},{9,5},{1... | collective-permute-start | bytes 4718600 | tf_op jit(solution)/shard_map/ppermute | solution.py:64
  59.4 9.8 %grads.4.refs_5_ = f32[512,4096]{1,0:T(8,128)S(1)} custom-call(bf16[192,4096]{1,0:T(8,128)(2,1)S(1)} %pad_maximum_fusion.refs_0_, bf16[192,4096]{1,0:T(8,128)(2,1)S(1)} %constant_dynamic-update-slice_fusion.refs_1_, bf16[192,4096]{1,0:T(8,128)(2,1)S(1)} %constant_dynamic-update-slice_fusion.4.refs_2_, ...), custom_call_target="tpu_custom_call" | custom-call | flops 6442450944 | bytes 6291456 | tf_op jit(solution)/shard_map/grads/pallas_call | solution.py:166
  69.2 4.1 %collective-permute-done.5.refs_2_ = bf16[192,4096]{1,0:T(8,128)(2,1)S(1)} collective-permute-done((bf16[192,4096]{1,0:T(8,128)(2,1)S(1)}, bf16[192,4096]{1,0:T(8,128)(2,1)S(1)}, u32[]{:S(2)}, u32[]{:S(2)}) %collective-permute-start.5) | collective-permute-done | bytes 1572896 | tf_op jit(solution)/shard_map/ppermute | solution.py:64
  76.3 10.2 %grads.5.refs_5_ = f32[512,4096]{1,0:T(8,128)S(1)} custom-call(bf16[192,4096]{1,0:T(8,128)(2,1)S(1)} %collective-permute-done.12.refs_0_, bf16[192,4096]{1,0:T(8,128)(2,1)S(1)} %collective-permute-done.13.refs_1_, bf16[192,4096]{1,0:T(8,128)(2,1)S(1)} %collective-permute-done.5.refs_2_, ...), custom_call_target="tpu_custom_call", output_to_operand_aliasing={{}: (5, {})} | custom-call | flops 6442450944 | bytes 6291456 | tf_op jit(solution)/shard_map/grads/pallas_call | solution.py:166
  86.5 3.7 %collective-permute-done.14.refs_0_ = bf16[192,4096]{1,0:T(8,128)(2,1)S(1)} collective-permute-done((bf16[192,4096]{1,0:T(8,128)(2,1)S(1)}, bf16[192,4096]{1,0:T(8,128)(2,1)S(1)}, u32[]{:S(2)}, u32[]{:S(2)}) %collective-permute-start.14) | collective-permute-done | bytes 1572896 | tf_op jit(solution)/shard_map/ppermute | solution.py:64
  93.1 13.9 %collective-permute-done.8.refs_2_ = bf16[192,4096]{1,0:T(8,128)(2,1)S(1)} collective-permute-done((bf16[192,4096]{1,0:T(8,128)(2,1)S(1)}, bf16[192,4096]{1,0:T(8,128)(2,1)S(1)}, u32[]{:S(2)}, u32[]{:S(2)}) %collective-permute-start.8) | collective-permute-done | bytes 1572896 | tf_op jit(solution)/shard_map/ppermute | solution.py:64
  110.0 10.2 %grads.6.refs_3_ = f32[512,4096]{1,0:T(8,128)S(1)} custom-call(bf16[192,4096]{1,0:T(8,128)(2,1)S(1)} %collective-permute-done.14.refs_0_, bf16[192,4096]{1,0:T(8,128)(2,1)S(1)} %collective-permute-done.15.refs_1_, bf16[192,4096]{1,0:T(8,128)(2,1)S(1)} %collective-permute-done.8.refs_2_, ...), custom_call_target="tpu_custom_call", output_to_operand_aliasing={{}: (5, {})} | custom-call | flops 6442450944 | bytes 6291456 | tf_op jit(solution)/shard_map/grads/pallas_call | solution.py:166
  120.2 3.2 %collective-permute-done.17.refs_1_ = bf16[192,4096]{1,0:T(8,128)(2,1)S(1)} collective-permute-done((bf16[192,4096]{1,0:T(8,128)(2,1)S(1)}, bf16[192,4096]{1,0:T(8,128)(2,1)S(1)}, u32[]{:S(2)}, u32[]{:S(2)}) %collective-permute-start.17) | collective-permute-done | bytes 1572896 | tf_op jit(solution)/shard_map/ppermute | solution.py:64
  123.9 6.6 %grads.7.refs_4_.refs_5_ = f32[512,4096]{1,0:T(8,128)S(1)} custom-call(bf16[192,4096]{1,0:T(8,128)(2,1)S(1)} %collective-permute-done.16.refs_0_, bf16[192,4096]{1,0:T(8,128)(2,1)S(1)} %collective-permute-done.17.refs_1_, bf16[512,4096]{1,0:T(8,128)(2,1)S(1)} %bitcast.192, f32[512,4096]{1,0:T(8,128)S(1)} %grads.6.refs_3_), custom_call_target="tpu_custom_call", output_to_operand_aliasing={{}: (3, {})} | custom-call | flops 3221225472 | bytes 3145728 | tf_op jit(solution)/shard_map/grads/pallas_call | solution.py:166
  130.5 9.8 %collective-permute-done.11.refs_2_ = bf16[192,4096]{1,0:T(8,128)(2,1)S(1)} collective-permute-done((bf16[192,4096]{1,0:T(8,128)(2,1)S(1)}, bf16[192,4096]{1,0:T(8,128)(2,1)S(1)}, u32[]{:S(2)}, u32[]{:S(2)}) %collective-permute-start.11) | collective-permute-done | bytes 1572896 | tf_op jit(solution)/shard_map/ppermute | solution.py:64
  141.4 9.3 %pseudo_0.1 = (bf16[3,64,2048]{2,1,0:T(8,128)(2,1)S(1)}, bf16[3,64,2048]{2,1,0:T(8,128)(2,1)S(1)}, bf16[2,64,1024]{2,1,0:T(8,128)(2,1)S(1)}, bf16[2,64,1024]{2,1,0:T(8,128)(2,1)S(1)}, bf16[512,384]{1,0:T(8,128)(2,1)S(1)}) custom-call(s32[2]{0:T(128)S(1)} %pad_add_fusion.refs_0_, bf16[192,4096]{1,0:T(8,128)(2,1)S(1)} %collective-permute-done.10.refs_1_, ...), custom_call_target="tpu_custom_call" | custom-call | flops 2415919104 | bytes 15728640 | tf_op jit(solution)/shard_map/pseudo_0/pallas_call | solution.py:260
  156.2 6.4 %pseudo_1.1 = (bf16[3,64,2048]{2,1,0:T(8,128)(2,1)S(1)}, bf16[3,64,2048]{2,1,0:T(8,128)(2,1)S(1)}, bf16[2,64,1024]{2,1,0:T(8,128)(2,1)S(1)}, bf16[2,64,1024]{2,1,0:T(8,128)(2,1)S(1)}) custom-call(s32[2]{0:T(128)S(1)} %pad_add_fusion.refs_0_, bf16[192,4096]{1,0:T(8,128)(2,1)S(1)} %collective-permute-done.10.refs_1_, bf16[192,4096]{1,0:T(8,128)(2,1)} %copy-done.8, ...), custom_call_target="tpu_custom_call" | custom-call | flops 805306368 | bytes 15728640 | tf_op jit(solution)/shard_map/pseudo_1/pallas_call | solution.py:260
  176.8 20.9 %collective-permute-done.26 = bf16[2,64,4096]{2,1,0:T(8,128)(2,1)S(1)} collective-permute-done((bf16[2,64,4096]{2,1,0:T(8,128)(2,1)S(1)}, bf16[2,64,4096]{2,1,0:T(8,128)(2,1)S(1)}, u32[]{:S(2)}, u32[]{:S(2)}) %collective-permute-start.26) | collective-permute-done | bytes 1048608 | tf_op jit(solution)/shard_map/ppermute | solution.py:53
  197.7 3.0 %collective-permute-done.29 = bf16[2,64,4096]{2,1,0:T(8,128)(2,1)S(1)} collective-permute-done((bf16[2,64,4096]{2,1,0:T(8,128)(2,1)S(1)}, bf16[2,64,4096]{2,1,0:T(8,128)(2,1)S(1)}, u32[]{:S(2)}, u32[]{:S(2)}) %collective-permute-start.29) | collective-permute-done | bytes 1048608 | tf_op jit(solution)/shard_map/ppermute | solution.py:53
  208.4 13.0 %collective-permute-done.31.prv = bf16[2,64,4096]{2,1,0:T(8,128)(2,1)S(1)} collective-permute-done((bf16[2,64,4096]{2,1,0:T(8,128)(2,1)S(1)}, bf16[2,64,4096]{2,1,0:T(8,128)(2,1)S(1)}, u32[]{:S(2)}, u32[]{:S(2)}) %collective-permute-start.31) | collective-permute-done | bytes 1048608 | tf_op jit(solution)/shard_map/ppermute | solution.py:53
  221.4 6.6 %collective-permute-done.30.nxt = bf16[2,64,4096]{2,1,0:T(8,128)(2,1)S(1)} collective-permute-done((bf16[2,64,4096]{2,1,0:T(8,128)(2,1)S(1)}, bf16[2,64,4096]{2,1,0:T(8,128)(2,1)S(1)}, u32[]{:S(2)}, u32[]{:S(2)}) %collective-permute-start.30) | collective-permute-done | bytes 1048608 | tf_op jit(solution)/shard_map/ppermute | solution.py:53
  235.7 3.0 %near_own_kernel.1.begun = bf16[8,64,4096]{2,1,0:T(8,128)(2,1)} custom-call(s32[6]{0:T(128)} %pad_add_fusion.1.info, bf16[2,64,4096]{2,1,0:T(8,128)(2,1)} %copy-done.3, bf16[2,64,4096]{2,1,0:T(8,128)(2,1)} %copy-done.7, bf16[2,64,4096]{2,1,0:T(8,128)(2,1)} %copy-done.6), custom_call_target="tpu_custom_call" | custom-call | bytes 4194304 | tf_op jit(solution)/shard_map/near_own_kernel/pallas_call | solution.py:306
  239.5 5.6 %collective-permute-done.35.other_l = bf16[64,2048]{1,0:T(8,128)(2,1)S(1)} collective-permute-done((bf16[64,2048]{1,0:T(8,128)(2,1)S(1)}, bf16[64,2048]{1,0:T(8,128)(2,1)S(1)}, u32[]{:S(2)}, u32[]{:S(2)}) %collective-permute-start.35) | collective-permute-done | bytes 262176 | tf_op jit(solution)/shard_map/ppermute | solution.py:53
  245.9 3.2 %rest_kernel.1 = bf16[8,64,4096]{2,1,0:T(8,128)(2,1)} custom-call(s32[6]{0:T(128)} %pad_add_fusion.1.info, bf16[3,64,4096]{2,1,0:T(8,128)(2,1)} %collective-permute-done.32.near, bf16[64,2048]{1,0:T(8,128)(2,1)} %copy-done.9, bf16[64,2048]{1,0:T(8,128)(2,1)} %copy-done.10, bf16[64,2048]{1,0:T(8,128)(2,1)} %copy-done.11, ...), custom_call_target="tpu_custom_call", output_to_operand_aliasing={{}: (6, {})} | custom-call | bytes 4194304 | tf_op jit(solution)/shard_map/rest_kernel/pallas_call | solution.py:306
  (144 shorter events, 64.3 us)
Async XLA Ops:
  0.6 25.6 %collective-permute-start.3 = (bf16[192,2048]{1,0:T(8,128)(2,1)}, bf16[192,2048]{1,0:T(8,128)(2,1)S(1)}, u32[]{:S(2)}, u32[]{:S(2)}) collective-permute-start(bf16[192,2048]{1,0:T(8,128)(2,1)} %bitcast.200), channel_id=1, source_target_pairs={{0,3},{1,0},{2,1},{3,2},{4,7},{5,4},{6,5},{7,6},{8,11},{9,8},{10,9... | collective-permute-start | bytes 2359304 | tf_op jit(solution)/shard_map/ppermute | solution.py:64
  5.3 24.6 %collective-permute-start.1 = (bf16[192,2048]{1,0:T(8,128)(2,1)}, bf16[192,2048]{1,0:T(8,128)(2,1)S(1)}, u32[]{:S(2)}, u32[]{:S(2)}) collective-permute-start(bf16[192,2048]{1,0:T(8,128)(2,1)} %bitcast.201), channel_id=1, source_target_pairs={{0,1},{1,2},{2,3},{3,0},{4,5},{5,6},{6,7},{7,4},{8,9},{9,10},{10,1... | collective-permute-start | bytes 2359304 | tf_op jit(solution)/shard_map/ppermute | solution.py:64
  5.3 21.0 %collective-permute-start = (bf16[192,2048]{1,0:T(8,128)(2,1)}, bf16[192,2048]{1,0:T(8,128)(2,1)S(1)}, u32[]{:S(2)}, u32[]{:S(2)}) collective-permute-start(bf16[192,2048]{1,0:T(8,128)(2,1)} %bitcast.203), channel_id=1, source_target_pairs={{0,1},{1,2},{2,3},{3,0},{4,5},{5,6},{6,7},{7,4},{8,9},{9,10},{10,1... | collective-permute-start | bytes 2359304 | tf_op jit(solution)/shard_map/ppermute | solution.py:64
  5.3 41.2 %collective-permute-start.7 = (bf16[192,2048]{1,0:T(8,128)(2,1)}, bf16[192,2048]{1,0:T(8,128)(2,1)S(1)}, u32[]{:S(2)}, u32[]{:S(2)}) collective-permute-start(bf16[192,2048]{1,0:T(8,128)(2,1)} %bitcast.204), channel_id=1, source_target_pairs={{0,3},{1,0},{2,1},{3,2},{4,7},{5,4},{6,5},{7,6},{8,11},{9,8},{10,9... | collective-permute-start | bytes 2359304 | tf_op jit(solution)/shard_map/ppermute | solution.py:64
  26.3 15.7 %collective-permute-start.2 = (bf16[192,2048]{1,0:T(8,128)(2,1)S(1)}, bf16[192,2048]{1,0:T(8,128)(2,1)S(1)}, u32[]{:S(2)}, u32[]{:S(2)}) collective-permute-start(bf16[192,2048]{1,0:T(8,128)(2,1)S(1)} %collective-permute-done), channel_id=1, source_target_pairs={{0,1},{1,2},{2,3},{3,0},{4,5},{5,6},{6,7},{7,4},{8,9},{9,10},{10,1... | collective-permute-start | bytes 2359304 | tf_op jit(solution)/shard_map/ppermute | solution.py:64
  26.3 15.7 %collective-permute-start.4 = (bf16[192,2048]{1,0:T(8,128)(2,1)S(1)}, bf16[192,2048]{1,0:T(8,128)(2,1)S(1)}, u32[]{:S(2)}, u32[]{:S(2)}) collective-permute-start(bf16[192,2048]{1,0:T(8,128)(2,1)S(1)} %collective-permute-done.3), channel_id=1, source_target_pairs={{0,3},{1,0},{2,1},{3,2},{4,7},{5,4},{6,5},{7,6},{8,11},{9,8},{10,9... | collective-permute-start | bytes 2359304 | tf_op jit(solution)/shard_map/ppermute | solution.py:64
  29.0 27.5 %collective-permute-start.12 = (bf16[192,4096]{1,0:T(8,128)(2,1)S(1)}, bf16[192,4096]{1,0:T(8,128)(2,1)S(1)}, u32[]{:S(2)}, u32[]{:S(2)}) collective-permute-start(bf16[192,4096]{1,0:T(8,128)(2,1)S(1)} %pad_maximum_fusion.refs_0_), channel_id=1, source_target_pairs={{0,4},{1,5},{2,6},{3,7},{4,8},{5,9},{6,10},{7,11},{8,12},{9,13},{1... | collective-permute-start | bytes 4718600 | tf_op jit(solution)/shard_map/ppermute | solution.py:64
  29.9 26.6 %collective-permute-start.13 = (bf16[192,4096]{1,0:T(8,128)(2,1)S(1)}, bf16[192,4096]{1,0:T(8,128)(2,1)S(1)}, u32[]{:S(2)}, u32[]{:S(2)}) collective-permute-start(bf16[192,4096]{1,0:T(8,128)(2,1)S(1)} %pad_maximum_fusion.refs_0_), channel_id=1, source_target_pairs={{0,12},{1,13},{2,14},{3,15},{4,0},{5,1},{6,2},{7,3},{8,4},{9,5},{1... | collective-permute-start | bytes 4718600 | tf_op jit(solution)/shard_map/ppermute | solution.py:64
  41.9 31.4 %collective-permute-start.5 = (bf16[192,4096]{1,0:T(8,128)(2,1)S(1)}, bf16[192,4096]{1,0:T(8,128)(2,1)S(1)}, u32[]{:S(2)}, u32[]{:S(2)}) collective-permute-start(bf16[192,4096]{1,0:T(8,128)(2,1)S(1)} %constant_dynamic-update-slice_fusion.refs_1_), channel_id=1, source_target_pairs={{0,4},{1,5},{2,6},{3,7},{4,8},{5,9},{6,10},{7,11},{8,12},{9,13},{1... | collective-permute-start | bytes 4718600 | tf_op jit(solution)/shard_map/ppermute | solution.py:64
  45.3 28.1 %collective-permute-start.6 = (bf16[192,4096]{1,0:T(8,128)(2,1)S(1)}, bf16[192,4096]{1,0:T(8,128)(2,1)S(1)}, u32[]{:S(2)}, u32[]{:S(2)}) collective-permute-start(bf16[192,4096]{1,0:T(8,128)(2,1)S(1)} %constant_dynamic-update-slice_fusion.refs_1_), channel_id=1, source_target_pairs={{0,12},{1,13},{2,14},{3,15},{4,0},{5,1},{6,2},{7,3},{8,4},{9,5},{1... | collective-permute-start | bytes 4718600 | tf_op jit(solution)/shard_map/ppermute | solution.py:64
  56.5 33.7 %collective-permute-start.14 = (bf16[192,4096]{1,0:T(8,128)(2,1)S(1)}, bf16[192,4096]{1,0:T(8,128)(2,1)S(1)}, u32[]{:S(2)}, u32[]{:S(2)}) collective-permute-start(bf16[192,4096]{1,0:T(8,128)(2,1)S(1)} %constant_dynamic-update-slice_fusion.4.refs_2_), channel_id=1, source_target_pairs={{0,4},{1,5},{2,6},{3,7},{4,8},{5,9},{6,10},{7,11},{8,12},{9,13},{1... | collective-permute-start | bytes 4718600 | tf_op jit(solution)/shard_map/ppermute | solution.py:64
  56.5 33.7 %collective-permute-start.15 = (bf16[192,4096]{1,0:T(8,128)(2,1)S(1)}, bf16[192,4096]{1,0:T(8,128)(2,1)S(1)}, u32[]{:S(2)}, u32[]{:S(2)}) collective-permute-start(bf16[192,4096]{1,0:T(8,128)(2,1)S(1)} %constant_dynamic-update-slice_fusion.4.refs_2_), channel_id=1, source_target_pairs={{0,12},{1,13},{2,14},{3,15},{4,0},{5,1},{6,2},{7,3},{8,4},{9,5},{1... | collective-permute-start | bytes 4718600 | tf_op jit(solution)/shard_map/ppermute | solution.py:64
  73.3 33.7 %collective-permute-start.8 = (bf16[192,4096]{1,0:T(8,128)(2,1)S(1)}, bf16[192,4096]{1,0:T(8,128)(2,1)S(1)}, u32[]{:S(2)}, u32[]{:S(2)}) collective-permute-start(bf16[192,4096]{1,0:T(8,128)(2,1)S(1)} %constant_dynamic-update-slice_fusion.2.refs_3_), channel_id=1, source_target_pairs={{0,4},{1,5},{2,6},{3,7},{4,8},{5,9},{6,10},{7,11},{8,12},{9,13},{1... | collective-permute-start | bytes 4718600 | tf_op jit(solution)/shard_map/ppermute | solution.py:64
  73.3 33.7 %collective-permute-start.9 = (bf16[192,4096]{1,0:T(8,128)(2,1)S(1)}, bf16[192,4096]{1,0:T(8,128)(2,1)S(1)}, u32[]{:S(2)}, u32[]{:S(2)}) collective-permute-start(bf16[192,4096]{1,0:T(8,128)(2,1)S(1)} %constant_dynamic-update-slice_fusion.2.refs_3_), channel_id=1, source_target_pairs={{0,12},{1,13},{2,14},{3,15},{4,0},{5,1},{6,2},{7,3},{8,4},{9,5},{1... | collective-permute-start | bytes 4718600 | tf_op jit(solution)/shard_map/ppermute | solution.py:64
  90.2 33.3 %collective-permute-start.17 = (bf16[192,4096]{1,0:T(8,128)(2,1)S(1)}, bf16[192,4096]{1,0:T(8,128)(2,1)S(1)}, u32[]{:S(2)}, u32[]{:S(2)}) collective-permute-start(bf16[192,4096]{1,0:T(8,128)(2,1)S(1)} %collective-permute-done.15.refs_1_), channel_id=1, source_target_pairs={{0,12},{1,13},{2,14},{3,15},{4,0},{5,1},{6,2},{7,3},{8,4},{9,5},{1... | collective-permute-start | bytes 4718600 | tf_op jit(solution)/shard_map/ppermute | solution.py:64
  93.1 30.7 %collective-permute-start.16 = (bf16[192,4096]{1,0:T(8,128)(2,1)S(1)}, bf16[192,4096]{1,0:T(8,128)(2,1)S(1)}, u32[]{:S(2)}, u32[]{:S(2)}) collective-permute-start(bf16[192,4096]{1,0:T(8,128)(2,1)S(1)} %collective-permute-done.12.refs_0_), channel_id=1, source_target_pairs={{0,4},{1,5},{2,6},{3,7},{4,8},{5,9},{6,10},{7,11},{8,12},{9,13},{1... | collective-permute-start | bytes 4718600 | tf_op jit(solution)/shard_map/ppermute | solution.py:64
  107.0 33.3 %collective-permute-start.11 = (bf16[192,4096]{1,0:T(8,128)(2,1)S(1)}, bf16[192,4096]{1,0:T(8,128)(2,1)S(1)}, u32[]{:S(2)}, u32[]{:S(2)}) collective-permute-start(bf16[192,4096]{1,0:T(8,128)(2,1)S(1)} %collective-permute-done.9.refs_3_), channel_id=1, source_target_pairs={{0,12},{1,13},{2,14},{3,15},{4,0},{5,1},{6,2},{7,3},{8,4},{9,5},{1... | collective-permute-start | bytes 4718600 | tf_op jit(solution)/shard_map/ppermute | solution.py:64
  110.0 30.4 %collective-permute-start.10 = (bf16[192,4096]{1,0:T(8,128)(2,1)S(1)}, bf16[192,4096]{1,0:T(8,128)(2,1)S(1)}, u32[]{:S(2)}, u32[]{:S(2)}) collective-permute-start(bf16[192,4096]{1,0:T(8,128)(2,1)S(1)} %collective-permute-done.5.refs_2_), channel_id=1, source_target_pairs={{0,4},{1,5},{2,6},{3,7},{4,8},{5,9},{6,10},{7,11},{8,12},{9,13},{1... | collective-permute-start | bytes 4718600 | tf_op jit(solution)/shard_map/ppermute | solution.py:64
  174.2 23.6 %collective-permute-start.26 = (bf16[2,64,4096]{2,1,0:T(8,128)(2,1)S(1)}, bf16[2,64,4096]{2,1,0:T(8,128)(2,1)S(1)}, u32[]{:S(2)}, u32[]{:S(2)}) collective-permute-start(bf16[2,64,4096]{2,1,0:T(8,128)(2,1)S(1)} %pad_maximum_fusion.2), channel_id=1, source_target_pairs={{0,32},{16,112},{32,64},{48,16},{64,96},{80,48},{96,0},{112,80},{1... | collective-permute-start | bytes 3145736 | tf_op jit(solution)/shard_map/ppermute | solution.py:53
  175.5 25.2 %collective-permute-start.29 = (bf16[2,64,4096]{2,1,0:T(8,128)(2,1)S(1)}, bf16[2,64,4096]{2,1,0:T(8,128)(2,1)S(1)}, u32[]{:S(2)}, u32[]{:S(2)}) collective-permute-start(bf16[2,64,4096]{2,1,0:T(8,128)(2,1)S(1)} %pad_maximum_fusion.3), channel_id=1, source_target_pairs={{0,96},{16,48},{32,0},{48,80},{64,32},{80,112},{96,64},{112,16},{1... | collective-permute-start | bytes 3145736 | tf_op jit(solution)/shard_map/ppermute | solution.py:53
  201.7 19.7 %collective-permute-start.31 = (bf16[2,64,4096]{2,1,0:T(8,128)(2,1)S(1)}, bf16[2,64,4096]{2,1,0:T(8,128)(2,1)S(1)}, u32[]{:S(2)}, u32[]{:S(2)}) collective-permute-start(bf16[2,64,4096]{2,1,0:T(8,128)(2,1)S(1)} %get-tuple-element.55.own), channel_id=1, source_target_pairs={{0,32},{16,112},{32,64},{48,16},{64,96},{80,48},{96,0},{112,80},{1... | collective-permute-start | bytes 3145736 | tf_op jit(solution)/shard_map/ppermute | solution.py:53
  206.9 21.1 %collective-permute-start.30 = (bf16[2,64,4096]{2,1,0:T(8,128)(2,1)S(1)}, bf16[2,64,4096]{2,1,0:T(8,128)(2,1)S(1)}, u32[]{:S(2)}, u32[]{:S(2)}) collective-permute-start(bf16[2,64,4096]{2,1,0:T(8,128)(2,1)S(1)} %get-tuple-element.55.own), channel_id=1, source_target_pairs={{0,96},{16,48},{32,0},{48,80},{64,32},{80,112},{96,64},{112,16},{1... | collective-permute-start | bytes 3145736 | tf_op jit(solution)/shard_map/ppermute | solution.py:53
  229.5 15.6 %collective-permute-start.32 = (bf16[3,64,4096]{2,1,0:T(8,128)(2,1)}, bf16[3,64,4096]{2,1,0:T(8,128)(2,1)}, u32[]{:S(2)}, u32[]{:S(2)}) collective-permute-start(bf16[3,64,4096]{2,1,0:T(8,128)(2,1)} %pad_maximum_fusion.1), channel_id=1, source_target_pairs={{0,16},{16,0},{32,48},{48,32},{64,80},{80,64},{96,112},{112,96},{1... | collective-permute-start | bytes 4718600 | tf_op jit(solution)/shard_map/ppermute | solution.py:53
  231.2 13.9 %collective-permute-start.35 = (bf16[64,2048]{1,0:T(8,128)(2,1)S(1)}, bf16[64,2048]{1,0:T(8,128)(2,1)S(1)}, u32[]{:S(2)}, u32[]{:S(2)}) collective-permute-start(bf16[64,2048]{1,0:T(8,128)(2,1)S(1)} %get-tuple-element.63), channel_id=1, source_target_pairs={{0,48},{16,96},{32,80},{48,0},{64,112},{80,32},{96,16},{112,64},{1... | collective-permute-start | bytes 786440 | tf_op jit(solution)/shard_map/ppermute | solution.py:53
  (26 other events, 262.6 us)

commit v3 on v2

--- a/solution.py
+++ b/solution.py
@@ -199,78 +199,66 @@
     return (first_new / (root + ADAM_EPS) + (INNER_RATE * DECAY) * start.astype(F32)).astype(BF16)
 
 
-def pseudo_kernel(n, part, features, hidden_scale, *refs):
+def pseudo_kernel(n, features, hidden_scale, *refs):
     where, pieces = refs[0], refs[1 : 1 + n]
-    base = part * features
-    if part == 0:
-        w, acc, m, v, keep, swap, far_keep, far_swap, act_t = refs[1 + n : 10 + n]
-        total, dpre_t, right, sem = refs[10 + n :]
-        fetch(pieces, right, sem)
-        hidden_both(right, w, act_t, dpre_t, features, hidden_scale)
-        left, scale = dpre_t, features ** (-0.5)
-    else:
-        left, w, acc, m, v, keep, swap, far_keep, far_swap, total, right, sem = refs[1 + n :]
-        scale = hidden_scale
-        fetch(pieces, right, sem, pl.ds(base, features))
+    w, acc, m, v, keep, swap, far_keep, far_swap, total, act_t, dpre_t, xg, sem = refs[1 + n :]
+    fetch(pieces, xg, sem)
+    hidden_both(xg, w, act_t, dpre_t, features, hidden_scale)
     y, core = where[0], where[1]
     rows = w.shape[0] // SETS
-    per = far_keep.shape[2] // COLS
-
-    def columns(j, carry):
-        here = pl.ds(pl.multiple_of(j * COLS, COLS), COLS)
-        cols = pl.ds(pl.multiple_of(base + j * COLS, COLS), COLS)
-        total[...] = acc[:, cols] + jnp.dot(left[...], right[:, here], preferred_element_type=F32)
-
-        def stepped(d, parity):
-            chip = lax.rem(y + jnp.where(parity == 0, d, YS - d), YS)
-            at = pl.ds(pl.multiple_of((2 * chip + parity) * rows, rows), rows)
-            return adam(total[at, :], scale, m[at, cols], v[at, cols], w[at, cols])
-
-        def ring(i, carry):
-            for out, parity in ((keep, core), (swap, 1 - core)):
-                out[i, :, here] = stepped(i + i // 2, parity)
+    for half, left, scale in ((0, dpre_t, features ** (-0.5)), (1, act_t, hidden_scale)):
+
+        def columns(j, carry, half=half, left=left, scale=scale):
+            here = pl.ds(pl.multiple_of(j * COLS, COLS), COLS)
+            cols = pl.ds(pl.multiple_of(half * features + j * COLS, COLS), COLS)
+            total[...] = acc[:, cols] + jnp.dot(left[...], xg[:, cols], preferred_element_type=F32)
+
+            def stepped(d, parity):
+                chip = lax.rem(y + jnp.where(parity == 0, d, YS - d), YS)
+                at = pl.ds(pl.multiple_of((2 * chip + parity) * rows, rows), rows)
+                return adam(total[at, :], scale, m[at, cols], v[at, cols], w[at, cols])
+
+            def ring(i, carry):
+                for out, parity in ((keep, core), (swap, 1 - core)):
+                    out[i, :, cols] = stepped(i + i // 2, parity)
+                return carry
+
+            lax.fori_loop(0, YS - 1, ring, carry)
+            for out, parity in ((far_keep, core), (far_swap, 1 - core)):
+                out[half, :, here] = stepped(2, parity)
             return carry
 
-        lax.fori_loop(0, YS - 1, ring, carry)
-        put = pl.ds(pl.multiple_of(lax.rem(j, per) * COLS, COLS), COLS)
-        for out, parity in ((far_keep, core), (far_swap, 1 - core)):
-            out[lax.div(j, per), :, put] = stepped(2, parity)
-        return carry
-
-    lax.fori_loop(0, features // COLS, columns, 0)
-
-
-def last_pseudo(part, where, pieces, act, w, acc, m, v, hidden_scale):
+        lax.fori_loop(0, features // COLS, columns, 0)
+
+
+def last_pseudo(where, pieces, w, acc, m, v, hidden_scale):
     n = len(pieces)
     units, width = w.shape
     features = width // 2
     rows = units // SETS
     tokens = sum(p.shape[0] for p in pieces)
-    hid = (units, tokens)
-    near = pltpu.VMEM((YS - 1, rows, features), BF16)
-    far = pltpu.VMEM((2, rows, features // 2), BF16)
-    out_shape = [near, near, far, far]
-    scratch = [pltpu.VMEM((units, COLS), F32)]
-    if part == 0:
-        out_shape.append(pltpu.VMEM(hid, BF16))
-        scratch += [pltpu.VMEM(hid, BF16), pltpu.VMEM((tokens, width), BF16)]
-    else:
-        scratch += [pltpu.VMEM((tokens, features), BF16)]
-    tail = (() if part == 0 else (act,)) + (w, acc, m, v)
+    near = pltpu.VMEM((YS - 1, rows, width), BF16)
+    far = pltpu.VMEM((2, rows, features), BF16)
     return pl.pallas_call(
-        functools.partial(pseudo_kernel, n, part, features, hidden_scale),
-        in_specs=[pl.BlockSpec(memory_space=pltpu.SMEM)] + [HBM] * n + [VMEM] * len(tail),
-        out_specs=[VMEM] * len(out_shape),
-        scratch_shapes=scratch + [pltpu.SemaphoreType.DMA((n,))],
-        out_shape=out_shape,
+        functools.partial(pseudo_kernel, n, features, hidden_scale),
+        in_specs=[pl.BlockSpec(memory_space=pltpu.SMEM)] + [HBM] * n + [VMEM] * 4,
+        out_specs=[VMEM] * 4,
+        scratch_shapes=[
+            pltpu.VMEM((units, COLS), F32),
+            pltpu.VMEM((units, tokens), BF16),
+            pltpu.VMEM((units, tokens), BF16),
+            pltpu.VMEM((tokens, width), BF16),
+            pltpu.SemaphoreType.DMA((n,)),
+        ],
+        out_shape=[near, near, far, far],
         compiler_params=pltpu.CompilerParams(vmem_limit_bytes=LIMIT),
         cost_estimate=pl.CostEstimate(
-            flops=(6 if part == 0 else 2) * features * tokens * units,
-            bytes_accessed=units * features * 12 + tokens * width * 2,
+            flops=8 * features * tokens * units,
+            bytes_accessed=units * width * 12 + tokens * width * 2,
             transcendentals=units * tokens,
         ),
-        name="pseudo_%d" % part,
-    )(where, *pieces, *tail)
+        name="pseudo",
+    )(where, *pieces, w, acc, m, v)
 
 
 def home(info, d, parity):
@@ -292,10 +280,13 @@
     )
 
 
-def rest_kernel(info, near, own_l, own_r, other_l, other_r, begun, out, sem):
+def rest_kernel(info, near_own, near, own_l, own_r, other_l, other_r, begun, out, sem):
     half = own_l.shape[1]
     left, right = pl.ds(0, half), pl.ds(half, half)
-    pairs = [(near.at[i], out.at[home(info, d, 1 - info[1])]) for i, d in enumerate((0, 1, 3))]
+    pairs = [
+        (a, out.at[home(info, d, 1 - info[1])])
+        for a, d in ((near_own, 0), (near.at[0], 1), (near.at[1], 3))
+    ]
     for parity, l, r in ((info[1], own_l, own_r), (1 - info[1], other_l, other_r)):
         far = home(info, 2, parity)
         pairs += [(l, out.at[far, :, left]), (r, out.at[far, :, right])]
@@ -375,8 +366,9 @@
         ((-1, 1), (1, 1), (-1, 2), (1, 2)),
         ((2, 0), (2, 1)),
     )
-    w, where, weights, picks, share, info = lax.optimization_barrier(
-        (w, where, weights, picks, share, info)
+    seconds = {k: picks[k] == 1 for k in (4, 5, 7, 8, 9, 10, 11)}
+    w, where, weights, seconds, share, info = lax.optimization_barrier(
+        (w, where, weights, seconds, share, info)
     )
     w, m, v = resident(w), resident(m), resident(v)
     acc = None
@@ -391,7 +383,6 @@
 
     common = common_expert_parameters[0]
     inertia = outer_inertia[0]
-    mid = features // 2
 
     def weighed(k, a):
         return weights[k][:, None, None] * a.astype(F32)[None]
@@ -401,44 +392,40 @@
         rights = on_path(far_keep[1], -1), on_path(far_swap[1], 1, 1)
         return (on_path(swap, 0, 1), *lefts, *rights)
 
-    def sums(keep, came):
-        near = came[0]
-
-        def merged(i, d, lo=0, hi=features):
-            return weighed(d, keep[i, :, lo:hi]) + weighed(4 + d, near[i, :, lo:hi])
-
-        up = [merged(1, 1, 0, mid) + weighed(8, came[1]) + weighed(9, came[2]), merged(1, 1, mid)]
-        down = [merged(2, 3, 0, mid), merged(2, 3, mid) + weighed(10, came[3]) + weighed(11, came[4])]
-        return merged(0, 0), up, down
-
-    acc = resident(acc)
-    keep_0, *out_0, act = last_pseudo(0, where, rest, None, w, acc, m, v, hidden_scale)
-    came_0 = exchange(*out_0)
-    keep_1, *out_1 = last_pseudo(1, where, rest, resident(act), w, acc, m, v, hidden_scale)
-    came_1 = exchange(*lax.optimization_barrier((*out_1, *came_0))[:3])
-    here_0, up_0, down_0 = sums(keep_0, came_0)
-    here_1, up_1, down_1 = sums(keep_1, came_1)
-    part_up = on_path(jnp.concatenate([a.astype(BF16) for a in up_0 + up_1], -1), 1)
-    part_down = on_path(jnp.concatenate([a.astype(BF16) for a in down_0 + down_1], -1), -1)
-
-    total = jnp.concatenate([here_0, here_1], -1) + part_up.astype(F32) + part_down.astype(F32)
-    average = total / share
-    new_inertia = INERTIA_FACTOR * inertia + average
-    new_experts = common - GLOBAL_LEARNING * (average + INERTIA_FACTOR * new_inertia)
-    updated = new_experts.astype(BF16)
+    keep, *outs = last_pseudo(where, rest, w, resident(acc), m, v, hidden_scale)
+    mate_keep, l_same, l_cross, r_same, r_cross = exchange(*outs)
+
+    def merged(i, d, lo=0, hi=width):
+        return weighed(d, keep[i, :, lo:hi]) + weighed(4 + d, mate_keep[i, :, lo:hi])
+
+    up_l = merged(1, 1, 0, features) + weighed(8, l_same) + weighed(9, l_cross)
+    down_r = merged(2, 3, features) + weighed(10, r_same) + weighed(11, r_cross)
+    up = jnp.concatenate([up_l.astype(BF16), merged(1, 1, features).astype(BF16)], -1)
+    down = jnp.concatenate([merged(2, 3, 0, features).astype(BF16), down_r.astype(BF16)], -1)
+    part_up, part_down = on_path(up, 1), on_path(down, -1)
+    total = merged(0, 0) + part_up.astype(F32) + part_down.astype(F32)
+
+    def refreshed(total):
+        average = total / share
+        new_inertia = INERTIA_FACTOR * inertia + average
+        return common - GLOBAL_LEARNING * (average + INERTIA_FACTOR * new_inertia), new_inertia
+
+    updated = refreshed(total)[0].astype(BF16)
     prv, nxt = on_path(updated, 1), on_path(updated, -1)
+    new_experts, new_inertia = refreshed(after(total, prv, nxt))
 
     def picked(k, a, lo=0, hi=width):
-        return jnp.where(picks[k] == 1, a[1, :, lo:hi], a[0, :, lo:hi])
+        return jnp.where(seconds[k], a[1, :, lo:hi], a[0, :, lo:hi])
 
     own_l = on_path(picked(8, prv, 0, features), 1)
     other_l = on_path(picked(9, prv, 0, features), 1, 1)
     own_r = on_path(picked(10, nxt, features), -1)
     other_r = on_path(picked(11, nxt, features), -1, 1)
-    near = on_path(jnp.stack([picked(4, updated), picked(5, nxt), picked(7, prv)]), 0, 1)
+    near_own = on_path(picked(4, updated), 0, 1)
+    near = on_path(jnp.stack([picked(5, nxt), picked(7, prv)]), 0, 1)
     returned = assemble(near_own_kernel, info, (updated, nxt, prv), (), 3, rows, width)
     far = (own_l, own_r, other_l, other_r)
-    returned = assemble(rest_kernel, info, (near, *far), (returned,), 7, rows, width)
+    returned = assemble(rest_kernel, info, (near_own, near, *far), (returned,), 7, rows, width)
     return (new_experts[None], new_inertia[None], returned[None])
 
 

time: 250 us -> 249 us (level)
    ppermute x18, waiting for transfers between devices: 59.9 us -> 54.8 us  [send(): return lax.ppermute(a, ('path', 'fsdp'), plane_hop(*to))]
    ppermute x19 -> x15, waiting for transfers between devices: 55.6 us -> 59.8 us  [on_path(): return lax.ppermute(a, 'path', path_hop(hop, flip))]
    ppermute x19 -> x15, starting transfers between devices: 16.4 us -> 14.8 us  [on_path(): return lax.ppermute(a, 'path', path_hop(hop, flip))]
    pallas_call x2 -> x1, Pallas kernels: 15.6 us -> 14.2 us  [last_pseudo(): pl.pallas_call(functools.partial(pseudo_kernel, n, features, hidden_scale...]
  transfers between devices with their start and end apart: 37 -> 33, of which waited for: 19 -> 20; matrix products, arithmetic and copies ran while one was open for 7% -> 8% of each run, Pallas kernels for 19% -> 16%
where the time goes in v3:
time: 249 us; the launch traced here: 247 us
  waiting for transfers between devices  115 us (46%)
  Pallas kernels  57 us (23%)
  starting transfers between devices  44 us (18%)
  local copies, waits for them, and re-layouts  12.3 us (5%)
  other arithmetic  12.2 us (5%)
  between operations  6.93 us (3%)
    ppermute x15, waiting for transfers between devices, on_path(): return lax.ppermute(a, 'path', path_hop(hop, flip))  59.8 us
    ppermute x18, waiting for transfers between devices, send(): return lax.ppermute(a, ('path', 'fsdp'), plane_hop(*to))  54.8 us
    pallas_call x4, Pallas kernels, accumulate(): pl.pallas_call(functools.partial(grads_kernel, n, first, features, hidden...  36.5 us
    ppermute x18, starting transfers between devices, send(): return lax.ppermute(a, ('path', 'fsdp'), plane_hop(*to))  29.3 us
    ppermute x15, starting transfers between devices, on_path(): return lax.ppermute(a, 'path', path_hop(hop, flip))  14.8 us
    pallas_call x1, Pallas kernels, last_pseudo(): pl.pallas_call(functools.partial(pseudo_kernel, n, features, hidden_scale...  14.2 us
    pallas_call x2, Pallas kernels, assemble(): pl.pallas_call(kernel, in_specs=[pl.BlockSpec(memory_space=pltpu.SMEM)] +...  6.25 us
  transfers between devices with their start and end apart: 33, of which 20 were waited for; matrix products, arithmetic and copies ran while one was open for 8% of the time, Pallas kernels for 16%

profile of v3, /device:TPU:1, one launch (start us, length us, event | category | flops | bytes accessed | tf_op | source)
XLA Modules:
  0.0 247.0 jit_solution(6311431078427234152)
XLA Ops:
  0.6 4.7 %collective-permute-start.3 = (bf16[192,2048]{1,0:T(8,128)(2,1)}, bf16[192,2048]{1,0:T(8,128)(2,1)S(1)}, u32[]{:S(2)}, u32[]{:S(2)}) collective-permute-start(bf16[192,2048]{1,0:T(8,128)(2,1)} %bitcast.157), channel_id=1, source_target_pairs={{0,3},{1,0},{2,1},{3,2},{4,7},{5,4},{6,5},{7,6},{8,11},{9,8},{10,9... | collective-permute-start | bytes 2359304 | tf_op jit(solution)/shard_map/ppermute | solution.py:64
  32.3 9.6 %collective-permute-done.2 = bf16[192,2048]{1,0:T(8,128)(2,1)S(1)} collective-permute-done((bf16[192,2048]{1,0:T(8,128)(2,1)S(1)}, bf16[192,2048]{1,0:T(8,128)(2,1)S(1)}, u32[]{:S(2)}, u32[]{:S(2)}) %collective-permute-start.2) | collective-permute-done | bytes 786464 | tf_op jit(solution)/shard_map/ppermute | solution.py:64
  41.9 3.8 %collective-permute-start.5 = (bf16[192,4096]{1,0:T(8,128)(2,1)S(1)}, bf16[192,4096]{1,0:T(8,128)(2,1)S(1)}, u32[]{:S(2)}, u32[]{:S(2)}) collective-permute-start(bf16[192,4096]{1,0:T(8,128)(2,1)S(1)} %constant_dynamic-update-slice_fusion.refs_1_), channel_id=1, source_target_pairs={{0,4},{1,5},{2,6},{3,7},{4,8},{5,9},{6,10},{7,11},{8,12},{9,13},{1... | collective-permute-start | bytes 4718600 | tf_op jit(solution)/shard_map/ppermute | solution.py:64
  46.9 9.5 %collective-permute-done.12.refs_0_ = bf16[192,4096]{1,0:T(8,128)(2,1)S(1)} collective-permute-done((bf16[192,4096]{1,0:T(8,128)(2,1)S(1)}, bf16[192,4096]{1,0:T(8,128)(2,1)S(1)}, u32[]{:S(2)}, u32[]{:S(2)}) %collective-permute-start.12) | collective-permute-done | bytes 1572896 | tf_op jit(solution)/shard_map/ppermute | solution.py:64
  56.5 3.0 %collective-permute-start.15 = (bf16[192,4096]{1,0:T(8,128)(2,1)S(1)}, bf16[192,4096]{1,0:T(8,128)(2,1)S(1)}, u32[]{:S(2)}, u32[]{:S(2)}) collective-permute-start(bf16[192,4096]{1,0:T(8,128)(2,1)S(1)} %constant_dynamic-update-slice_fusion.4.refs_2_), channel_id=1, source_target_pairs={{0,12},{1,13},{2,14},{3,15},{4,0},{5,1},{6,2},{7,3},{8,4},{9,5},{1... | collective-permute-start | bytes 4718600 | tf_op jit(solution)/shard_map/ppermute | solution.py:64
  59.4 9.7 %grads.4.refs_5_ = f32[512,4096]{1,0:T(8,128)S(1)} custom-call(bf16[192,4096]{1,0:T(8,128)(2,1)S(1)} %pad_maximum_fusion.refs_0_, bf16[192,4096]{1,0:T(8,128)(2,1)S(1)} %constant_dynamic-update-slice_fusion.refs_1_, bf16[192,4096]{1,0:T(8,128)(2,1)S(1)} %constant_dynamic-update-slice_fusion.4.refs_2_, ...), custom_call_target="tpu_custom_call" | custom-call | flops 6442450944 | bytes 6291456 | tf_op jit(solution)/shard_map/grads/pallas_call | solution.py:166
  69.2 4.1 %collective-permute-done.5.refs_2_ = bf16[192,4096]{1,0:T(8,128)(2,1)S(1)} collective-permute-done((bf16[192,4096]{1,0:T(8,128)(2,1)S(1)}, bf16[192,4096]{1,0:T(8,128)(2,1)S(1)}, u32[]{:S(2)}, u32[]{:S(2)}) %collective-permute-start.5) | collective-permute-done | bytes 1572896 | tf_op jit(solution)/shard_map/ppermute | solution.py:64
  73.3 3.0 %collective-permute-start.9 = (bf16[192,4096]{1,0:T(8,128)(2,1)S(1)}, bf16[192,4096]{1,0:T(8,128)(2,1)S(1)}, u32[]{:S(2)}, u32[]{:S(2)}) collective-permute-start(bf16[192,4096]{1,0:T(8,128)(2,1)S(1)} %constant_dynamic-update-slice_fusion.2.refs_3_), channel_id=1, source_target_pairs={{0,12},{1,13},{2,14},{3,15},{4,0},{5,1},{6,2},{7,3},{8,4},{9,5},{1... | collective-permute-start | bytes 4718600 | tf_op jit(solution)/shard_map/ppermute | solution.py:64
  76.3 10.1 %grads.5.refs_5_ = f32[512,4096]{1,0:T(8,128)S(1)} custom-call(bf16[192,4096]{1,0:T(8,128)(2,1)S(1)} %collective-permute-done.12.refs_0_, bf16[192,4096]{1,0:T(8,128)(2,1)S(1)} %collective-permute-done.13.refs_1_, bf16[192,4096]{1,0:T(8,128)(2,1)S(1)} %collective-permute-done.5.refs_2_, ...), custom_call_target="tpu_custom_call", output_to_operand_aliasing={{}: (5, {})} | custom-call | flops 6442450944 | bytes 6291456 | tf_op jit(solution)/shard_map/grads/pallas_call | solution.py:166
  86.4 3.8 %collective-permute-done.14.refs_0_ = bf16[192,4096]{1,0:T(8,128)(2,1)S(1)} collective-permute-done((bf16[192,4096]{1,0:T(8,128)(2,1)S(1)}, bf16[192,4096]{1,0:T(8,128)(2,1)S(1)}, u32[]{:S(2)}, u32[]{:S(2)}) %collective-permute-start.14) | collective-permute-done | bytes 1572896 | tf_op jit(solution)/shard_map/ppermute | solution.py:64
  90.2 3.0 %collective-permute-start.17 = (bf16[192,4096]{1,0:T(8,128)(2,1)S(1)}, bf16[192,4096]{1,0:T(8,128)(2,1)S(1)}, u32[]{:S(2)}, u32[]{:S(2)}) collective-permute-start(bf16[192,4096]{1,0:T(8,128)(2,1)S(1)} %collective-permute-done.15.refs_1_), channel_id=1, source_target_pairs={{0,12},{1,13},{2,14},{3,15},{4,0},{5,1},{6,2},{7,3},{8,4},{9,5},{1... | collective-permute-start | bytes 4718600 | tf_op jit(solution)/shard_map/ppermute | solution.py:64
  93.1 13.9 %collective-permute-done.8.refs_2_ = bf16[192,4096]{1,0:T(8,128)(2,1)S(1)} collective-permute-done((bf16[192,4096]{1,0:T(8,128)(2,1)S(1)}, bf16[192,4096]{1,0:T(8,128)(2,1)S(1)}, u32[]{:S(2)}, u32[]{:S(2)}) %collective-permute-start.8) | collective-permute-done | bytes 1572896 | tf_op jit(solution)/shard_map/ppermute | solution.py:64
  107.0 3.0 %collective-permute-start.11 = (bf16[192,4096]{1,0:T(8,128)(2,1)S(1)}, bf16[192,4096]{1,0:T(8,128)(2,1)S(1)}, u32[]{:S(2)}, u32[]{:S(2)}) collective-permute-start(bf16[192,4096]{1,0:T(8,128)(2,1)S(1)} %collective-permute-done.9.refs_3_), channel_id=1, source_target_pairs={{0,12},{1,13},{2,14},{3,15},{4,0},{5,1},{6,2},{7,3},{8,4},{9,5},{1... | collective-permute-start | bytes 4718600 | tf_op jit(solution)/shard_map/ppermute | solution.py:64
  110.0 10.1 %grads.6.refs_3_ = f32[512,4096]{1,0:T(8,128)S(1)} custom-call(bf16[192,4096]{1,0:T(8,128)(2,1)S(1)} %collective-permute-done.14.refs_0_, bf16[192,4096]{1,0:T(8,128)(2,1)S(1)} %collective-permute-done.15.refs_1_, bf16[192,4096]{1,0:T(8,128)(2,1)S(1)} %collective-permute-done.8.refs_2_, ...), custom_call_target="tpu_custom_call", output_to_operand_aliasing={{}: (5, {})} | custom-call | flops 6442450944 | bytes 6291456 | tf_op jit(solution)/shard_map/grads/pallas_call | solution.py:166
  120.1 3.3 %collective-permute-done.17.refs_1_ = bf16[192,4096]{1,0:T(8,128)(2,1)S(1)} collective-permute-done((bf16[192,4096]{1,0:T(8,128)(2,1)S(1)}, bf16[192,4096]{1,0:T(8,128)(2,1)S(1)}, u32[]{:S(2)}, u32[]{:S(2)}) %collective-permute-start.17) | collective-permute-done | bytes 1572896 | tf_op jit(solution)/shard_map/ppermute | solution.py:64
  123.9 6.5 %grads.7.refs_4_ = f32[512,4096]{1,0:T(8,128)S(1)} custom-call(bf16[192,4096]{1,0:T(8,128)(2,1)S(1)} %collective-permute-done.16.refs_0_, bf16[192,4096]{1,0:T(8,128)(2,1)S(1)} %collective-permute-done.17.refs_1_, bf16[512,4096]{1,0:T(8,128)(2,1)S(1)} %bitcast.152, f32[512,4096]{1,0:T(8,128)S(1)} %grads.6.refs_3_), custom_call_target="tpu_custom_call", output_to_operand_aliasing={{}: (3, {})} | custom-call | flops 3221225472 | bytes 3145728 | tf_op jit(solution)/shard_map/grads/pallas_call | solution.py:166
  130.4 9.8 %collective-permute-done.11.refs_2_ = bf16[192,4096]{1,0:T(8,128)(2,1)S(1)} collective-permute-done((bf16[192,4096]{1,0:T(8,128)(2,1)S(1)}, bf16[192,4096]{1,0:T(8,128)(2,1)S(1)}, u32[]{:S(2)}, u32[]{:S(2)}) %collective-permute-start.11) | collective-permute-done | bytes 1572896 | tf_op jit(solution)/shard_map/ppermute | solution.py:64
  141.9 14.2 %pseudo.1 = (bf16[3,64,4096]{2,1,0:T(8,128)(2,1)S(1)}, bf16[3,64,4096]{2,1,0:T(8,128)(2,1)S(1)}, bf16[2,64,2048]{2,1,0:T(8,128)(2,1)S(1)}, bf16[2,64,2048]{2,1,0:T(8,128)(2,1)S(1)}) custom-call(s32[2]{0:T(128)} %pad_add_fusion.refs_0_, bf16[192,4096]{1,0:T(8,128)(2,1)} %copy-done.9, bf16[192,4096]{1,0:T(8,128)(2,1)} %copy-done.8, ...), custom_call_target="tpu_custom_call" | custom-call | flops 3221225472 | bytes 28311552 | tf_op jit(solution)/shard_map/pseudo/pallas_call | solution.py:242
  164.1 3.5 %collective-permute-done.20 = bf16[64,2048]{1,0:T(8,128)(2,1)S(1)} collective-permute-done((bf16[64,2048]{1,0:T(8,128)(2,1)S(1)}, bf16[64,2048]{1,0:T(8,128)(2,1)S(1)}, u32[]{:S(2)}, u32[]{:S(2)}) %collective-permute-start.20) | collective-permute-done | bytes 262176 | tf_op jit(solution)/shard_map/ppermute | solution.py:53
  167.6 4.6 %collective-permute-done.22 = bf16[64,2048]{1,0:T(8,128)(2,1)S(1)} collective-permute-done((bf16[64,2048]{1,0:T(8,128)(2,1)S(1)}, bf16[64,2048]{1,0:T(8,128)(2,1)S(1)}, u32[]{:S(2)}, u32[]{:S(2)}) %collective-permute-start.22) | collective-permute-done | bytes 262176 | tf_op jit(solution)/shard_map/ppermute | solution.py:53
  175.7 21.1 %collective-permute-done.21 = bf16[2,64,4096]{2,1,0:T(8,128)(2,1)S(1)} collective-permute-done((bf16[2,64,4096]{2,1,0:T(8,128)(2,1)S(1)}, bf16[2,64,4096]{2,1,0:T(8,128)(2,1)S(1)}, u32[]{:S(2)}, u32[]{:S(2)}) %collective-permute-start.21) | collective-permute-done | bytes 1048608 | tf_op jit(solution)/shard_map/ppermute | solution.py:53
  203.3 22.0 %collective-permute-done.25.prv = bf16[2,64,4096]{2,1,0:T(8,128)(2,1)S(1)} collective-permute-done((bf16[2,64,4096]{2,1,0:T(8,128)(2,1)S(1)}, bf16[2,64,4096]{2,1,0:T(8,128)(2,1)S(1)}, u32[]{:S(2)}, u32[]{:S(2)}) %collective-permute-start.25) | collective-permute-done | bytes 1048608 | tf_op jit(solution)/shard_map/ppermute | solution.py:53
  235.8 3.0 %near_own_kernel.1.begun = bf16[8,64,4096]{2,1,0:T(8,128)(2,1)} custom-call(s32[6]{0:T(128)} %pad_add_fusion.1.info, bf16[2,64,4096]{2,1,0:T(8,128)(2,1)} %copy-done.3, bf16[2,64,4096]{2,1,0:T(8,128)(2,1)} %copy-done.7, bf16[2,64,4096]{2,1,0:T(8,128)(2,1)} %copy-done.6), custom_call_target="tpu_custom_call" | custom-call | bytes 4194304 | tf_op jit(solution)/shard_map/near_own_kernel/pallas_call | solution.py:297
  243.6 3.2 %rest_kernel.1 = bf16[8,64,4096]{2,1,0:T(8,128)(2,1)} custom-call(s32[6]{0:T(128)} %pad_add_fusion.1.info, bf16[64,4096]{1,0:T(8,128)(2,1)} %copy-done.11, bf16[2,64,4096]{2,1,0:T(8,128)(2,1)} %copy-done.10, bf16[64,2048]{1,0:T(8,128)(2,1)} %copy-done.12, bf16[64,2048]{1,0:T(8,128)(2,1)} %copy-done.13, ...), custom_call_target="tpu_custom_call", output_to_operand_aliasing={{}: (7, {})} | custom-call | bytes 4194304 | tf_op jit(solution)/shard_map/rest_kernel/pallas_call | solution.py:297
  (130 shorter events, 57.5 us)
Async XLA Ops:
  0.6 25.6 %collective-permute-start.3 = (bf16[192,2048]{1,0:T(8,128)(2,1)}, bf16[192,2048]{1,0:T(8,128)(2,1)S(1)}, u32[]{:S(2)}, u32[]{:S(2)}) collective-permute-start(bf16[192,2048]{1,0:T(8,128)(2,1)} %bitcast.157), channel_id=1, source_target_pairs={{0,3},{1,0},{2,1},{3,2},{4,7},{5,4},{6,5},{7,6},{8,11},{9,8},{10,9... | collective-permute-start | bytes 2359304 | tf_op jit(solution)/shard_map/ppermute | solution.py:64
  5.3 24.8 %collective-permute-start.1 = (bf16[192,2048]{1,0:T(8,128)(2,1)}, bf16[192,2048]{1,0:T(8,128)(2,1)S(1)}, u32[]{:S(2)}, u32[]{:S(2)}) collective-permute-start(bf16[192,2048]{1,0:T(8,128)(2,1)} %bitcast.158), channel_id=1, source_target_pairs={{0,1},{1,2},{2,3},{3,0},{4,5},{5,6},{6,7},{7,4},{8,9},{9,10},{10,1... | collective-permute-start | bytes 2359304 | tf_op jit(solution)/shard_map/ppermute | solution.py:64
  5.3 21.0 %collective-permute-start = (bf16[192,2048]{1,0:T(8,128)(2,1)}, bf16[192,2048]{1,0:T(8,128)(2,1)S(1)}, u32[]{:S(2)}, u32[]{:S(2)}) collective-permute-start(bf16[192,2048]{1,0:T(8,128)(2,1)} %bitcast.160), channel_id=1, source_target_pairs={{0,1},{1,2},{2,3},{3,0},{4,5},{5,6},{6,7},{7,4},{8,9},{9,10},{10,1... | collective-permute-start | bytes 2359304 | tf_op jit(solution)/shard_map/ppermute | solution.py:64
  5.3 41.3 %collective-permute-start.7 = (bf16[192,2048]{1,0:T(8,128)(2,1)}, bf16[192,2048]{1,0:T(8,128)(2,1)S(1)}, u32[]{:S(2)}, u32[]{:S(2)}) collective-permute-start(bf16[192,2048]{1,0:T(8,128)(2,1)} %bitcast.161), channel_id=1, source_target_pairs={{0,3},{1,0},{2,1},{3,2},{4,7},{5,4},{6,5},{7,6},{8,11},{9,8},{10,9... | collective-permute-start | bytes 2359304 | tf_op jit(solution)/shard_map/ppermute | solution.py:64
  26.3 15.7 %collective-permute-start.2 = (bf16[192,2048]{1,0:T(8,128)(2,1)S(1)}, bf16[192,2048]{1,0:T(8,128)(2,1)S(1)}, u32[]{:S(2)}, u32[]{:S(2)}) collective-permute-start(bf16[192,2048]{1,0:T(8,128)(2,1)S(1)} %collective-permute-done), channel_id=1, source_target_pairs={{0,1},{1,2},{2,3},{3,0},{4,5},{5,6},{6,7},{7,4},{8,9},{9,10},{10,1... | collective-permute-start | bytes 2359304 | tf_op jit(solution)/shard_map/ppermute | solution.py:64
  26.3 15.7 %collective-permute-start.4 = (bf16[192,2048]{1,0:T(8,128)(2,1)S(1)}, bf16[192,2048]{1,0:T(8,128)(2,1)S(1)}, u32[]{:S(2)}, u32[]{:S(2)}) collective-permute-start(bf16[192,2048]{1,0:T(8,128)(2,1)S(1)} %collective-permute-done.3), channel_id=1, source_target_pairs={{0,3},{1,0},{2,1},{3,2},{4,7},{5,4},{6,5},{7,6},{8,11},{9,8},{10,9... | collective-permute-start | bytes 2359304 | tf_op jit(solution)/shard_map/ppermute | solution.py:64
  29.0 27.5 %collective-permute-start.12 = (bf16[192,4096]{1,0:T(8,128)(2,1)S(1)}, bf16[192,4096]{1,0:T(8,128)(2,1)S(1)}, u32[]{:S(2)}, u32[]{:S(2)}) collective-permute-start(bf16[192,4096]{1,0:T(8,128)(2,1)S(1)} %pad_maximum_fusion.refs_0_), channel_id=1, source_target_pairs={{0,4},{1,5},{2,6},{3,7},{4,8},{5,9},{6,10},{7,11},{8,12},{9,13},{1... | collective-permute-start | bytes 4718600 | tf_op jit(solution)/shard_map/ppermute | solution.py:64
  30.1 26.3 %collective-permute-start.13 = (bf16[192,4096]{1,0:T(8,128)(2,1)S(1)}, bf16[192,4096]{1,0:T(8,128)(2,1)S(1)}, u32[]{:S(2)}, u32[]{:S(2)}) collective-permute-start(bf16[192,4096]{1,0:T(8,128)(2,1)S(1)} %pad_maximum_fusion.refs_0_), channel_id=1, source_target_pairs={{0,12},{1,13},{2,14},{3,15},{4,0},{5,1},{6,2},{7,3},{8,4},{9,5},{1... | collective-permute-start | bytes 4718600 | tf_op jit(solution)/shard_map/ppermute | solution.py:64
  41.9 31.4 %collective-permute-start.5 = (bf16[192,4096]{1,0:T(8,128)(2,1)S(1)}, bf16[192,4096]{1,0:T(8,128)(2,1)S(1)}, u32[]{:S(2)}, u32[]{:S(2)}) collective-permute-start(bf16[192,4096]{1,0:T(8,128)(2,1)S(1)} %constant_dynamic-update-slice_fusion.refs_1_), channel_id=1, source_target_pairs={{0,4},{1,5},{2,6},{3,7},{4,8},{5,9},{6,10},{7,11},{8,12},{9,13},{1... | collective-permute-start | bytes 4718600 | tf_op jit(solution)/shard_map/ppermute | solution.py:64
  45.7 27.6 %collective-permute-start.6 = (bf16[192,4096]{1,0:T(8,128)(2,1)S(1)}, bf16[192,4096]{1,0:T(8,128)(2,1)S(1)}, u32[]{:S(2)}, u32[]{:S(2)}) collective-permute-start(bf16[192,4096]{1,0:T(8,128)(2,1)S(1)} %constant_dynamic-update-slice_fusion.refs_1_), channel_id=1, source_target_pairs={{0,12},{1,13},{2,14},{3,15},{4,0},{5,1},{6,2},{7,3},{8,4},{9,5},{1... | collective-permute-start | bytes 4718600 | tf_op jit(solution)/shard_map/ppermute | solution.py:64
  56.5 33.7 %collective-permute-start.14 = (bf16[192,4096]{1,0:T(8,128)(2,1)S(1)}, bf16[192,4096]{1,0:T(8,128)(2,1)S(1)}, u32[]{:S(2)}, u32[]{:S(2)}) collective-permute-start(bf16[192,4096]{1,0:T(8,128)(2,1)S(1)} %constant_dynamic-update-slice_fusion.4.refs_2_), channel_id=1, source_target_pairs={{0,4},{1,5},{2,6},{3,7},{4,8},{5,9},{6,10},{7,11},{8,12},{9,13},{1... | collective-permute-start | bytes 4718600 | tf_op jit(solution)/shard_map/ppermute | solution.py:64
  56.5 33.7 %collective-permute-start.15 = (bf16[192,4096]{1,0:T(8,128)(2,1)S(1)}, bf16[192,4096]{1,0:T(8,128)(2,1)S(1)}, u32[]{:S(2)}, u32[]{:S(2)}) collective-permute-start(bf16[192,4096]{1,0:T(8,128)(2,1)S(1)} %constant_dynamic-update-slice_fusion.4.refs_2_), channel_id=1, source_target_pairs={{0,12},{1,13},{2,14},{3,15},{4,0},{5,1},{6,2},{7,3},{8,4},{9,5},{1... | collective-permute-start | bytes 4718600 | tf_op jit(solution)/shard_map/ppermute | solution.py:64
  73.3 33.7 %collective-permute-start.8 = (bf16[192,4096]{1,0:T(8,128)(2,1)S(1)}, bf16[192,4096]{1,0:T(8,128)(2,1)S(1)}, u32[]{:S(2)}, u32[]{:S(2)}) collective-permute-start(bf16[192,4096]{1,0:T(8,128)(2,1)S(1)} %constant_dynamic-update-slice_fusion.2.refs_3_), channel_id=1, source_target_pairs={{0,4},{1,5},{2,6},{3,7},{4,8},{5,9},{6,10},{7,11},{8,12},{9,13},{1... | collective-permute-start | bytes 4718600 | tf_op jit(solution)/shard_map/ppermute | solution.py:64
  73.3 33.7 %collective-permute-start.9 = (bf16[192,4096]{1,0:T(8,128)(2,1)S(1)}, bf16[192,4096]{1,0:T(8,128)(2,1)S(1)}, u32[]{:S(2)}, u32[]{:S(2)}) collective-permute-start(bf16[192,4096]{1,0:T(8,128)(2,1)S(1)} %constant_dynamic-update-slice_fusion.2.refs_3_), channel_id=1, source_target_pairs={{0,12},{1,13},{2,14},{3,15},{4,0},{5,1},{6,2},{7,3},{8,4},{9,5},{1... | collective-permute-start | bytes 4718600 | tf_op jit(solution)/shard_map/ppermute | solution.py:64
  90.2 33.3 %collective-permute-start.17 = (bf16[192,4096]{1,0:T(8,128)(2,1)S(1)}, bf16[192,4096]{1,0:T(8,128)(2,1)S(1)}, u32[]{:S(2)}, u32[]{:S(2)}) collective-permute-start(bf16[192,4096]{1,0:T(8,128)(2,1)S(1)} %collective-permute-done.15.refs_1_), channel_id=1, source_target_pairs={{0,12},{1,13},{2,14},{3,15},{4,0},{5,1},{6,2},{7,3},{8,4},{9,5},{1... | collective-permute-start | bytes 4718600 | tf_op jit(solution)/shard_map/ppermute | solution.py:64
  93.1 30.7 %collective-permute-start.16 = (bf16[192,4096]{1,0:T(8,128)(2,1)S(1)}, bf16[192,4096]{1,0:T(8,128)(2,1)S(1)}, u32[]{:S(2)}, u32[]{:S(2)}) collective-permute-start(bf16[192,4096]{1,0:T(8,128)(2,1)S(1)} %collective-permute-done.12.refs_0_), channel_id=1, source_target_pairs={{0,4},{1,5},{2,6},{3,7},{4,8},{5,9},{6,10},{7,11},{8,12},{9,13},{1... | collective-permute-start | bytes 4718600 | tf_op jit(solution)/shard_map/ppermute | solution.py:64
  107.0 33.3 %collective-permute-start.11 = (bf16[192,4096]{1,0:T(8,128)(2,1)S(1)}, bf16[192,4096]{1,0:T(8,128)(2,1)S(1)}, u32[]{:S(2)}, u32[]{:S(2)}) collective-permute-start(bf16[192,4096]{1,0:T(8,128)(2,1)S(1)} %collective-permute-done.9.refs_3_), channel_id=1, source_target_pairs={{0,12},{1,13},{2,14},{3,15},{4,0},{5,1},{6,2},{7,3},{8,4},{9,5},{1... | collective-permute-start | bytes 4718600 | tf_op jit(solution)/shard_map/ppermute | solution.py:64
  110.0 30.4 %collective-permute-start.10 = (bf16[192,4096]{1,0:T(8,128)(2,1)S(1)}, bf16[192,4096]{1,0:T(8,128)(2,1)S(1)}, u32[]{:S(2)}, u32[]{:S(2)}) collective-permute-start(bf16[192,4096]{1,0:T(8,128)(2,1)S(1)} %collective-permute-done.5.refs_2_), channel_id=1, source_target_pairs={{0,4},{1,5},{2,6},{3,7},{4,8},{5,9},{6,10},{7,11},{8,12},{9,13},{1... | collective-permute-start | bytes 4718600 | tf_op jit(solution)/shard_map/ppermute | solution.py:64
  156.2 16.1 %collective-permute-start.18 = (bf16[3,64,4096]{2,1,0:T(8,128)(2,1)S(1)}, bf16[3,64,4096]{2,1,0:T(8,128)(2,1)S(1)}, u32[]{:S(2)}, u32[]{:S(2)}) collective-permute-start(bf16[3,64,4096]{2,1,0:T(8,128)(2,1)S(1)} %get-tuple-element.40), channel_id=1, source_target_pairs={{0,16},{16,0},{32,48},{48,32},{64,80},{80,64},{96,112},{112,96},{1... | collective-permute-start | bytes 4718600 | tf_op jit(solution)/shard_map/ppermute | solution.py:53
  173.1 23.8 %collective-permute-start.21 = (bf16[2,64,4096]{2,1,0:T(8,128)(2,1)S(1)}, bf16[2,64,4096]{2,1,0:T(8,128)(2,1)S(1)}, u32[]{:S(2)}, u32[]{:S(2)}) collective-permute-start(bf16[2,64,4096]{2,1,0:T(8,128)(2,1)S(1)} %pad_maximum_fusion.1), channel_id=1, source_target_pairs={{0,32},{16,112},{32,64},{48,16},{64,96},{80,48},{96,0},{112,80},{1... | collective-permute-start | bytes 3145736 | tf_op jit(solution)/shard_map/ppermute | solution.py:53
  175.2 24.0 %collective-permute-start.24 = (bf16[2,64,4096]{2,1,0:T(8,128)(2,1)S(1)}, bf16[2,64,4096]{2,1,0:T(8,128)(2,1)S(1)}, u32[]{:S(2)}, u32[]{:S(2)}) collective-permute-start(bf16[2,64,4096]{2,1,0:T(8,128)(2,1)S(1)} %pad_maximum_fusion.2), channel_id=1, source_target_pairs={{0,96},{16,48},{32,0},{48,80},{64,32},{80,112},{96,64},{112,16},{1... | collective-permute-start | bytes 3145736 | tf_op jit(solution)/shard_map/ppermute | solution.py:53
  200.3 24.9 %collective-permute-start.25 = (bf16[2,64,4096]{2,1,0:T(8,128)(2,1)S(1)}, bf16[2,64,4096]{2,1,0:T(8,128)(2,1)S(1)}, u32[]{:S(2)}, u32[]{:S(2)}) collective-permute-start(bf16[2,64,4096]{2,1,0:T(8,128)(2,1)S(1)} %get-tuple-element.53.own), channel_id=1, source_target_pairs={{0,32},{16,112},{32,64},{48,16},{64,96},{80,48},{96,0},{112,80},{1... | collective-permute-start | bytes 3145736 | tf_op jit(solution)/shard_map/ppermute | solution.py:53
  202.2 24.2 %collective-permute-start.26 = (bf16[2,64,4096]{2,1,0:T(8,128)(2,1)S(1)}, bf16[2,64,4096]{2,1,0:T(8,128)(2,1)S(1)}, u32[]{:S(2)}, u32[]{:S(2)}) collective-permute-start(bf16[2,64,4096]{2,1,0:T(8,128)(2,1)S(1)} %get-tuple-element.53.own), channel_id=1, source_target_pairs={{0,96},{16,48},{32,0},{48,80},{64,32},{80,112},{96,64},{112,16},{1... | collective-permute-start | bytes 3145736 | tf_op jit(solution)/shard_map/ppermute | solution.py:53
  202.3 30.9 %collective-permute-start.27 = (bf16[64,4096]{1,0:T(8,128)(2,1)S(1)}, bf16[64,4096]{1,0:T(8,128)(2,1)S(1)}, u32[]{:S(2)}, u32[]{:S(2)}) collective-permute-start(bf16[64,4096]{1,0:T(8,128)(2,1)S(1)} %fusion.7), channel_id=1, source_target_pairs={{0,16},{16,0},{32,48},{48,32},{64,80},{80,64},{96,112},{112,96},{1... | collective-permute-start | bytes 1572872 | tf_op jit(solution)/shard_map/ppermute | solution.py:53
  (25 other events, 235.4 us)

commit v4 on v3

--- a/solution.py
+++ b/solution.py
@@ -199,66 +199,71 @@
     return (first_new / (root + ADAM_EPS) + (INNER_RATE * DECAY) * start.astype(F32)).astype(BF16)
 
 
-def pseudo_kernel(n, features, hidden_scale, *refs):
-    where, pieces = refs[0], refs[1 : 1 + n]
-    w, acc, m, v, keep, swap, far_keep, far_swap, total, act_t, dpre_t, xg, sem = refs[1 + n :]
-    fetch(pieces, xg, sem)
-    hidden_both(xg, w, act_t, dpre_t, features, hidden_scale)
+TAIL = (((2, 0), (2, 1)), ((0, 1), (1, 1), (3, 1)), ((0, 0), (1, 0), (3, 0)))
+
+
+def pseudo_kernel(n, part, features, hidden_scale, *refs):
+    where = refs[0]
+    if part == 0:
+        pieces = refs[1 : 1 + n]
+        w, acc, m, v, out, xg, act_t, dpre_t, total, lines, sem = refs[1 + n :]
+        fetch(pieces, xg, sem)
+        hidden_both(xg, w, act_t, dpre_t, features, hidden_scale)
+    else:
+        w, acc, m, v, xg, act_t, dpre_t, out, total, lines = refs[1:]
     y, core = where[0], where[1]
     rows = w.shape[0] // SETS
+    starts = []
+    for d, other in TAIL[part]:
+        parity = 1 - core if other else core
+        chip = lax.rem(y + jnp.where(parity == 0, d, YS - d), YS)
+        starts.append(pl.multiple_of((2 * chip + parity) * rows, rows))
     for half, left, scale in ((0, dpre_t, features ** (-0.5)), (1, act_t, hidden_scale)):
-
-        def columns(j, carry, half=half, left=left, scale=scale):
-            here = pl.ds(pl.multiple_of(j * COLS, COLS), COLS)
+        for k, at in enumerate(starts):
+            lines[k * rows : (k + 1) * rows, :] = left[pl.ds(at, rows), :]
+
+        def columns(j, carry, half=half, scale=scale):
             cols = pl.ds(pl.multiple_of(half * features + j * COLS, COLS), COLS)
-            total[...] = acc[:, cols] + jnp.dot(left[...], xg[:, cols], preferred_element_type=F32)
-
-            def stepped(d, parity):
-                chip = lax.rem(y + jnp.where(parity == 0, d, YS - d), YS)
-                at = pl.ds(pl.multiple_of((2 * chip + parity) * rows, rows), rows)
-                return adam(total[at, :], scale, m[at, cols], v[at, cols], w[at, cols])
-
-            def ring(i, carry):
-                for out, parity in ((keep, core), (swap, 1 - core)):
-                    out[i, :, cols] = stepped(i + i // 2, parity)
-                return carry
-
-            lax.fori_loop(0, YS - 1, ring, carry)
-            for out, parity in ((far_keep, core), (far_swap, 1 - core)):
-                out[half, :, here] = stepped(2, parity)
+            total[...] = jnp.dot(lines[...], xg[:, cols], preferred_element_type=F32)
+            for k, start in enumerate(starts):
+                at = pl.ds(start, rows)
+                grads = acc[at, cols] + total[k * rows : (k + 1) * rows, :]
+                out[k, :, cols] = adam(grads, scale, m[at, cols], v[at, cols], w[at, cols])
             return carry
 
         lax.fori_loop(0, features // COLS, columns, 0)
 
 
-def last_pseudo(where, pieces, w, acc, m, v, hidden_scale):
-    n = len(pieces)
+def tail_pseudo(part, where, given, w, acc, m, v, hidden_scale):
     units, width = w.shape
     features = width // 2
     rows = units // SETS
-    tokens = sum(p.shape[0] for p in pieces)
-    near = pltpu.VMEM((YS - 1, rows, width), BF16)
-    far = pltpu.VMEM((2, rows, features), BF16)
+    count = len(TAIL[part])
+    tokens = sum(p.shape[0] for p in given) if part == 0 else given[0].shape[0]
+    hid = pltpu.VMEM((units, tokens), BF16)
+    kept = (w, acc, m, v)
+    out_shape = [pltpu.VMEM((count, rows, width), BF16)]
+    scratch = [pltpu.VMEM((count * rows, COLS), F32), pltpu.VMEM((count * rows, tokens), BF16)]
+    if part == 0:
+        operands, specs = (*given, *kept), [ANY] * len(given) + [VMEM] * 4
+        out_shape += [pltpu.VMEM((tokens, width), BF16), hid, hid]
+        scratch.append(pltpu.SemaphoreType.DMA((len(given),)))
+    else:
+        operands, specs = (*kept, *given), [VMEM] * 7
     return pl.pallas_call(
-        functools.partial(pseudo_kernel, n, features, hidden_scale),
-        in_specs=[pl.BlockSpec(memory_space=pltpu.SMEM)] + [HBM] * n + [VMEM] * 4,
-        out_specs=[VMEM] * 4,
-        scratch_shapes=[
-            pltpu.VMEM((units, COLS), F32),
-            pltpu.VMEM((units, tokens), BF16),
-            pltpu.VMEM((units, tokens), BF16),
-            pltpu.VMEM((tokens, width), BF16),
-            pltpu.SemaphoreType.DMA((n,)),
-        ],
-        out_shape=[near, near, far, far],
+        functools.partial(pseudo_kernel, len(given), part, features, hidden_scale),
+        in_specs=[pl.BlockSpec(memory_space=pltpu.SMEM)] + specs,
+        out_specs=[VMEM] * len(out_shape),
+        scratch_shapes=scratch,
+        out_shape=out_shape,
         compiler_params=pltpu.CompilerParams(vmem_limit_bytes=LIMIT),
         cost_estimate=pl.CostEstimate(
-            flops=8 * features * tokens * units,
-            bytes_accessed=units * width * 12 + tokens * width * 2,
-            transcendentals=units * tokens,
+            flops=4 * features * tokens * (rows * count + (units if part == 0 else 0)),
+            bytes_accessed=rows * count * width * 12,
+            transcendentals=rows * count * width,
         ),
-        name="pseudo",
-    )(where, *pieces, w, acc, m, v)
+        name="tail_%d" % part,
+    )(where, *operands)
 
 
 def home(info, d, parity):
@@ -387,13 +392,14 @@
     def weighed(k, a):
         return weights[k][:, None, None] * a.astype(F32)[None]
 
-    def exchange(swap, far_keep, far_swap):
-        lefts = on_path(far_keep[0], 1), on_path(far_swap[0], -1, 1)
-        rights = on_path(far_keep[1], -1), on_path(far_swap[1], 1, 1)
-        return (on_path(swap, 0, 1), *lefts, *rights)
-
-    keep, *outs = last_pseudo(where, rest, w, resident(acc), m, v, hidden_scale)
-    mate_keep, l_same, l_cross, r_same, r_cross = exchange(*outs)
+    acc = resident(acc)
+    far, *given = tail_pseudo(0, where, rest, w, acc, m, v, hidden_scale)
+    given = [resident(a) for a in given]
+    l_same, r_same = on_path(far[0, :, :features], 1), on_path(far[0, :, features:], -1)
+    l_cross, r_cross = on_path(far[1, :, :features], -1, 1), on_path(far[1, :, features:], 1, 1)
+    (swap,) = tail_pseudo(1, where, given, w, acc, m, v, hidden_scale)
+    mate_keep = on_path(after(swap, l_same, r_same, l_cross, r_cross), 0, 1)
+    (keep,) = tail_pseudo(2, after(where, swap), given, w, acc, m, v, hidden_scale)
 
     def merged(i, d, lo=0, hi=width):
         return weighed(d, keep[i, :, lo:hi]) + weighed(4 + d, mate_keep[i, :, lo:hi])
@@ -424,8 +430,8 @@
     near_own = on_path(picked(4, updated), 0, 1)
     near = on_path(jnp.stack([picked(5, nxt), picked(7, prv)]), 0, 1)
     returned = assemble(near_own_kernel, info, (updated, nxt, prv), (), 3, rows, width)
-    far = (own_l, own_r, other_l, other_r)
-    returned = assemble(rest_kernel, info, (near_own, near, *far), (returned,), 7, rows, width)
+    sent = [resident(a) for a in (near_own, near, own_l, own_r, other_l, other_r)]
+    returned = assemble(rest_kernel, info, sent, (returned,), 7, rows, width)
     return (new_experts[None], new_inertia[None], returned[None])
 
 

time: 249 us -> 248 us (level)
  waiting for transfers between devices: 115 us -> 105 us
  starting transfers between devices: 44 us -> 47.9 us
  Pallas kernels: 57 us -> 59.7 us
    ppermute x15, waiting for transfers between devices: 59.8 us -> 53.2 us  [on_path(): return lax.ppermute(a, 'path', path_hop(hop, flip))]
    ppermute x15, starting transfers between devices: 14.8 us -> 18.8 us  [on_path(): return lax.ppermute(a, 'path', path_hop(hop, flip))]
    ppermute x18, waiting for transfers between devices: 54.8 us -> 51.5 us  [send(): return lax.ppermute(a, ('path', 'fsdp'), plane_hop(*to))]
    pallas_call x1 -> x3, Pallas kernels: 14.2 us -> 16.6 us  [tail_pseudo(): pl.pallas_call(functools.partial(pseudo_kernel, len(given), part, feature...]
  transfers between devices with their start and end apart: 33 -> 33, of which waited for: 20 -> 15; matrix products, arithmetic and copies ran while one was open for 8% -> 9% of each run, Pallas kernels for 16% -> 20%
where the time goes in v4:
time: 248 us; the launch traced here: 246 us
  waiting for transfers between devices  105 us (42%)
  Pallas kernels  59.7 us (24%)
  starting transfers between devices  47.9 us (19%)
  local copies, waits for them, and re-layouts  14.7 us (6%)
  other arithmetic  12.2 us (5%)
  between operations  6.99 us (3%)
    ppermute x15, waiting for transfers between devices, on_path(): return lax.ppermute(a, 'path', path_hop(hop, flip))  53.2 us
    ppermute x18, waiting for transfers between devices, send(): return lax.ppermute(a, ('path', 'fsdp'), plane_hop(*to))  51.5 us
    pallas_call x4, Pallas kernels, accumulate(): pl.pallas_call(functools.partial(grads_kernel, n, first, features, hidden...  37.8 us
    ppermute x18, starting transfers between devices, send(): return lax.ppermute(a, ('path', 'fsdp'), plane_hop(*to))  29.1 us
    ppermute x15, starting transfers between devices, on_path(): return lax.ppermute(a, 'path', path_hop(hop, flip))  18.8 us
    pallas_call x3, Pallas kernels, tail_pseudo(): pl.pallas_call(functools.partial(pseudo_kernel, len(given), part, feature...  16.6 us
    pallas_call x2, Pallas kernels, assemble(): pl.pallas_call(kernel, in_specs=[pl.BlockSpec(memory_space=pltpu.SMEM)] +...  5.25 us
  transfers between devices with their start and end apart: 33, of which 15 were waited for; matrix products, arithmetic and copies ran while one was open for 9% of the time, Pallas kernels for 20%

profile of v4, /device:TPU:1, one launch (start us, length us, event | category | flops | bytes accessed | tf_op | source)
XLA Modules:
  0.0 246.2 jit_solution(4998864526703678917)
XLA Ops:
  0.6 4.7 %collective-permute-start.1 = (bf16[192,2048]{1,0:T(8,128)(2,1)}, bf16[192,2048]{1,0:T(8,128)(2,1)S(1)}, u32[]{:S(2)}, u32[]{:S(2)}) collective-permute-start(bf16[192,2048]{1,0:T(8,128)(2,1)} %bitcast.173), channel_id=1, source_target_pairs={{0,3},{1,0},{2,1},{3,2},{4,7},{5,4},{6,5},{7,6},{8,11},{9,8},{10,9... | collective-permute-start | bytes 2359304 | tf_op jit(solution)/shard_map/ppermute | solution.py:64
  33.0 9.8 %collective-permute-done.8 = bf16[192,2048]{1,0:T(8,128)(2,1)S(1)} collective-permute-done((bf16[192,2048]{1,0:T(8,128)(2,1)S(1)}, bf16[192,2048]{1,0:T(8,128)(2,1)S(1)}, u32[]{:S(2)}, u32[]{:S(2)}) %collective-permute-start.8) | collective-permute-done | bytes 786464 | tf_op jit(solution)/shard_map/ppermute | solution.py:64
  42.8 3.8 %collective-permute-start.10 = (bf16[192,4096]{1,0:T(8,128)(2,1)S(1)}, bf16[192,4096]{1,0:T(8,128)(2,1)S(1)}, u32[]{:S(2)}, u32[]{:S(2)}) collective-permute-start(bf16[192,4096]{1,0:T(8,128)(2,1)S(1)} %constant_dynamic-update-slice_fusion.2.refs_1_), channel_id=1, source_target_pairs={{0,4},{1,5},{2,6},{3,7},{4,8},{5,9},{6,10},{7,11},{8,12},{9,13},{1... | collective-permute-start | bytes 4718600 | tf_op jit(solution)/shard_map/ppermute | solution.py:64
  49.3 7.4 %collective-permute-done.2.refs_0_ = bf16[192,4096]{1,0:T(8,128)(2,1)S(1)} collective-permute-done((bf16[192,4096]{1,0:T(8,128)(2,1)S(1)}, bf16[192,4096]{1,0:T(8,128)(2,1)S(1)}, u32[]{:S(2)}, u32[]{:S(2)}) %collective-permute-start.2) | collective-permute-done | bytes 1572896 | tf_op jit(solution)/shard_map/ppermute | solution.py:64
  59.7 11.0 %grads.4.refs_5_ = f32[512,4096]{1,0:T(8,128)S(1)} custom-call(bf16[192,4096]{1,0:T(8,128)(2,1)S(1)} %pad_maximum_fusion.refs_0_, bf16[192,4096]{1,0:T(8,128)(2,1)S(1)} %constant_dynamic-update-slice_fusion.2.refs_1_, bf16[192,4096]{1,0:T(8,128)(2,1)S(1)} %constant_dynamic-update-slice_fusion.refs_2_, ...), custom_call_target="tpu_custom_call" | custom-call | flops 6442450944 | bytes 6291456 | tf_op jit(solution)/shard_map/grads/pallas_call | solution.py:166
  73.6 3.0 %collective-permute-start.15 = (bf16[192,4096]{1,0:T(8,128)(2,1)}, bf16[192,4096]{1,0:T(8,128)(2,1)S(1)}, u32[]{:S(2)}, u32[]{:S(2)}) collective-permute-start(bf16[192,4096]{1,0:T(8,128)(2,1)} %constant_dynamic-update-slice_fusion.4.refs_3_), channel_id=1, source_target_pairs={{0,12},{1,13},{2,14},{3,15},{4,0},{5,1},{6,2},{7,3},{8,4},{9,5},{1... | collective-permute-start | bytes 4718600 | tf_op jit(solution)/shard_map/ppermute | solution.py:64
  76.5 10.1 %grads.5.refs_5_ = f32[512,4096]{1,0:T(8,128)S(1)} custom-call(bf16[192,4096]{1,0:T(8,128)(2,1)S(1)} %collective-permute-done.2.refs_0_, bf16[192,4096]{1,0:T(8,128)(2,1)S(1)} %collective-permute-done.4.refs_1_, bf16[192,4096]{1,0:T(8,128)(2,1)S(1)} %collective-permute-done.10.refs_2_, ...), custom_call_target="tpu_custom_call", output_to_operand_aliasing={{}: (5, {})} | custom-call | flops 6442450944 | bytes 6291456 | tf_op jit(solution)/shard_map/grads/pallas_call | solution.py:166
  86.7 3.8 %collective-permute-done.5.refs_0_ = bf16[192,4096]{1,0:T(8,128)(2,1)S(1)} collective-permute-done((bf16[192,4096]{1,0:T(8,128)(2,1)S(1)}, bf16[192,4096]{1,0:T(8,128)(2,1)S(1)}, u32[]{:S(2)}, u32[]{:S(2)}) %collective-permute-start.5) | collective-permute-done | bytes 1572896 | tf_op jit(solution)/shard_map/ppermute | solution.py:64
  90.4 3.0 %collective-permute-start.13 = (bf16[192,4096]{1,0:T(8,128)(2,1)S(1)}, bf16[192,4096]{1,0:T(8,128)(2,1)S(1)}, u32[]{:S(2)}, u32[]{:S(2)}) collective-permute-start(bf16[192,4096]{1,0:T(8,128)(2,1)S(1)} %collective-permute-done.6.refs_1_), channel_id=1, source_target_pairs={{0,12},{1,13},{2,14},{3,15},{4,0},{5,1},{6,2},{7,3},{8,4},{9,5},{1... | collective-permute-start | bytes 4718600 | tf_op jit(solution)/shard_map/ppermute | solution.py:64
  93.4 13.9 %collective-permute-done.14.refs_2_ = bf16[192,4096]{1,0:T(8,128)(2,1)S(1)} collective-permute-done((bf16[192,4096]{1,0:T(8,128)(2,1)}, bf16[192,4096]{1,0:T(8,128)(2,1)S(1)}, u32[]{:S(2)}, u32[]{:S(2)}) %collective-permute-start.14) | collective-permute-done | bytes 1572896 | tf_op jit(solution)/shard_map/ppermute | solution.py:64
  107.3 3.0 %collective-permute-start.17 = (bf16[192,4096]{1,0:T(8,128)(2,1)S(1)}, bf16[192,4096]{1,0:T(8,128)(2,1)}, u32[]{:S(2)}, u32[]{:S(2)}) collective-permute-start(bf16[192,4096]{1,0:T(8,128)(2,1)S(1)} %collective-permute-done.15.refs_3_), channel_id=1, source_target_pairs={{0,12},{1,13},{2,14},{3,15},{4,0},{5,1},{6,2},{7,3},{8,4},{9,5},{1... | collective-permute-start | bytes 4718600 | tf_op jit(solution)/shard_map/ppermute | solution.py:64
  110.2 10.1 %grads.6.refs_3_ = f32[512,4096]{1,0:T(8,128)S(1)} custom-call(bf16[192,4096]{1,0:T(8,128)(2,1)S(1)} %collective-permute-done.5.refs_0_, bf16[192,4096]{1,0:T(8,128)(2,1)S(1)} %collective-permute-done.6.refs_1_, bf16[192,4096]{1,0:T(8,128)(2,1)S(1)} %collective-permute-done.14.refs_2_, ...), custom_call_target="tpu_custom_call", output_to_operand_aliasing={{}: (5, {})} | custom-call | flops 6442450944 | bytes 6291456 | tf_op jit(solution)/shard_map/grads/pallas_call | solution.py:166
  120.4 3.8 %collective-permute-done.12.refs_0_ = bf16[192,4096]{1,0:T(8,128)(2,1)S(1)} collective-permute-done((bf16[192,4096]{1,0:T(8,128)(2,1)S(1)}, bf16[192,4096]{1,0:T(8,128)(2,1)S(1)}, u32[]{:S(2)}, u32[]{:S(2)}) %collective-permute-start.12) | collective-permute-done | bytes 1572896 | tf_op jit(solution)/shard_map/ppermute | solution.py:64
  124.1 6.6 %grads.7.refs_4_.refs_2_ = f32[512,4096]{1,0:T(8,128)S(1)} custom-call(bf16[192,4096]{1,0:T(8,128)(2,1)S(1)} %collective-permute-done.12.refs_0_, bf16[192,4096]{1,0:T(8,128)(2,1)S(1)} %collective-permute-done.13.refs_1_, bf16[512,4096]{1,0:T(8,128)(2,1)S(1)} %bitcast.162, f32[512,4096]{1,0:T(8,128)S(1)} %grads.6.refs_3_), custom_call_target="tpu_custom_call", output_to_operand_aliasing={{}: (3, {})} | custom-call | flops 3221225472 | bytes 3145728 | tf_op jit(solution)/shard_map/grads/pallas_call | solution.py:166
  130.7 10.0 %collective-permute-done.16.refs_1_ = bf16[192,4096]{1,0:T(8,128)(2,1)S(1)} collective-permute-done((bf16[192,4096]{1,0:T(8,128)(2,1)S(1)}, bf16[192,4096]{1,0:T(8,128)(2,1)S(1)}, u32[]{:S(2)}, u32[]{:S(2)}) %collective-permute-start.16) | collective-permute-done | bytes 1572896 | tf_op jit(solution)/shard_map/ppermute | solution.py:64
  141.8 8.0 %tail_0.1 = (bf16[2,64,4096]{2,1,0:T(8,128)(2,1)S(1)}, bf16[384,4096]{1,0:T(8,128)(2,1)S(1)}, bf16[512,384]{1,0:T(8,128)(2,1)S(1)}, bf16[512,384]{1,0:T(8,128)(2,1)S(1)}) custom-call(s32[2]{0:T(128)} %pad_add_fusion.refs_0_, bf16[192,4096]{1,0:T(8,128)(2,1)} %copy-done.10, bf16[192,4096]{1,0:T(8,128)(2,1)} %collective-permute-done.17.refs_2_, ...), custom_call_target="tpu_custom_call" | custom-call | flops 2013265920 | bytes 6291456 | tf_op jit(solution)/shard_map/tail_0/pallas_call | solution.py:253
  154.9 4.3 %tail_1.1 = bf16[3,64,4096]{2,1,0:T(8,128)(2,1)S(1)} custom-call(s32[2]{0:T(128)} %pad_add_fusion.refs_0_, bf16[512,4096]{1,0:T(8,128)(2,1)S(1)} %bitcast.164, f32[512,4096]{1,0:T(8,128)S(1)} %grads.7.refs_4_.refs_2_, bf16[512,4096]{1,0:T(8,128)(2,1)S(1)} %bitcast.167, bf16[512,4096]{1,0:T(8,128)(2,1)S(1)} %bitcast.170, ...), custom_call_target="tpu_custom_call" | custom-call | flops 603979776 | bytes 9437184 | tf_op jit(solution)/shard_map/tail_1/pallas_call | solution.py:253
  166.0 4.3 %tail_2.1 = bf16[3,64,4096]{2,1,0:T(8,128)(2,1)S(1)} custom-call(s32[2]{0:T(128)} %pad_add_fusion.refs_0_, bf16[512,4096]{1,0:T(8,128)(2,1)S(1)} %bitcast.165, f32[512,4096]{1,0:T(8,128)S(1)} %grads.7.refs_4_.refs_2_, bf16[512,4096]{1,0:T(8,128)(2,1)S(1)} %bitcast.168, bf16[512,4096]{1,0:T(8,128)(2,1)S(1)} %bitcast.171, ...), custom_call_target="tpu_custom_call" | custom-call | flops 603979776 | bytes 9437184 | tf_op jit(solution)/shard_map/tail_2/pallas_call | solution.py:253
  175.3 18.9 %collective-permute-done.24 = bf16[2,64,4096]{2,1,0:T(8,128)(2,1)S(1)} collective-permute-done((bf16[2,64,4096]{2,1,0:T(8,128)(2,1)S(1)}, bf16[2,64,4096]{2,1,0:T(8,128)(2,1)S(1)}, u32[]{:S(2)}, u32[]{:S(2)}) %collective-permute-start.24) | collective-permute-done | bytes 1048608 | tf_op jit(solution)/shard_map/ppermute | solution.py:53
  194.2 3.0 %collective-permute-done.23 = bf16[2,64,4096]{2,1,0:T(8,128)(2,1)S(1)} collective-permute-done((bf16[2,64,4096]{2,1,0:T(8,128)(2,1)S(1)}, bf16[2,64,4096]{2,1,0:T(8,128)(2,1)S(1)}, u32[]{:S(2)}, u32[]{:S(2)}) %collective-permute-start.23) | collective-permute-done | bytes 1048608 | tf_op jit(solution)/shard_map/ppermute | solution.py:53
  198.4 3.1 %collective-permute-start.25 = (bf16[2,64,4096]{2,1,0:T(8,128)(2,1)S(1)}, bf16[2,64,4096]{2,1,0:T(8,128)(2,1)S(1)}, u32[]{:S(2)}, u32[]{:S(2)}) collective-permute-start(bf16[2,64,4096]{2,1,0:T(8,128)(2,1)S(1)} %get-tuple-element.57.own), channel_id=1, source_target_pairs={{0,32},{16,112},{32,64},{48,16},{64,96},{80,48},{96,0},{112,80},{1... | collective-permute-start | bytes 3145736 | tf_op jit(solution)/shard_map/ppermute | solution.py:53
  202.9 19.9 %collective-permute-done.25.prv = bf16[2,64,4096]{2,1,0:T(8,128)(2,1)S(1)} collective-permute-done((bf16[2,64,4096]{2,1,0:T(8,128)(2,1)S(1)}, bf16[2,64,4096]{2,1,0:T(8,128)(2,1)S(1)}, u32[]{:S(2)}, u32[]{:S(2)}) %collective-permute-start.25) | collective-permute-done | bytes 1048608 | tf_op jit(solution)/shard_map/ppermute | solution.py:53
  222.8 3.3 %collective-permute-done.26.nxt = bf16[2,64,4096]{2,1,0:T(8,128)(2,1)S(1)} collective-permute-done((bf16[2,64,4096]{2,1,0:T(8,128)(2,1)S(1)}, bf16[2,64,4096]{2,1,0:T(8,128)(2,1)S(1)}, u32[]{:S(2)}, u32[]{:S(2)}) %collective-permute-start.26) | collective-permute-done | bytes 1048608 | tf_op jit(solution)/shard_map/ppermute | solution.py:53
  235.0 3.0 %near_own_kernel.1.begun = bf16[8,64,4096]{2,1,0:T(8,128)(2,1)} custom-call(s32[6]{0:T(128)} %pad_add_fusion.1.info, bf16[2,64,4096]{2,1,0:T(8,128)(2,1)} %copy-done.5, bf16[2,64,4096]{2,1,0:T(8,128)(2,1)} %copy-done.9, bf16[2,64,4096]{2,1,0:T(8,128)(2,1)} %copy-done.8), custom_call_target="tpu_custom_call" | custom-call | bytes 4194304 | tf_op jit(solution)/shard_map/near_own_kernel/pallas_call | solution.py:302
  (121 shorter events, 67.5 us)
Async XLA Ops:
  0.6 26.2 %collective-permute-start.1 = (bf16[192,2048]{1,0:T(8,128)(2,1)}, bf16[192,2048]{1,0:T(8,128)(2,1)S(1)}, u32[]{:S(2)}, u32[]{:S(2)}) collective-permute-start(bf16[192,2048]{1,0:T(8,128)(2,1)} %bitcast.173), channel_id=1, source_target_pairs={{0,3},{1,0},{2,1},{3,2},{4,7},{5,4},{6,5},{7,6},{8,11},{9,8},{10,9... | collective-permute-start | bytes 2359304 | tf_op jit(solution)/shard_map/ppermute | solution.py:64
  5.3 25.4 %collective-permute-start.7 = (bf16[192,2048]{1,0:T(8,128)(2,1)}, bf16[192,2048]{1,0:T(8,128)(2,1)S(1)}, u32[]{:S(2)}, u32[]{:S(2)}) collective-permute-start(bf16[192,2048]{1,0:T(8,128)(2,1)} %bitcast.174), channel_id=1, source_target_pairs={{0,1},{1,2},{2,3},{3,0},{4,5},{5,6},{6,7},{7,4},{8,9},{9,10},{10,1... | collective-permute-start | bytes 2359304 | tf_op jit(solution)/shard_map/ppermute | solution.py:64
  5.3 21.5 %collective-permute-start = (bf16[192,2048]{1,0:T(8,128)(2,1)}, bf16[192,2048]{1,0:T(8,128)(2,1)S(1)}, u32[]{:S(2)}, u32[]{:S(2)}) collective-permute-start(bf16[192,2048]{1,0:T(8,128)(2,1)} %bitcast.176), channel_id=1, source_target_pairs={{0,1},{1,2},{2,3},{3,0},{4,5},{5,6},{6,7},{7,4},{8,9},{9,10},{10,1... | collective-permute-start | bytes 2359304 | tf_op jit(solution)/shard_map/ppermute | solution.py:64
  5.3 42.0 %collective-permute-start.3 = (bf16[192,2048]{1,0:T(8,128)(2,1)}, bf16[192,2048]{1,0:T(8,128)(2,1)S(1)}, u32[]{:S(2)}, u32[]{:S(2)}) collective-permute-start(bf16[192,2048]{1,0:T(8,128)(2,1)} %bitcast.177), channel_id=1, source_target_pairs={{0,3},{1,0},{2,1},{3,2},{4,7},{5,4},{6,5},{7,6},{8,11},{9,8},{10,9... | collective-permute-start | bytes 2359304 | tf_op jit(solution)/shard_map/ppermute | solution.py:64
  26.8 16.0 %collective-permute-start.8 = (bf16[192,2048]{1,0:T(8,128)(2,1)S(1)}, bf16[192,2048]{1,0:T(8,128)(2,1)S(1)}, u32[]{:S(2)}, u32[]{:S(2)}) collective-permute-start(bf16[192,2048]{1,0:T(8,128)(2,1)S(1)} %collective-permute-done), channel_id=1, source_target_pairs={{0,1},{1,2},{2,3},{3,0},{4,5},{5,6},{6,7},{7,4},{8,9},{9,10},{10,1... | collective-permute-start | bytes 2359304 | tf_op jit(solution)/shard_map/ppermute | solution.py:64
  26.9 15.9 %collective-permute-start.9 = (bf16[192,2048]{1,0:T(8,128)(2,1)S(1)}, bf16[192,2048]{1,0:T(8,128)(2,1)S(1)}, u32[]{:S(2)}, u32[]{:S(2)}) collective-permute-start(bf16[192,2048]{1,0:T(8,128)(2,1)S(1)} %collective-permute-done.1), channel_id=1, source_target_pairs={{0,3},{1,0},{2,1},{3,2},{4,7},{5,4},{6,5},{7,6},{8,11},{9,8},{10,9... | collective-permute-start | bytes 2359304 | tf_op jit(solution)/shard_map/ppermute | solution.py:64
  29.5 27.2 %collective-permute-start.2 = (bf16[192,4096]{1,0:T(8,128)(2,1)S(1)}, bf16[192,4096]{1,0:T(8,128)(2,1)S(1)}, u32[]{:S(2)}, u32[]{:S(2)}) collective-permute-start(bf16[192,4096]{1,0:T(8,128)(2,1)S(1)} %pad_maximum_fusion.refs_0_), channel_id=1, source_target_pairs={{0,4},{1,5},{2,6},{3,7},{4,8},{5,9},{6,10},{7,11},{8,12},{9,13},{1... | collective-permute-start | bytes 4718600 | tf_op jit(solution)/shard_map/ppermute | solution.py:64
  30.7 26.0 %collective-permute-start.4 = (bf16[192,4096]{1,0:T(8,128)(2,1)S(1)}, bf16[192,4096]{1,0:T(8,128)(2,1)S(1)}, u32[]{:S(2)}, u32[]{:S(2)}) collective-permute-start(bf16[192,4096]{1,0:T(8,128)(2,1)S(1)} %pad_maximum_fusion.refs_0_), channel_id=1, source_target_pairs={{0,12},{1,13},{2,14},{3,15},{4,0},{5,1},{6,2},{7,3},{8,4},{9,5},{1... | collective-permute-start | bytes 4718600 | tf_op jit(solution)/shard_map/ppermute | solution.py:64
  42.8 30.8 %collective-permute-start.10 = (bf16[192,4096]{1,0:T(8,128)(2,1)S(1)}, bf16[192,4096]{1,0:T(8,128)(2,1)S(1)}, u32[]{:S(2)}, u32[]{:S(2)}) collective-permute-start(bf16[192,4096]{1,0:T(8,128)(2,1)S(1)} %constant_dynamic-update-slice_fusion.2.refs_1_), channel_id=1, source_target_pairs={{0,4},{1,5},{2,6},{3,7},{4,8},{5,9},{6,10},{7,11},{8,12},{9,13},{1... | collective-permute-start | bytes 4718600 | tf_op jit(solution)/shard_map/ppermute | solution.py:64
  46.6 27.0 %collective-permute-start.11 = (bf16[192,4096]{1,0:T(8,128)(2,1)S(1)}, bf16[192,4096]{1,0:T(8,128)(2,1)S(1)}, u32[]{:S(2)}, u32[]{:S(2)}) collective-permute-start(bf16[192,4096]{1,0:T(8,128)(2,1)S(1)} %constant_dynamic-update-slice_fusion.2.refs_1_), channel_id=1, source_target_pairs={{0,12},{1,13},{2,14},{3,15},{4,0},{5,1},{6,2},{7,3},{8,4},{9,5},{1... | collective-permute-start | bytes 4718600 | tf_op jit(solution)/shard_map/ppermute | solution.py:64
  56.7 33.7 %collective-permute-start.5 = (bf16[192,4096]{1,0:T(8,128)(2,1)S(1)}, bf16[192,4096]{1,0:T(8,128)(2,1)S(1)}, u32[]{:S(2)}, u32[]{:S(2)}) collective-permute-start(bf16[192,4096]{1,0:T(8,128)(2,1)S(1)} %constant_dynamic-update-slice_fusion.refs_2_), channel_id=1, source_target_pairs={{0,4},{1,5},{2,6},{3,7},{4,8},{5,9},{6,10},{7,11},{8,12},{9,13},{1... | collective-permute-start | bytes 4718600 | tf_op jit(solution)/shard_map/ppermute | solution.py:64
  56.7 33.7 %collective-permute-start.6 = (bf16[192,4096]{1,0:T(8,128)(2,1)S(1)}, bf16[192,4096]{1,0:T(8,128)(2,1)S(1)}, u32[]{:S(2)}, u32[]{:S(2)}) collective-permute-start(bf16[192,4096]{1,0:T(8,128)(2,1)S(1)} %constant_dynamic-update-slice_fusion.refs_2_), channel_id=1, source_target_pairs={{0,12},{1,13},{2,14},{3,15},{4,0},{5,1},{6,2},{7,3},{8,4},{9,5},{1... | collective-permute-start | bytes 4718600 | tf_op jit(solution)/shard_map/ppermute | solution.py:64
  73.6 33.7 %collective-permute-start.14 = (bf16[192,4096]{1,0:T(8,128)(2,1)}, bf16[192,4096]{1,0:T(8,128)(2,1)S(1)}, u32[]{:S(2)}, u32[]{:S(2)}) collective-permute-start(bf16[192,4096]{1,0:T(8,128)(2,1)} %constant_dynamic-update-slice_fusion.4.refs_3_), channel_id=1, source_target_pairs={{0,4},{1,5},{2,6},{3,7},{4,8},{5,9},{6,10},{7,11},{8,12},{9,13},{1... | collective-permute-start | bytes 4718600 | tf_op jit(solution)/shard_map/ppermute | solution.py:64
  73.6 33.7 %collective-permute-start.15 = (bf16[192,4096]{1,0:T(8,128)(2,1)}, bf16[192,4096]{1,0:T(8,128)(2,1)S(1)}, u32[]{:S(2)}, u32[]{:S(2)}) collective-permute-start(bf16[192,4096]{1,0:T(8,128)(2,1)} %constant_dynamic-update-slice_fusion.4.refs_3_), channel_id=1, source_target_pairs={{0,12},{1,13},{2,14},{3,15},{4,0},{5,1},{6,2},{7,3},{8,4},{9,5},{1... | collective-permute-start | bytes 4718600 | tf_op jit(solution)/shard_map/ppermute | solution.py:64
  90.4 33.7 %collective-permute-start.12 = (bf16[192,4096]{1,0:T(8,128)(2,1)S(1)}, bf16[192,4096]{1,0:T(8,128)(2,1)S(1)}, u32[]{:S(2)}, u32[]{:S(2)}) collective-permute-start(bf16[192,4096]{1,0:T(8,128)(2,1)S(1)} %collective-permute-done.2.refs_0_), channel_id=1, source_target_pairs={{0,4},{1,5},{2,6},{3,7},{4,8},{5,9},{6,10},{7,11},{8,12},{9,13},{1... | collective-permute-start | bytes 4718600 | tf_op jit(solution)/shard_map/ppermute | solution.py:64
  90.4 33.7 %collective-permute-start.13 = (bf16[192,4096]{1,0:T(8,128)(2,1)S(1)}, bf16[192,4096]{1,0:T(8,128)(2,1)S(1)}, u32[]{:S(2)}, u32[]{:S(2)}) collective-permute-start(bf16[192,4096]{1,0:T(8,128)(2,1)S(1)} %collective-permute-done.6.refs_1_), channel_id=1, source_target_pairs={{0,12},{1,13},{2,14},{3,15},{4,0},{5,1},{6,2},{7,3},{8,4},{9,5},{1... | collective-permute-start | bytes 4718600 | tf_op jit(solution)/shard_map/ppermute | solution.py:64
  107.3 33.4 %collective-permute-start.16 = (bf16[192,4096]{1,0:T(8,128)(2,1)S(1)}, bf16[192,4096]{1,0:T(8,128)(2,1)S(1)}, u32[]{:S(2)}, u32[]{:S(2)}) collective-permute-start(bf16[192,4096]{1,0:T(8,128)(2,1)S(1)} %collective-permute-done.10.refs_2_), channel_id=1, source_target_pairs={{0,4},{1,5},{2,6},{3,7},{4,8},{5,9},{6,10},{7,11},{8,12},{9,13},{1... | collective-permute-start | bytes 4718600 | tf_op jit(solution)/shard_map/ppermute | solution.py:64
  107.3 33.4 %collective-permute-start.17 = (bf16[192,4096]{1,0:T(8,128)(2,1)S(1)}, bf16[192,4096]{1,0:T(8,128)(2,1)}, u32[]{:S(2)}, u32[]{:S(2)}) collective-permute-start(bf16[192,4096]{1,0:T(8,128)(2,1)S(1)} %collective-permute-done.15.refs_3_), channel_id=1, source_target_pairs={{0,12},{1,13},{2,14},{3,15},{4,0},{5,1},{6,2},{7,3},{8,4},{9,5},{1... | collective-permute-start | bytes 4718600 | tf_op jit(solution)/shard_map/ppermute | solution.py:64
  171.5 22.7 %collective-permute-start.24 = (bf16[2,64,4096]{2,1,0:T(8,128)(2,1)S(1)}, bf16[2,64,4096]{2,1,0:T(8,128)(2,1)S(1)}, u32[]{:S(2)}, u32[]{:S(2)}) collective-permute-start(bf16[2,64,4096]{2,1,0:T(8,128)(2,1)S(1)} %pad_maximum_fusion.2), channel_id=1, source_target_pairs={{0,96},{16,48},{32,0},{48,80},{64,32},{80,112},{96,64},{112,16},{1... | collective-permute-start | bytes 3145736 | tf_op jit(solution)/shard_map/ppermute | solution.py:53
  172.3 25.0 %collective-permute-start.23 = (bf16[2,64,4096]{2,1,0:T(8,128)(2,1)S(1)}, bf16[2,64,4096]{2,1,0:T(8,128)(2,1)S(1)}, u32[]{:S(2)}, u32[]{:S(2)}) collective-permute-start(bf16[2,64,4096]{2,1,0:T(8,128)(2,1)S(1)} %pad_maximum_fusion.1), channel_id=1, source_target_pairs={{0,32},{16,112},{32,64},{48,16},{64,96},{80,48},{96,0},{112,80},{1... | collective-permute-start | bytes 3145736 | tf_op jit(solution)/shard_map/ppermute | solution.py:53
  198.4 24.4 %collective-permute-start.25 = (bf16[2,64,4096]{2,1,0:T(8,128)(2,1)S(1)}, bf16[2,64,4096]{2,1,0:T(8,128)(2,1)S(1)}, u32[]{:S(2)}, u32[]{:S(2)}) collective-permute-start(bf16[2,64,4096]{2,1,0:T(8,128)(2,1)S(1)} %get-tuple-element.57.own), channel_id=1, source_target_pairs={{0,32},{16,112},{32,64},{48,16},{64,96},{80,48},{96,0},{112,80},{1... | collective-permute-start | bytes 3145736 | tf_op jit(solution)/shard_map/ppermute | solution.py:53
  201.4 24.7 %collective-permute-start.26 = (bf16[2,64,4096]{2,1,0:T(8,128)(2,1)S(1)}, bf16[2,64,4096]{2,1,0:T(8,128)(2,1)S(1)}, u32[]{:S(2)}, u32[]{:S(2)}) collective-permute-start(bf16[2,64,4096]{2,1,0:T(8,128)(2,1)S(1)} %get-tuple-element.57.own), channel_id=1, source_target_pairs={{0,96},{16,48},{32,0},{48,80},{64,32},{80,112},{96,64},{112,16},{1... | collective-permute-start | bytes 3145736 | tf_op jit(solution)/shard_map/ppermute | solution.py:53
  201.5 30.8 %collective-permute-start.27 = (bf16[64,4096]{1,0:T(8,128)(2,1)S(1)}, bf16[64,4096]{1,0:T(8,128)(2,1)S(1)}, u32[]{:S(2)}, u32[]{:S(2)}) collective-permute-start(bf16[64,4096]{1,0:T(8,128)(2,1)S(1)} %fusion.7), channel_id=1, source_target_pairs={{0,16},{16,0},{32,48},{48,32},{64,80},{80,64},{96,112},{112,96},{1... | collective-permute-start | bytes 1572872 | tf_op jit(solution)/shard_map/ppermute | solution.py:53
  227.5 14.1 %collective-permute-start.28 = (bf16[2,64,4096]{2,1,0:T(8,128)(2,1)}, bf16[2,64,4096]{2,1,0:T(8,128)(2,1)S(1)}, u32[]{:S(2)}, u32[]{:S(2)}) collective-permute-start(bf16[2,64,4096]{2,1,0:T(8,128)(2,1)} %pad_maximum_fusion.3), channel_id=1, source_target_pairs={{0,16},{16,0},{32,48},{48,32},{64,80},{80,64},{96,112},{112,96},{1... | collective-permute-start | bytes 3145736 | tf_op jit(solution)/shard_map/ppermute | solution.py:53
  (20 other events, 225.0 us)

commit v5 on v4

--- a/solution.py
+++ b/solution.py
@@ -28,7 +28,7 @@
 BF16 = jnp.bfloat16
 COLS = 512
 CHUNK = 256
-LIMIT = 30 << 20
+LIMIT = 24 << 20
 
 
 def plane_hop(da, db):
@@ -308,6 +308,7 @@
         out_shape=jax.ShapeDtypeStruct((SETS, rows, width), BF16),
         scratch_shapes=[pltpu.SemaphoreType.DMA((copies,))],
         input_output_aliases={1 + len(pieces): 0} if begun else {},
+        compiler_params=pltpu.CompilerParams(vmem_limit_bytes=8 << 20),
         cost_estimate=pl.CostEstimate(
             flops=0, bytes_accessed=SETS * rows * width * 2, transcendentals=0
         ),
@@ -398,7 +399,7 @@
     l_same, r_same = on_path(far[0, :, :features], 1), on_path(far[0, :, features:], -1)
     l_cross, r_cross = on_path(far[1, :, :features], -1, 1), on_path(far[1, :, features:], 1, 1)
     (swap,) = tail_pseudo(1, where, given, w, acc, m, v, hidden_scale)
-    mate_keep = on_path(after(swap, l_same, r_same, l_cross, r_cross), 0, 1)
+    mate_keep = on_path(after(swap, l_same, r_same), 0, 1)
     (keep,) = tail_pseudo(2, after(where, swap), given, w, acc, m, v, hidden_scale)
 
     def merged(i, d, lo=0, hi=width):
@@ -429,7 +430,7 @@
     other_r = on_path(picked(11, nxt, features), -1, 1)
     near_own = on_path(picked(4, updated), 0, 1)
     near = on_path(jnp.stack([picked(5, nxt), picked(7, prv)]), 0, 1)
-    returned = assemble(near_own_kernel, info, (updated, nxt, prv), (), 3, rows, width)
+    returned = assemble(near_own_kernel, info, [resident(a) for a in (updated, nxt, prv)], (), 3, rows, width)
     sent = [resident(a) for a in (near_own, near, own_l, own_r, other_l, other_r)]
     returned = assemble(rest_kernel, info, sent, (returned,), 7, rows, width)
     return (new_experts[None], new_inertia[None], returned[None])

time: 248 us -> 240 us (0.968)
  waiting for transfers between devices: 105 us -> 112 us
  local copies, waits for them, and re-layouts: 14.7 us -> 8.91 us
  Pallas kernels: 59.7 us -> 55.4 us
  other arithmetic: 12.2 us -> 9.35 us
    ppermute x18, waiting for transfers between devices: 51.5 us -> 55.9 us  [send(): return lax.ppermute(a, ('path', 'fsdp'), plane_hop(*to))]
    unnamed x25 -> x13, local copies, waits for them, and re-layouts: 4.47 us -> 0.18 us
    ppermute x15, waiting for transfers between devices: 53.2 us -> 56.5 us  [on_path(): return lax.ppermute(a, 'path', path_hop(hop, flip))]
  transfers between devices with their start and end apart: 33 -> 33, of which waited for: 15 -> 17; matrix products, arithmetic and copies ran while one was open for 9% -> 7% of each run, Pallas kernels for 20% -> 20%
where the time goes in v5:
time: 240 us
  waiting for transfers between devices  112 us (47%)
  Pallas kernels  55.4 us (23%)
  starting transfers between devices  46.6 us (19%)
  other arithmetic  9.35 us (4%)
  local copies, waits for them, and re-layouts  8.91 us (4%)
  between operations  6.78 us (3%)
    ppermute x15, waiting for transfers between devices, on_path(): return lax.ppermute(a, 'path', path_hop(hop, flip))  56.5 us
    ppermute x18, waiting for transfers between devices, send(): return lax.ppermute(a, ('path', 'fsdp'), plane_hop(*to))  55.9 us
    pallas_call x4, Pallas kernels, accumulate(): pl.pallas_call(functools.partial(grads_kernel, n, first, features, hidden...  36.8 us
    ppermute x18, starting transfers between devices, send(): return lax.ppermute(a, ('path', 'fsdp'), plane_hop(*to))  29.1 us
    ppermute x15, starting transfers between devices, on_path(): return lax.ppermute(a, 'path', path_hop(hop, flip))  17.5 us
    pallas_call x3, Pallas kernels, tail_pseudo(): pl.pallas_call(functools.partial(pseudo_kernel, len(given), part, feature...  14.8 us
  transfers between devices with their start and end apart: 33, of which 17 were waited for; matrix products, arithmetic and copies ran while one was open for 7% of the time, Pallas kernels for 20%

profile of v5, /device:TPU:1, one launch (start us, length us, event | category | flops | bytes accessed | tf_op | source)
XLA Modules:
  0.0 239.6 jit_solution(14823802395283463148)
XLA Ops:
  0.6 4.7 %collective-permute-start.1 = (bf16[192,2048]{1,0:T(8,128)(2,1)}, bf16[192,2048]{1,0:T(8,128)(2,1)S(1)}, u32[]{:S(2)}, u32[]{:S(2)}) collective-permute-start(bf16[192,2048]{1,0:T(8,128)(2,1)} %bitcast.173), channel_id=1, source_target_pairs={{0,3},{1,0},{2,1},{3,2},{4,7},{5,4},{6,5},{7,6},{8,11},{9,8},{10,9... | collective-permute-start | bytes 2359304 | tf_op jit(solution)/shard_map/ppermute | solution.py:64
  31.8 10.1 %collective-permute-done.8 = bf16[192,2048]{1,0:T(8,128)(2,1)S(1)} collective-permute-done((bf16[192,2048]{1,0:T(8,128)(2,1)S(1)}, bf16[192,2048]{1,0:T(8,128)(2,1)S(1)}, u32[]{:S(2)}, u32[]{:S(2)}) %collective-permute-start.8) | collective-permute-done | bytes 786464 | tf_op jit(solution)/shard_map/ppermute | solution.py:64
  41.9 3.3 %collective-permute-start.10 = (bf16[192,4096]{1,0:T(8,128)(2,1)S(1)}, bf16[192,4096]{1,0:T(8,128)(2,1)S(1)}, u32[]{:S(2)}, u32[]{:S(2)}) collective-permute-start(bf16[192,4096]{1,0:T(8,128)(2,1)S(1)} %constant_dynamic-update-slice_fusion.2.refs_1_), channel_id=1, source_target_pairs={{0,4},{1,5},{2,6},{3,7},{4,8},{5,9},{6,10},{7,11},{8,12},{9,13},{1... | collective-permute-start | bytes 4718600 | tf_op jit(solution)/shard_map/ppermute | solution.py:64
  46.8 9.7 %collective-permute-done.2.refs_0_ = bf16[192,4096]{1,0:T(8,128)(2,1)S(1)} collective-permute-done((bf16[192,4096]{1,0:T(8,128)(2,1)S(1)}, bf16[192,4096]{1,0:T(8,128)(2,1)S(1)}, u32[]{:S(2)}, u32[]{:S(2)}) %collective-permute-start.2) | collective-permute-done | bytes 1572896 | tf_op jit(solution)/shard_map/ppermute | solution.py:64
  56.5 3.0 %collective-permute-start.6 = (bf16[192,4096]{1,0:T(8,128)(2,1)S(1)}, bf16[192,4096]{1,0:T(8,128)(2,1)S(1)}, u32[]{:S(2)}, u32[]{:S(2)}) collective-permute-start(bf16[192,4096]{1,0:T(8,128)(2,1)S(1)} %constant_dynamic-update-slice_fusion.refs_2_), channel_id=1, source_target_pairs={{0,12},{1,13},{2,14},{3,15},{4,0},{5,1},{6,2},{7,3},{8,4},{9,5},{1... | collective-permute-start | bytes 4718600 | tf_op jit(solution)/shard_map/ppermute | solution.py:64
  59.4 9.8 %grads.4.refs_5_ = f32[512,4096]{1,0:T(8,128)S(1)} custom-call(bf16[192,4096]{1,0:T(8,128)(2,1)S(1)} %pad_maximum_fusion.refs_0_, bf16[192,4096]{1,0:T(8,128)(2,1)S(1)} %constant_dynamic-update-slice_fusion.2.refs_1_, bf16[192,4096]{1,0:T(8,128)(2,1)S(1)} %constant_dynamic-update-slice_fusion.refs_2_, ...), custom_call_target="tpu_custom_call" | custom-call | flops 6442450944 | bytes 6291456 | tf_op jit(solution)/shard_map/grads/pallas_call | solution.py:166
  69.2 4.1 %collective-permute-done.10.refs_2_ = bf16[192,4096]{1,0:T(8,128)(2,1)S(1)} collective-permute-done((bf16[192,4096]{1,0:T(8,128)(2,1)S(1)}, bf16[192,4096]{1,0:T(8,128)(2,1)S(1)}, u32[]{:S(2)}, u32[]{:S(2)}) %collective-permute-start.10) | collective-permute-done | bytes 1572896 | tf_op jit(solution)/shard_map/ppermute | solution.py:64
  76.3 10.2 %grads.5.refs_5_ = f32[512,4096]{1,0:T(8,128)S(1)} custom-call(bf16[192,4096]{1,0:T(8,128)(2,1)S(1)} %collective-permute-done.2.refs_0_, bf16[192,4096]{1,0:T(8,128)(2,1)S(1)} %collective-permute-done.4.refs_1_, bf16[192,4096]{1,0:T(8,128)(2,1)S(1)} %collective-permute-done.10.refs_2_, ...), custom_call_target="tpu_custom_call", output_to_operand_aliasing={{}: (5, {})} | custom-call | flops 6442450944 | bytes 6291456 | tf_op jit(solution)/shard_map/grads/pallas_call | solution.py:166
  86.5 3.7 %collective-permute-done.5.refs_0_ = bf16[192,4096]{1,0:T(8,128)(2,1)S(1)} collective-permute-done((bf16[192,4096]{1,0:T(8,128)(2,1)S(1)}, bf16[192,4096]{1,0:T(8,128)(2,1)S(1)}, u32[]{:S(2)}, u32[]{:S(2)}) %collective-permute-start.5) | collective-permute-done | bytes 1572896 | tf_op jit(solution)/shard_map/ppermute | solution.py:64
  93.1 13.9 %collective-permute-done.14.refs_2_ = bf16[192,4096]{1,0:T(8,128)(2,1)S(1)} collective-permute-done((bf16[192,4096]{1,0:T(8,128)(2,1)S(1)}, bf16[192,4096]{1,0:T(8,128)(2,1)S(1)}, u32[]{:S(2)}, u32[]{:S(2)}) %collective-permute-start.14) | collective-permute-done | bytes 1572896 | tf_op jit(solution)/shard_map/ppermute | solution.py:64
  107.0 3.0 %collective-permute-start.17 = (bf16[192,4096]{1,0:T(8,128)(2,1)S(1)}, bf16[192,4096]{1,0:T(8,128)(2,1)S(1)}, u32[]{:S(2)}, u32[]{:S(2)}) collective-permute-start(bf16[192,4096]{1,0:T(8,128)(2,1)S(1)} %collective-permute-done.15.refs_3_), channel_id=1, source_target_pairs={{0,12},{1,13},{2,14},{3,15},{4,0},{5,1},{6,2},{7,3},{8,4},{9,5},{1... | collective-permute-start | bytes 4718600 | tf_op jit(solution)/shard_map/ppermute | solution.py:64
  110.0 10.2 %grads.6.refs_3_ = f32[512,4096]{1,0:T(8,128)S(1)} custom-call(bf16[192,4096]{1,0:T(8,128)(2,1)S(1)} %collective-permute-done.5.refs_0_, bf16[192,4096]{1,0:T(8,128)(2,1)S(1)} %collective-permute-done.6.refs_1_, bf16[192,4096]{1,0:T(8,128)(2,1)S(1)} %collective-permute-done.14.refs_2_, ...), custom_call_target="tpu_custom_call", output_to_operand_aliasing={{}: (5, {})} | custom-call | flops 6442450944 | bytes 6291456 | tf_op jit(solution)/shard_map/grads/pallas_call | solution.py:166
  120.2 3.7 %collective-permute-done.12.refs_0_ = bf16[192,4096]{1,0:T(8,128)(2,1)S(1)} collective-permute-done((bf16[192,4096]{1,0:T(8,128)(2,1)S(1)}, bf16[192,4096]{1,0:T(8,128)(2,1)S(1)}, u32[]{:S(2)}, u32[]{:S(2)}) %collective-permute-start.12) | collective-permute-done | bytes 1572896 | tf_op jit(solution)/shard_map/ppermute | solution.py:64
  123.9 6.6 %grads.7.refs_4_.refs_2_ = f32[512,4096]{1,0:T(8,128)S(1)} custom-call(bf16[192,4096]{1,0:T(8,128)(2,1)S(1)} %collective-permute-done.12.refs_0_, bf16[192,4096]{1,0:T(8,128)(2,1)S(1)} %collective-permute-done.13.refs_1_, bf16[512,4096]{1,0:T(8,128)(2,1)S(1)} %bitcast.162, f32[512,4096]{1,0:T(8,128)S(1)} %grads.6.refs_3_), custom_call_target="tpu_custom_call", output_to_operand_aliasing={{}: (3, {})} | custom-call | flops 3221225472 | bytes 3145728 | tf_op jit(solution)/shard_map/grads/pallas_call | solution.py:166
  130.5 9.9 %collective-permute-done.16.refs_1_ = bf16[192,4096]{1,0:T(8,128)(2,1)S(1)} collective-permute-done((bf16[192,4096]{1,0:T(8,128)(2,1)S(1)}, bf16[192,4096]{1,0:T(8,128)(2,1)S(1)}, u32[]{:S(2)}, u32[]{:S(2)}) %collective-permute-start.16) | collective-permute-done | bytes 1572896 | tf_op jit(solution)/shard_map/ppermute | solution.py:64
  140.4 6.3 %tail_0.1 = (bf16[2,64,4096]{2,1,0:T(8,128)(2,1)S(1)}, bf16[384,4096]{1,0:T(8,128)(2,1)S(1)}, bf16[512,384]{1,0:T(8,128)(2,1)S(1)}, bf16[512,384]{1,0:T(8,128)(2,1)S(1)}) custom-call(s32[2]{0:T(128)S(1)} %pad_add_fusion.refs_0_, bf16[192,4096]{1,0:T(8,128)(2,1)S(1)} %collective-permute-done.16.refs_1_, ...), custom_call_target="tpu_custom_call" | custom-call | flops 2013265920 | bytes 6291456 | tf_op jit(solution)/shard_map/tail_0/pallas_call | solution.py:253
  149.6 4.3 %tail_1.1 = bf16[3,64,4096]{2,1,0:T(8,128)(2,1)S(1)} custom-call(s32[2]{0:T(128)S(1)} %pad_add_fusion.refs_0_, bf16[512,4096]{1,0:T(8,128)(2,1)S(1)} %bitcast.164, f32[512,4096]{1,0:T(8,128)S(1)} %grads.7.refs_4_.refs_2_, bf16[512,4096]{1,0:T(8,128)(2,1)S(1)} %bitcast.167, bf16[512,4096]{1,0:T(8,128)(2,1)S(1)} %bitcast.170, ...), custom_call_target="tpu_custom_call" | custom-call | flops 603979776 | bytes 9437184 | tf_op jit(solution)/shard_map/tail_1/pallas_call | solution.py:253
  156.3 3.2 %collective-permute-start.23 = (bf16[64,2048]{1,0:T(8,128)(2,1)S(1)}, bf16[64,2048]{1,0:T(8,128)(2,1)S(1)}, u32[]{:S(2)}, u32[]{:S(2)}) collective-permute-start(bf16[64,2048]{1,0:T(8,128)(2,1)S(1)} %get-tuple-element.76), channel_id=1, source_target_pairs={{0,48},{16,96},{32,80},{48,0},{64,112},{80,32},{96,16},{112,64},{1... | collective-permute-start | bytes 786440 | tf_op jit(solution)/shard_map/ppermute | solution.py:53
  159.5 4.3 %tail_2.1 = bf16[3,64,4096]{2,1,0:T(8,128)(2,1)S(1)} custom-call(s32[2]{0:T(128)S(1)} %pad_add_fusion.refs_0_, bf16[512,4096]{1,0:T(8,128)(2,1)S(1)} %bitcast.165, f32[512,4096]{1,0:T(8,128)S(1)} %grads.7.refs_4_.refs_2_, bf16[512,4096]{1,0:T(8,128)(2,1)S(1)} %bitcast.168, bf16[512,4096]{1,0:T(8,128)(2,1)S(1)} %bitcast.171, ...), custom_call_target="tpu_custom_call" | custom-call | flops 603979776 | bytes 9437184 | tf_op jit(solution)/shard_map/tail_2/pallas_call | solution.py:253
  171.3 18.9 %collective-permute-done.24 = bf16[2,64,4096]{2,1,0:T(8,128)(2,1)S(1)} collective-permute-done((bf16[2,64,4096]{2,1,0:T(8,128)(2,1)S(1)}, bf16[2,64,4096]{2,1,0:T(8,128)(2,1)S(1)}, u32[]{:S(2)}, u32[]{:S(2)}) %collective-permute-start.24) | collective-permute-done | bytes 1048608 | tf_op jit(solution)/shard_map/ppermute | solution.py:53
  190.1 3.5 %collective-permute-done.22 = bf16[2,64,4096]{2,1,0:T(8,128)(2,1)S(1)} collective-permute-done((bf16[2,64,4096]{2,1,0:T(8,128)(2,1)S(1)}, bf16[2,64,4096]{2,1,0:T(8,128)(2,1)S(1)}, u32[]{:S(2)}, u32[]{:S(2)}) %collective-permute-start.22) | collective-permute-done | bytes 1048608 | tf_op jit(solution)/shard_map/ppermute | solution.py:53
  198.9 20.0 %collective-permute-done.25.prv = bf16[2,64,4096]{2,1,0:T(8,128)(2,1)S(1)} collective-permute-done((bf16[2,64,4096]{2,1,0:T(8,128)(2,1)S(1)}, bf16[2,64,4096]{2,1,0:T(8,128)(2,1)S(1)}, u32[]{:S(2)}, u32[]{:S(2)}) %collective-permute-start.25) | collective-permute-done | bytes 1048608 | tf_op jit(solution)/shard_map/ppermute | solution.py:53
  218.9 3.2 %collective-permute-done.26.nxt = bf16[2,64,4096]{2,1,0:T(8,128)(2,1)S(1)} collective-permute-done((bf16[2,64,4096]{2,1,0:T(8,128)(2,1)S(1)}, bf16[2,64,4096]{2,1,0:T(8,128)(2,1)S(1)}, u32[]{:S(2)}, u32[]{:S(2)}) %collective-permute-start.26) | collective-permute-done | bytes 1048608 | tf_op jit(solution)/shard_map/ppermute | solution.py:53
  234.1 3.2 %collective-permute-done.31.other_l = bf16[64,2048]{1,0:T(8,128)(2,1)S(1)} collective-permute-done((bf16[64,2048]{1,0:T(8,128)(2,1)S(1)}, bf16[64,2048]{1,0:T(8,128)(2,1)S(1)}, u32[]{:S(2)}, u32[]{:S(2)}) %collective-permute-start.31) | collective-permute-done | bytes 262176 | tf_op jit(solution)/shard_map/ppermute | solution.py:53
  (109 shorter events, 60.3 us)
Async XLA Ops:
  0.6 25.6 %collective-permute-start.1 = (bf16[192,2048]{1,0:T(8,128)(2,1)}, bf16[192,2048]{1,0:T(8,128)(2,1)S(1)}, u32[]{:S(2)}, u32[]{:S(2)}) collective-permute-start(bf16[192,2048]{1,0:T(8,128)(2,1)} %bitcast.173), channel_id=1, source_target_pairs={{0,3},{1,0},{2,1},{3,2},{4,7},{5,4},{6,5},{7,6},{8,11},{9,8},{10,9... | collective-permute-start | bytes 2359304 | tf_op jit(solution)/shard_map/ppermute | solution.py:64
  5.3 24.6 %collective-permute-start.7 = (bf16[192,2048]{1,0:T(8,128)(2,1)}, bf16[192,2048]{1,0:T(8,128)(2,1)S(1)}, u32[]{:S(2)}, u32[]{:S(2)}) collective-permute-start(bf16[192,2048]{1,0:T(8,128)(2,1)} %bitcast.174), channel_id=1, source_target_pairs={{0,1},{1,2},{2,3},{3,0},{4,5},{5,6},{6,7},{7,4},{8,9},{9,10},{10,1... | collective-permute-start | bytes 2359304 | tf_op jit(solution)/shard_map/ppermute | solution.py:64
  5.3 21.0 %collective-permute-start = (bf16[192,2048]{1,0:T(8,128)(2,1)}, bf16[192,2048]{1,0:T(8,128)(2,1)S(1)}, u32[]{:S(2)}, u32[]{:S(2)}) collective-permute-start(bf16[192,2048]{1,0:T(8,128)(2,1)} %bitcast.176), channel_id=1, source_target_pairs={{0,1},{1,2},{2,3},{3,0},{4,5},{5,6},{6,7},{7,4},{8,9},{9,10},{10,1... | collective-permute-start | bytes 2359304 | tf_op jit(solution)/shard_map/ppermute | solution.py:64
  5.3 41.2 %collective-permute-start.3 = (bf16[192,2048]{1,0:T(8,128)(2,1)}, bf16[192,2048]{1,0:T(8,128)(2,1)S(1)}, u32[]{:S(2)}, u32[]{:S(2)}) collective-permute-start(bf16[192,2048]{1,0:T(8,128)(2,1)} %bitcast.177), channel_id=1, source_target_pairs={{0,3},{1,0},{2,1},{3,2},{4,7},{5,4},{6,5},{7,6},{8,11},{9,8},{10,9... | collective-permute-start | bytes 2359304 | tf_op jit(solution)/shard_map/ppermute | solution.py:64
  26.3 15.7 %collective-permute-start.8 = (bf16[192,2048]{1,0:T(8,128)(2,1)S(1)}, bf16[192,2048]{1,0:T(8,128)(2,1)S(1)}, u32[]{:S(2)}, u32[]{:S(2)}) collective-permute-start(bf16[192,2048]{1,0:T(8,128)(2,1)S(1)} %collective-permute-done), channel_id=1, source_target_pairs={{0,1},{1,2},{2,3},{3,0},{4,5},{5,6},{6,7},{7,4},{8,9},{9,10},{10,1... | collective-permute-start | bytes 2359304 | tf_op jit(solution)/shard_map/ppermute | solution.py:64
  26.3 15.7 %collective-permute-start.9 = (bf16[192,2048]{1,0:T(8,128)(2,1)S(1)}, bf16[192,2048]{1,0:T(8,128)(2,1)S(1)}, u32[]{:S(2)}, u32[]{:S(2)}) collective-permute-start(bf16[192,2048]{1,0:T(8,128)(2,1)S(1)} %collective-permute-done.1), channel_id=1, source_target_pairs={{0,3},{1,0},{2,1},{3,2},{4,7},{5,4},{6,5},{7,6},{8,11},{9,8},{10,9... | collective-permute-start | bytes 2359304 | tf_op jit(solution)/shard_map/ppermute | solution.py:64
  29.0 27.5 %collective-permute-start.2 = (bf16[192,4096]{1,0:T(8,128)(2,1)S(1)}, bf16[192,4096]{1,0:T(8,128)(2,1)S(1)}, u32[]{:S(2)}, u32[]{:S(2)}) collective-permute-start(bf16[192,4096]{1,0:T(8,128)(2,1)S(1)} %pad_maximum_fusion.refs_0_), channel_id=1, source_target_pairs={{0,4},{1,5},{2,6},{3,7},{4,8},{5,9},{6,10},{7,11},{8,12},{9,13},{1... | collective-permute-start | bytes 4718600 | tf_op jit(solution)/shard_map/ppermute | solution.py:64
  29.9 26.6 %collective-permute-start.4 = (bf16[192,4096]{1,0:T(8,128)(2,1)S(1)}, bf16[192,4096]{1,0:T(8,128)(2,1)S(1)}, u32[]{:S(2)}, u32[]{:S(2)}) collective-permute-start(bf16[192,4096]{1,0:T(8,128)(2,1)S(1)} %pad_maximum_fusion.refs_0_), channel_id=1, source_target_pairs={{0,12},{1,13},{2,14},{3,15},{4,0},{5,1},{6,2},{7,3},{8,4},{9,5},{1... | collective-permute-start | bytes 4718600 | tf_op jit(solution)/shard_map/ppermute | solution.py:64
  41.9 31.4 %collective-permute-start.10 = (bf16[192,4096]{1,0:T(8,128)(2,1)S(1)}, bf16[192,4096]{1,0:T(8,128)(2,1)S(1)}, u32[]{:S(2)}, u32[]{:S(2)}) collective-permute-start(bf16[192,4096]{1,0:T(8,128)(2,1)S(1)} %constant_dynamic-update-slice_fusion.2.refs_1_), channel_id=1, source_target_pairs={{0,4},{1,5},{2,6},{3,7},{4,8},{5,9},{6,10},{7,11},{8,12},{9,13},{1... | collective-permute-start | bytes 4718600 | tf_op jit(solution)/shard_map/ppermute | solution.py:64
  45.3 28.1 %collective-permute-start.11 = (bf16[192,4096]{1,0:T(8,128)(2,1)S(1)}, bf16[192,4096]{1,0:T(8,128)(2,1)S(1)}, u32[]{:S(2)}, u32[]{:S(2)}) collective-permute-start(bf16[192,4096]{1,0:T(8,128)(2,1)S(1)} %constant_dynamic-update-slice_fusion.2.refs_1_), channel_id=1, source_target_pairs={{0,12},{1,13},{2,14},{3,15},{4,0},{5,1},{6,2},{7,3},{8,4},{9,5},{1... | collective-permute-start | bytes 4718600 | tf_op jit(solution)/shard_map/ppermute | solution.py:64
  56.5 33.7 %collective-permute-start.5 = (bf16[192,4096]{1,0:T(8,128)(2,1)S(1)}, bf16[192,4096]{1,0:T(8,128)(2,1)S(1)}, u32[]{:S(2)}, u32[]{:S(2)}) collective-permute-start(bf16[192,4096]{1,0:T(8,128)(2,1)S(1)} %constant_dynamic-update-slice_fusion.refs_2_), channel_id=1, source_target_pairs={{0,4},{1,5},{2,6},{3,7},{4,8},{5,9},{6,10},{7,11},{8,12},{9,13},{1... | collective-permute-start | bytes 4718600 | tf_op jit(solution)/shard_map/ppermute | solution.py:64
  56.5 33.7 %collective-permute-start.6 = (bf16[192,4096]{1,0:T(8,128)(2,1)S(1)}, bf16[192,4096]{1,0:T(8,128)(2,1)S(1)}, u32[]{:S(2)}, u32[]{:S(2)}) collective-permute-start(bf16[192,4096]{1,0:T(8,128)(2,1)S(1)} %constant_dynamic-update-slice_fusion.refs_2_), channel_id=1, source_target_pairs={{0,12},{1,13},{2,14},{3,15},{4,0},{5,1},{6,2},{7,3},{8,4},{9,5},{1... | collective-permute-start | bytes 4718600 | tf_op jit(solution)/shard_map/ppermute | solution.py:64
  73.3 33.7 %collective-permute-start.14 = (bf16[192,4096]{1,0:T(8,128)(2,1)S(1)}, bf16[192,4096]{1,0:T(8,128)(2,1)S(1)}, u32[]{:S(2)}, u32[]{:S(2)}) collective-permute-start(bf16[192,4096]{1,0:T(8,128)(2,1)S(1)} %constant_dynamic-update-slice_fusion.4.refs_3_), channel_id=1, source_target_pairs={{0,4},{1,5},{2,6},{3,7},{4,8},{5,9},{6,10},{7,11},{8,12},{9,13},{1... | collective-permute-start | bytes 4718600 | tf_op jit(solution)/shard_map/ppermute | solution.py:64
  73.3 33.7 %collective-permute-start.15 = (bf16[192,4096]{1,0:T(8,128)(2,1)S(1)}, bf16[192,4096]{1,0:T(8,128)(2,1)S(1)}, u32[]{:S(2)}, u32[]{:S(2)}) collective-permute-start(bf16[192,4096]{1,0:T(8,128)(2,1)S(1)} %constant_dynamic-update-slice_fusion.4.refs_3_), channel_id=1, source_target_pairs={{0,12},{1,13},{2,14},{3,15},{4,0},{5,1},{6,2},{7,3},{8,4},{9,5},{1... | collective-permute-start | bytes 4718600 | tf_op jit(solution)/shard_map/ppermute | solution.py:64
  90.2 33.7 %collective-permute-start.12 = (bf16[192,4096]{1,0:T(8,128)(2,1)S(1)}, bf16[192,4096]{1,0:T(8,128)(2,1)S(1)}, u32[]{:S(2)}, u32[]{:S(2)}) collective-permute-start(bf16[192,4096]{1,0:T(8,128)(2,1)S(1)} %collective-permute-done.2.refs_0_), channel_id=1, source_target_pairs={{0,4},{1,5},{2,6},{3,7},{4,8},{5,9},{6,10},{7,11},{8,12},{9,13},{1... | collective-permute-start | bytes 4718600 | tf_op jit(solution)/shard_map/ppermute | solution.py:64
  90.2 33.7 %collective-permute-start.13 = (bf16[192,4096]{1,0:T(8,128)(2,1)S(1)}, bf16[192,4096]{1,0:T(8,128)(2,1)S(1)}, u32[]{:S(2)}, u32[]{:S(2)}) collective-permute-start(bf16[192,4096]{1,0:T(8,128)(2,1)S(1)} %collective-permute-done.6.refs_1_), channel_id=1, source_target_pairs={{0,12},{1,13},{2,14},{3,15},{4,0},{5,1},{6,2},{7,3},{8,4},{9,5},{1... | collective-permute-start | bytes 4718600 | tf_op jit(solution)/shard_map/ppermute | solution.py:64
  107.0 33.4 %collective-permute-start.16 = (bf16[192,4096]{1,0:T(8,128)(2,1)S(1)}, bf16[192,4096]{1,0:T(8,128)(2,1)S(1)}, u32[]{:S(2)}, u32[]{:S(2)}) collective-permute-start(bf16[192,4096]{1,0:T(8,128)(2,1)S(1)} %collective-permute-done.10.refs_2_), channel_id=1, source_target_pairs={{0,4},{1,5},{2,6},{3,7},{4,8},{5,9},{6,10},{7,11},{8,12},{9,13},{1... | collective-permute-start | bytes 4718600 | tf_op jit(solution)/shard_map/ppermute | solution.py:64
  107.0 33.4 %collective-permute-start.17 = (bf16[192,4096]{1,0:T(8,128)(2,1)S(1)}, bf16[192,4096]{1,0:T(8,128)(2,1)S(1)}, u32[]{:S(2)}, u32[]{:S(2)}) collective-permute-start(bf16[192,4096]{1,0:T(8,128)(2,1)S(1)} %collective-permute-done.15.refs_3_), channel_id=1, source_target_pairs={{0,12},{1,13},{2,14},{3,15},{4,0},{5,1},{6,2},{7,3},{8,4},{9,5},{1... | collective-permute-start | bytes 4718600 | tf_op jit(solution)/shard_map/ppermute | solution.py:64
  167.5 22.6 %collective-permute-start.24 = (bf16[2,64,4096]{2,1,0:T(8,128)(2,1)S(1)}, bf16[2,64,4096]{2,1,0:T(8,128)(2,1)S(1)}, u32[]{:S(2)}, u32[]{:S(2)}) collective-permute-start(bf16[2,64,4096]{2,1,0:T(8,128)(2,1)S(1)} %pad_maximum_fusion.2), channel_id=1, source_target_pairs={{0,96},{16,48},{32,0},{48,80},{64,32},{80,112},{96,64},{112,16},{1... | collective-permute-start | bytes 3145736 | tf_op jit(solution)/shard_map/ppermute | solution.py:53
  168.2 25.4 %collective-permute-start.22 = (bf16[2,64,4096]{2,1,0:T(8,128)(2,1)S(1)}, bf16[2,64,4096]{2,1,0:T(8,128)(2,1)S(1)}, u32[]{:S(2)}, u32[]{:S(2)}) collective-permute-start(bf16[2,64,4096]{2,1,0:T(8,128)(2,1)S(1)} %pad_maximum_fusion.1), channel_id=1, source_target_pairs={{0,32},{16,112},{32,64},{48,16},{64,96},{80,48},{96,0},{112,80},{1... | collective-permute-start | bytes 3145736 | tf_op jit(solution)/shard_map/ppermute | solution.py:53
  194.7 24.2 %collective-permute-start.25 = (bf16[2,64,4096]{2,1,0:T(8,128)(2,1)S(1)}, bf16[2,64,4096]{2,1,0:T(8,128)(2,1)S(1)}, u32[]{:S(2)}, u32[]{:S(2)}) collective-permute-start(bf16[2,64,4096]{2,1,0:T(8,128)(2,1)S(1)} %get-tuple-element.57.own), channel_id=1, source_target_pairs={{0,32},{16,112},{32,64},{48,16},{64,96},{80,48},{96,0},{112,80},{1... | collective-permute-start | bytes 3145736 | tf_op jit(solution)/shard_map/ppermute | solution.py:53
  197.5 24.6 %collective-permute-start.26 = (bf16[2,64,4096]{2,1,0:T(8,128)(2,1)S(1)}, bf16[2,64,4096]{2,1,0:T(8,128)(2,1)S(1)}, u32[]{:S(2)}, u32[]{:S(2)}) collective-permute-start(bf16[2,64,4096]{2,1,0:T(8,128)(2,1)S(1)} %get-tuple-element.57.own), channel_id=1, source_target_pairs={{0,96},{16,48},{32,0},{48,80},{64,32},{80,112},{96,64},{112,16},{1... | collective-permute-start | bytes 3145736 | tf_op jit(solution)/shard_map/ppermute | solution.py:53
  197.5 29.2 %collective-permute-start.27 = (bf16[64,4096]{1,0:T(8,128)(2,1)S(1)}, bf16[64,4096]{1,0:T(8,128)(2,1)S(1)}, u32[]{:S(2)}, u32[]{:S(2)}) collective-permute-start(bf16[64,4096]{1,0:T(8,128)(2,1)S(1)} %fusion.7), channel_id=1, source_target_pairs={{0,16},{16,0},{32,48},{48,32},{64,80},{80,64},{96,112},{112,96},{1... | collective-permute-start | bytes 1572872 | tf_op jit(solution)/shard_map/ppermute | solution.py:53
  222.3 15.0 %collective-permute-start.28 = (bf16[2,64,4096]{2,1,0:T(8,128)(2,1)S(1)}, bf16[2,64,4096]{2,1,0:T(8,128)(2,1)S(1)}, u32[]{:S(2)}, u32[]{:S(2)}) collective-permute-start(bf16[2,64,4096]{2,1,0:T(8,128)(2,1)S(1)} %pad_maximum_fusion.3), channel_id=1, source_target_pairs={{0,16},{16,0},{32,48},{48,32},{64,80},{80,64},{96,112},{112,96},{1... | collective-permute-start | bytes 3145736 | tf_op jit(solution)/shard_map/ppermute | solution.py:53
  (14 other events, 181.4 us)

commit v6 on v5

--- a/solution.py
+++ b/solution.py
@@ -67,13 +67,12 @@
         return jnp.concatenate([x, g], 1)
 
     x_prv, g_nxt = send(x, (0, 1)), send(g, (0, -1))
-    x_nxt, g_prv = send(x, (0, -1)), send(g, (0, 1))
+    x_nxt, g_prv = send(x, (0, -1), x_prv, g_nxt), send(g, (0, 1), x_prv, g_nxt)
     x_far, g_far = send(x_prv, (0, 1)), send(g_nxt, (0, -1))
     own = join(x, g)
     got = {(0, 0): own, (0, -1): join(x_prv, g_prv), (0, 1): join(x_nxt, g_nxt)}
     got[0, 2] = join(x_far, g_far)
-    got[-1, 0] = send(own, (1, 0), x_prv, g_nxt)
-    got[1, 0] = send(own, (-1, 0), x_prv, g_nxt)
+    got[-1, 0], got[1, 0] = send(own, (1, 0)), send(own, (-1, 0))
     got[-1, -1] = send(got[0, -1], (1, 0), x_far, g_far)
     got[1, -1] = send(got[0, -1], (-1, 0), x_far, g_far)
     hold = {3: compute(0, got)}

time: 240 us -> 243 us (1.012)
  waiting for transfers between devices: 112 us -> 118 us
  starting transfers between devices: 46.6 us -> 40.9 us
  local copies, waits for them, and re-layouts: 8.91 us -> 11.8 us
    ppermute x15, waiting for transfers between devices: 56.5 us -> 61.5 us  [on_path(): return lax.ppermute(a, 'path', path_hop(hop, flip))]
    ppermute x18, starting transfers between devices: 29.1 us -> 25.2 us  [send(): return lax.ppermute(a, ('path', 'fsdp'), plane_hop(*to))]
  transfers between devices with their start and end apart: 33 -> 33, of which waited for: 17 -> 16; matrix products, arithmetic and copies ran while one was open for 7% -> 7% of each run, Pallas kernels for 20% -> 20%
where the time goes in v6:
time: 243 us; the launch traced here: 242 us
  waiting for transfers between devices  118 us (49%)
  Pallas kernels  56.5 us (23%)
  starting transfers between devices  40.9 us (17%)
  local copies, waits for them, and re-layouts  11.8 us (5%)
  other arithmetic  7.96 us (3%)
  between operations  6.87 us (3%)
    ppermute x15, waiting for transfers between devices, on_path(): return lax.ppermute(a, 'path', path_hop(hop, flip))  61.5 us
    ppermute x18, waiting for transfers between devices, send(): return lax.ppermute(a, ('path', 'fsdp'), plane_hop(*to))  56.9 us
    pallas_call x4, Pallas kernels, accumulate(): pl.pallas_call(functools.partial(grads_kernel, n, first, features, hidden...  37.9 us
    ppermute x18, starting transfers between devices, send(): return lax.ppermute(a, ('path', 'fsdp'), plane_hop(*to))  25.2 us
    ppermute x15, starting transfers between devices, on_path(): return lax.ppermute(a, 'path', path_hop(hop, flip))  15.7 us
    pallas_call x3, Pallas kernels, tail_pseudo(): pl.pallas_call(functools.partial(pseudo_kernel, len(given), part, feature...  14.8 us
  transfers between devices with their start and end apart: 33, of which 16 were waited for; matrix products, arithmetic and copies ran while one was open for 7% of the time, Pallas kernels for 20%

profile of v6, /device:TPU:1, one launch (start us, length us, event | category | flops | bytes accessed | tf_op | source)
XLA Modules:
  0.0 242.4 jit_solution(6435469711401399568)
XLA Ops:
  26.2 14.3 %collective-permute-done.7 = bf16[192,2048]{1,0:T(8,128)(2,1)} collective-permute-done((bf16[192,2048]{1,0:T(8,128)(2,1)}, bf16[192,2048]{1,0:T(8,128)(2,1)}, u32[]{:S(2)}, u32[]{:S(2)}) %collective-permute-start.7) | collective-permute-done | bytes 786464 | tf_op jit(solution)/shard_map/ppermute | solution.py:64
  44.5 4.3 %collective-permute-done.8 = bf16[192,2048]{1,0:T(8,128)(2,1)S(1)} collective-permute-done((bf16[192,2048]{1,0:T(8,128)(2,1)}, bf16[192,2048]{1,0:T(8,128)(2,1)S(1)}, u32[]{:S(2)}, u32[]{:S(2)}) %collective-permute-start.8) | collective-permute-done | bytes 786464 | tf_op jit(solution)/shard_map/ppermute | solution.py:64
  48.9 3.0 %collective-permute-done.9 = bf16[192,2048]{1,0:T(8,128)(2,1)S(1)} collective-permute-done((bf16[192,2048]{1,0:T(8,128)(2,1)}, bf16[192,2048]{1,0:T(8,128)(2,1)S(1)}, u32[]{:S(2)}, u32[]{:S(2)}) %collective-permute-start.9) | collective-permute-done | bytes 786464 | tf_op jit(solution)/shard_map/ppermute | solution.py:64
  58.9 9.8 %grads.4.refs_5_ = f32[512,4096]{1,0:T(8,128)S(1)} custom-call(bf16[192,4096]{1,0:T(8,128)(2,1)S(1)} %pad_maximum_fusion.refs_0_, bf16[192,4096]{1,0:T(8,128)(2,1)S(1)} %constant_dynamic-update-slice_fusion.2.refs_1_, bf16[192,4096]{1,0:T(8,128)(2,1)S(1)} %constant_dynamic-update-slice_fusion.refs_2_, ...), custom_call_target="tpu_custom_call" | custom-call | flops 6442450944 | bytes 6291456 | tf_op jit(solution)/shard_map/grads/pallas_call | solution.py:165
  68.7 3.9 %collective-permute-done.10.refs_2_ = bf16[192,4096]{1,0:T(8,128)(2,1)S(1)} collective-permute-done((bf16[192,4096]{1,0:T(8,128)(2,1)S(1)}, bf16[192,4096]{1,0:T(8,128)(2,1)S(1)}, u32[]{:S(2)}, u32[]{:S(2)}) %collective-permute-start.10) | collective-permute-done | bytes 1572896 | tf_op jit(solution)/shard_map/ppermute | solution.py:64
  75.3 11.3 %grads.5.refs_5_ = f32[512,4096]{1,0:T(8,128)S(1)} custom-call(bf16[192,4096]{1,0:T(8,128)(2,1)S(1)} %collective-permute-done.refs_0_, bf16[192,4096]{1,0:T(8,128)(2,1)} %collective-permute-done.4.refs_1_, bf16[192,4096]{1,0:T(8,128)(2,1)S(1)} %collective-permute-done.10.refs_2_, ...), custom_call_target="tpu_custom_call", output_to_operand_aliasing={{}: (5, {})} | custom-call | flops 6442450944 | bytes 6291456 | tf_op jit(solution)/shard_map/grads/pallas_call | solution.py:165
  86.6 2.9 %collective-permute-done.5.refs_0_ = bf16[192,4096]{1,0:T(8,128)(2,1)S(1)} collective-permute-done((bf16[192,4096]{1,0:T(8,128)(2,1)S(1)}, bf16[192,4096]{1,0:T(8,128)(2,1)S(1)}, u32[]{:S(2)}, u32[]{:S(2)}) %collective-permute-start.5) | collective-permute-done | bytes 1572896 | tf_op jit(solution)/shard_map/ppermute | solution.py:64
  92.2 14.2 %collective-permute-done.14.refs_2_ = bf16[192,4096]{1,0:T(8,128)(2,1)S(1)} collective-permute-done((bf16[192,4096]{1,0:T(8,128)(2,1)S(1)}, bf16[192,4096]{1,0:T(8,128)(2,1)S(1)}, u32[]{:S(2)}, u32[]{:S(2)}) %collective-permute-start.14) | collective-permute-done | bytes 1572896 | tf_op jit(solution)/shard_map/ppermute | solution.py:64
  109.0 10.2 %grads.6.refs_3_ = f32[512,4096]{1,0:T(8,128)S(1)} custom-call(bf16[192,4096]{1,0:T(8,128)(2,1)S(1)} %collective-permute-done.5.refs_0_, bf16[192,4096]{1,0:T(8,128)(2,1)S(1)} %collective-permute-done.6.refs_1_, bf16[192,4096]{1,0:T(8,128)(2,1)S(1)} %collective-permute-done.14.refs_2_, ...), custom_call_target="tpu_custom_call", output_to_operand_aliasing={{}: (5, {})} | custom-call | flops 6442450944 | bytes 6291456 | tf_op jit(solution)/shard_map/grads/pallas_call | solution.py:165
  119.3 4.0 %collective-permute-done.12.refs_0_ = bf16[192,4096]{1,0:T(8,128)(2,1)S(1)} collective-permute-done((bf16[192,4096]{1,0:T(8,128)(2,1)S(1)}, bf16[192,4096]{1,0:T(8,128)(2,1)S(1)}, u32[]{:S(2)}, u32[]{:S(2)}) %collective-permute-start.12) | collective-permute-done | bytes 1572896 | tf_op jit(solution)/shard_map/ppermute | solution.py:64
  123.2 6.6 %grads.7.refs_4_.refs_2_ = f32[512,4096]{1,0:T(8,128)S(1)} custom-call(bf16[192,4096]{1,0:T(8,128)(2,1)S(1)} %collective-permute-done.12.refs_0_, bf16[192,4096]{1,0:T(8,128)(2,1)S(1)} %collective-permute-done.13.refs_1_, bf16[512,4096]{1,0:T(8,128)(2,1)S(1)} %bitcast.162, f32[512,4096]{1,0:T(8,128)S(1)} %grads.6.refs_3_), custom_call_target="tpu_custom_call", output_to_operand_aliasing={{}: (3, {})} | custom-call | flops 3221225472 | bytes 3145728 | tf_op jit(solution)/shard_map/grads/pallas_call | solution.py:165
  129.8 10.2 %collective-permute-done.16.refs_1_ = bf16[192,4096]{1,0:T(8,128)(2,1)S(1)} collective-permute-done((bf16[192,4096]{1,0:T(8,128)(2,1)S(1)}, bf16[192,4096]{1,0:T(8,128)(2,1)S(1)}, u32[]{:S(2)}, u32[]{:S(2)}) %collective-permute-start.16) | collective-permute-done | bytes 1572896 | tf_op jit(solution)/shard_map/ppermute | solution.py:64
  140.1 6.3 %tail_0.1 = (bf16[2,64,4096]{2,1,0:T(8,128)(2,1)S(1)}, bf16[384,4096]{1,0:T(8,128)(2,1)S(1)}, bf16[512,384]{1,0:T(8,128)(2,1)S(1)}, bf16[512,384]{1,0:T(8,128)(2,1)S(1)}) custom-call(s32[2]{0:T(128)S(1)} %pad_add_fusion.refs_0_, bf16[192,4096]{1,0:T(8,128)(2,1)S(1)} %collective-permute-done.16.refs_1_, ...), custom_call_target="tpu_custom_call" | custom-call | flops 2013265920 | bytes 6291456 | tf_op jit(solution)/shard_map/tail_0/pallas_call | solution.py:252
  146.4 2.8 %collective-permute-start.18 = (bf16[64,2048]{1,0:T(8,128)(2,1)S(1)}, bf16[64,2048]{1,0:T(8,128)(2,1)S(1)}, u32[]{:S(2)}, u32[]{:S(2)}) collective-permute-start(bf16[64,2048]{1,0:T(8,128)(2,1)S(1)} %get-tuple-element.80), channel_id=1, source_target_pairs={{0,32},{16,112},{32,64},{48,16},{64,96},{80,48},{96,0},{112,80},{1... | collective-permute-start | bytes 786440 | tf_op jit(solution)/shard_map/ppermute | solution.py:53
  149.3 4.3 %tail_1.1 = bf16[3,64,4096]{2,1,0:T(8,128)(2,1)S(1)} custom-call(s32[2]{0:T(128)S(1)} %pad_add_fusion.refs_0_, bf16[512,4096]{1,0:T(8,128)(2,1)S(1)} %bitcast.164, f32[512,4096]{1,0:T(8,128)S(1)} %grads.7.refs_4_.refs_2_, bf16[512,4096]{1,0:T(8,128)(2,1)S(1)} %bitcast.167, bf16[512,4096]{1,0:T(8,128)(2,1)S(1)} %bitcast.170, ...), custom_call_target="tpu_custom_call" | custom-call | flops 603979776 | bytes 9437184 | tf_op jit(solution)/shard_map/tail_1/pallas_call | solution.py:252
  153.6 4.6 %collective-permute-done.19 = bf16[64,2048]{1,0:T(8,128)(2,1)S(1)} collective-permute-done((bf16[64,2048]{1,0:T(8,128)(2,1)S(1)}, bf16[64,2048]{1,0:T(8,128)(2,1)S(1)}, u32[]{:S(2)}, u32[]{:S(2)}) %collective-permute-start.19) | collective-permute-done | bytes 262176 | tf_op jit(solution)/shard_map/ppermute | solution.py:53
  160.0 4.3 %tail_2.1 = bf16[3,64,4096]{2,1,0:T(8,128)(2,1)S(1)} custom-call(s32[2]{0:T(128)S(1)} %pad_add_fusion.refs_0_, bf16[512,4096]{1,0:T(8,128)(2,1)S(1)} %bitcast.165, f32[512,4096]{1,0:T(8,128)S(1)} %grads.7.refs_4_.refs_2_, bf16[512,4096]{1,0:T(8,128)(2,1)S(1)} %bitcast.168, bf16[512,4096]{1,0:T(8,128)(2,1)S(1)} %bitcast.171, ...), custom_call_target="tpu_custom_call" | custom-call | flops 603979776 | bytes 9437184 | tf_op jit(solution)/shard_map/tail_2/pallas_call | solution.py:252
  164.6 4.0 %collective-permute-done.23 = bf16[64,2048]{1,0:T(8,128)(2,1)S(1)} collective-permute-done((bf16[64,2048]{1,0:T(8,128)(2,1)S(1)}, bf16[64,2048]{1,0:T(8,128)(2,1)S(1)}, u32[]{:S(2)}, u32[]{:S(2)}) %collective-permute-start.23) | collective-permute-done | bytes 262176 | tf_op jit(solution)/shard_map/ppermute | solution.py:53
  170.1 2.9 %collective-permute-start.22 = (bf16[2,64,4096]{2,1,0:T(8,128)(2,1)S(1)}, bf16[2,64,4096]{2,1,0:T(8,128)(2,1)S(1)}, u32[]{:S(2)}, u32[]{:S(2)}) collective-permute-start(bf16[2,64,4096]{2,1,0:T(8,128)(2,1)S(1)} %pad_maximum_fusion.1), channel_id=1, source_target_pairs={{0,32},{16,112},{32,64},{48,16},{64,96},{80,48},{96,0},{112,80},{1... | collective-permute-start | bytes 3145736 | tf_op jit(solution)/shard_map/ppermute | solution.py:53
  173.2 20.3 %collective-permute-done.24 = bf16[2,64,4096]{2,1,0:T(8,128)(2,1)S(1)} collective-permute-done((bf16[2,64,4096]{2,1,0:T(8,128)(2,1)S(1)}, bf16[2,64,4096]{2,1,0:T(8,128)(2,1)S(1)}, u32[]{:S(2)}, u32[]{:S(2)}) %collective-permute-start.24) | collective-permute-done | bytes 1048608 | tf_op jit(solution)/shard_map/ppermute | solution.py:53
  200.8 19.3 %collective-permute-done.25.prv = bf16[2,64,4096]{2,1,0:T(8,128)(2,1)S(1)} collective-permute-done((bf16[2,64,4096]{2,1,0:T(8,128)(2,1)S(1)}, bf16[2,64,4096]{2,1,0:T(8,128)(2,1)S(1)}, u32[]{:S(2)}, u32[]{:S(2)}) %collective-permute-start.25) | collective-permute-done | bytes 1048608 | tf_op jit(solution)/shard_map/ppermute | solution.py:53
  220.1 4.1 %collective-permute-done.26.nxt = bf16[2,64,4096]{2,1,0:T(8,128)(2,1)S(1)} collective-permute-done((bf16[2,64,4096]{2,1,0:T(8,128)(2,1)S(1)}, bf16[2,64,4096]{2,1,0:T(8,128)(2,1)S(1)}, u32[]{:S(2)}, u32[]{:S(2)}) %collective-permute-start.26) | collective-permute-done | bytes 1048608 | tf_op jit(solution)/shard_map/ppermute | solution.py:53
  228.2 2.8 %fusion.6 = (f32[1,2,64,4096]{3,2,1,0:T(8,128)}, f32[1,2,64,4096]{3,2,1,0:T(8,128)}) fusion(f32[1,2,64,4096]{3,2,1,0:T(8,128)S(1)} %copy-done.4, f32[2,64,4096]{2,1,0:T(8,128)S(1)} %get-tuple-element.50, f32[2]{0:T(128)S(1)} %bitcast.186, f32[1,2,64,4096]{3,2,1,0:T(8,128)S(1)} %copy-done.5), kind=kLoop, calls=%fused_computation.12 | loop fusion | flops 3670016 | bytes 10485768 | tf_op jit(solution)/shard_map/broadcast_in_dim | solution.py:435
  234.5 5.7 %collective-permute-done.31.other_l = bf16[64,2048]{1,0:T(8,128)(2,1)S(1)} collective-permute-done((bf16[64,2048]{1,0:T(8,128)(2,1)S(1)}, bf16[64,2048]{1,0:T(8,128)(2,1)S(1)}, u32[]{:S(2)}, u32[]{:S(2)}) %collective-permute-start.31) | collective-permute-done | bytes 262176 | tf_op jit(solution)/shard_map/ppermute | solution.py:53
  (113 shorter events, 59.5 us)
Async XLA Ops:
  0.7 21.8 %collective-permute-start.1 = (bf16[192,2048]{1,0:T(8,128)(2,1)}, bf16[192,2048]{1,0:T(8,128)(2,1)}, u32[]{:S(2)}, u32[]{:S(2)}) collective-permute-start(bf16[192,2048]{1,0:T(8,128)(2,1)} %bitcast.176), channel_id=1, source_target_pairs={{0,1},{1,2},{2,3},{3,0},{4,5},{5,6},{6,7},{7,4},{8,9},{9,10},{10,1... | collective-permute-start | bytes 2359304 | tf_op jit(solution)/shard_map/ppermute | solution.py:64
  3.2 19.3 %collective-permute-start.2 = (bf16[192,2048]{1,0:T(8,128)(2,1)}, bf16[192,2048]{1,0:T(8,128)(2,1)}, u32[]{:S(2)}, u32[]{:S(2)}) collective-permute-start(bf16[192,2048]{1,0:T(8,128)(2,1)} %bitcast.173), channel_id=1, source_target_pairs={{0,3},{1,0},{2,1},{3,2},{4,7},{5,4},{6,5},{7,6},{8,11},{9,8},{10,9... | collective-permute-start | bytes 2359304 | tf_op jit(solution)/shard_map/ppermute | solution.py:64
  6.9 49.1 %collective-permute-start = (bf16[192,4096]{1,0:T(8,128)(2,1)S(1)}, bf16[192,4096]{1,0:T(8,128)(2,1)S(1)}, u32[]{:S(2)}, u32[]{:S(2)}) collective-permute-start(bf16[192,4096]{1,0:T(8,128)(2,1)S(1)} %pad_maximum_fusion.refs_0_), channel_id=1, source_target_pairs={{0,4},{1,5},{2,6},{3,7},{4,8},{5,9},{6,10},{7,11},{8,12},{9,13},{1... | collective-permute-start | bytes 4718600 | tf_op jit(solution)/shard_map/ppermute | solution.py:64
  8.1 47.9 %collective-permute-start.4 = (bf16[192,4096]{1,0:T(8,128)(2,1)S(1)}, bf16[192,4096]{1,0:T(8,128)(2,1)}, u32[]{:S(2)}, u32[]{:S(2)}) collective-permute-start(bf16[192,4096]{1,0:T(8,128)(2,1)S(1)} %pad_maximum_fusion.refs_0_), channel_id=1, source_target_pairs={{0,12},{1,13},{2,14},{3,15},{4,0},{5,1},{6,2},{7,3},{8,4},{9,5},{1... | collective-permute-start | bytes 4718600 | tf_op jit(solution)/shard_map/ppermute | solution.py:64
  22.5 18.0 %collective-permute-start.7 = (bf16[192,2048]{1,0:T(8,128)(2,1)}, bf16[192,2048]{1,0:T(8,128)(2,1)}, u32[]{:S(2)}, u32[]{:S(2)}) collective-permute-start(bf16[192,2048]{1,0:T(8,128)(2,1)} %bitcast.175), channel_id=1, source_target_pairs={{0,1},{1,2},{2,3},{3,0},{4,5},{5,6},{6,7},{7,4},{8,9},{9,10},{10,1... | collective-permute-start | bytes 2359304 | tf_op jit(solution)/shard_map/ppermute | solution.py:64
  23.6 31.0 %collective-permute-start.3 = (bf16[192,2048]{1,0:T(8,128)(2,1)}, bf16[192,2048]{1,0:T(8,128)(2,1)S(1)}, u32[]{:S(2)}, u32[]{:S(2)}) collective-permute-start(bf16[192,2048]{1,0:T(8,128)(2,1)} %bitcast.178), channel_id=1, source_target_pairs={{0,3},{1,0},{2,1},{3,2},{4,7},{5,4},{6,5},{7,6},{8,11},{9,8},{10,9... | collective-permute-start | bytes 2359304 | tf_op jit(solution)/shard_map/ppermute | solution.py:64
  26.2 22.6 %collective-permute-start.8 = (bf16[192,2048]{1,0:T(8,128)(2,1)}, bf16[192,2048]{1,0:T(8,128)(2,1)S(1)}, u32[]{:S(2)}, u32[]{:S(2)}) collective-permute-start(bf16[192,2048]{1,0:T(8,128)(2,1)} %collective-permute-done.1), channel_id=1, source_target_pairs={{0,1},{1,2},{2,3},{3,0},{4,5},{5,6},{6,7},{7,4},{8,9},{9,10},{10,1... | collective-permute-start | bytes 2359304 | tf_op jit(solution)/shard_map/ppermute | solution.py:64
  51.9 20.8 %collective-permute-start.10 = (bf16[192,4096]{1,0:T(8,128)(2,1)S(1)}, bf16[192,4096]{1,0:T(8,128)(2,1)S(1)}, u32[]{:S(2)}, u32[]{:S(2)}) collective-permute-start(bf16[192,4096]{1,0:T(8,128)(2,1)S(1)} %constant_dynamic-update-slice_fusion.2.refs_1_), channel_id=1, source_target_pairs={{0,4},{1,5},{2,6},{3,7},{4,8},{5,9},{6,10},{7,11},{8,12},{9,13},{1... | collective-permute-start | bytes 4718600 | tf_op jit(solution)/shard_map/ppermute | solution.py:64
  52.8 19.8 %collective-permute-start.11 = (bf16[192,4096]{1,0:T(8,128)(2,1)S(1)}, bf16[192,4096]{1,0:T(8,128)(2,1)S(1)}, u32[]{:S(2)}, u32[]{:S(2)}) collective-permute-start(bf16[192,4096]{1,0:T(8,128)(2,1)S(1)} %constant_dynamic-update-slice_fusion.2.refs_1_), channel_id=1, source_target_pairs={{0,12},{1,13},{2,14},{3,15},{4,0},{5,1},{6,2},{7,3},{8,4},{9,5},{1... | collective-permute-start | bytes 4718600 | tf_op jit(solution)/shard_map/ppermute | solution.py:64
  56.0 33.5 %collective-permute-start.5 = (bf16[192,4096]{1,0:T(8,128)(2,1)S(1)}, bf16[192,4096]{1,0:T(8,128)(2,1)S(1)}, u32[]{:S(2)}, u32[]{:S(2)}) collective-permute-start(bf16[192,4096]{1,0:T(8,128)(2,1)S(1)} %constant_dynamic-update-slice_fusion.refs_2_), channel_id=1, source_target_pairs={{0,4},{1,5},{2,6},{3,7},{4,8},{5,9},{6,10},{7,11},{8,12},{9,13},{1... | collective-permute-start | bytes 4718600 | tf_op jit(solution)/shard_map/ppermute | solution.py:64
  56.1 33.4 %collective-permute-start.6 = (bf16[192,4096]{1,0:T(8,128)(2,1)S(1)}, bf16[192,4096]{1,0:T(8,128)(2,1)S(1)}, u32[]{:S(2)}, u32[]{:S(2)}) collective-permute-start(bf16[192,4096]{1,0:T(8,128)(2,1)S(1)} %constant_dynamic-update-slice_fusion.refs_2_), channel_id=1, source_target_pairs={{0,12},{1,13},{2,14},{3,15},{4,0},{5,1},{6,2},{7,3},{8,4},{9,5},{1... | collective-permute-start | bytes 4718600 | tf_op jit(solution)/shard_map/ppermute | solution.py:64
  72.7 33.7 %collective-permute-start.14 = (bf16[192,4096]{1,0:T(8,128)(2,1)S(1)}, bf16[192,4096]{1,0:T(8,128)(2,1)S(1)}, u32[]{:S(2)}, u32[]{:S(2)}) collective-permute-start(bf16[192,4096]{1,0:T(8,128)(2,1)S(1)} %constant_dynamic-update-slice_fusion.4.refs_3_), channel_id=1, source_target_pairs={{0,4},{1,5},{2,6},{3,7},{4,8},{5,9},{6,10},{7,11},{8,12},{9,13},{1... | collective-permute-start | bytes 4718600 | tf_op jit(solution)/shard_map/ppermute | solution.py:64
  73.6 32.8 %collective-permute-start.15 = (bf16[192,4096]{1,0:T(8,128)(2,1)S(1)}, bf16[192,4096]{1,0:T(8,128)(2,1)S(1)}, u32[]{:S(2)}, u32[]{:S(2)}) collective-permute-start(bf16[192,4096]{1,0:T(8,128)(2,1)S(1)} %constant_dynamic-update-slice_fusion.4.refs_3_), channel_id=1, source_target_pairs={{0,12},{1,13},{2,14},{3,15},{4,0},{5,1},{6,2},{7,3},{8,4},{9,5},{1... | collective-permute-start | bytes 4718600 | tf_op jit(solution)/shard_map/ppermute | solution.py:64
  89.5 33.7 %collective-permute-start.12 = (bf16[192,4096]{1,0:T(8,128)(2,1)S(1)}, bf16[192,4096]{1,0:T(8,128)(2,1)S(1)}, u32[]{:S(2)}, u32[]{:S(2)}) collective-permute-start(bf16[192,4096]{1,0:T(8,128)(2,1)S(1)} %collective-permute-done.refs_0_), channel_id=1, source_target_pairs={{0,4},{1,5},{2,6},{3,7},{4,8},{5,9},{6,10},{7,11},{8,12},{9,13},{1... | collective-permute-start | bytes 4718600 | tf_op jit(solution)/shard_map/ppermute | solution.py:64
  90.5 32.8 %collective-permute-start.13 = (bf16[192,4096]{1,0:T(8,128)(2,1)S(1)}, bf16[192,4096]{1,0:T(8,128)(2,1)S(1)}, u32[]{:S(2)}, u32[]{:S(2)}) collective-permute-start(bf16[192,4096]{1,0:T(8,128)(2,1)S(1)} %collective-permute-done.6.refs_1_), channel_id=1, source_target_pairs={{0,12},{1,13},{2,14},{3,15},{4,0},{5,1},{6,2},{7,3},{8,4},{9,5},{1... | collective-permute-start | bytes 4718600 | tf_op jit(solution)/shard_map/ppermute | solution.py:64
  106.4 33.7 %collective-permute-start.16 = (bf16[192,4096]{1,0:T(8,128)(2,1)S(1)}, bf16[192,4096]{1,0:T(8,128)(2,1)S(1)}, u32[]{:S(2)}, u32[]{:S(2)}) collective-permute-start(bf16[192,4096]{1,0:T(8,128)(2,1)S(1)} %collective-permute-done.10.refs_2_), channel_id=1, source_target_pairs={{0,4},{1,5},{2,6},{3,7},{4,8},{5,9},{6,10},{7,11},{8,12},{9,13},{1... | collective-permute-start | bytes 4718600 | tf_op jit(solution)/shard_map/ppermute | solution.py:64
  107.3 32.8 %collective-permute-start.17 = (bf16[192,4096]{1,0:T(8,128)(2,1)S(1)}, bf16[192,4096]{1,0:T(8,128)(2,1)S(1)}, u32[]{:S(2)}, u32[]{:S(2)}) collective-permute-start(bf16[192,4096]{1,0:T(8,128)(2,1)S(1)} %collective-permute-done.15.refs_3_), channel_id=1, source_target_pairs={{0,12},{1,13},{2,14},{3,15},{4,0},{5,1},{6,2},{7,3},{8,4},{9,5},{1... | collective-permute-start | bytes 4718600 | tf_op jit(solution)/shard_map/ppermute | solution.py:64
  169.4 24.0 %collective-permute-start.24 = (bf16[2,64,4096]{2,1,0:T(8,128)(2,1)S(1)}, bf16[2,64,4096]{2,1,0:T(8,128)(2,1)S(1)}, u32[]{:S(2)}, u32[]{:S(2)}) collective-permute-start(bf16[2,64,4096]{2,1,0:T(8,128)(2,1)S(1)} %pad_maximum_fusion.2), channel_id=1, source_target_pairs={{0,96},{16,48},{32,0},{48,80},{64,32},{80,112},{96,64},{112,16},{1... | collective-permute-start | bytes 3145736 | tf_op jit(solution)/shard_map/ppermute | solution.py:53
  170.1 25.2 %collective-permute-start.22 = (bf16[2,64,4096]{2,1,0:T(8,128)(2,1)S(1)}, bf16[2,64,4096]{2,1,0:T(8,128)(2,1)S(1)}, u32[]{:S(2)}, u32[]{:S(2)}) collective-permute-start(bf16[2,64,4096]{2,1,0:T(8,128)(2,1)S(1)} %pad_maximum_fusion.1), channel_id=1, source_target_pairs={{0,32},{16,112},{32,64},{48,16},{64,96},{80,48},{96,0},{112,80},{1... | collective-permute-start | bytes 3145736 | tf_op jit(solution)/shard_map/ppermute | solution.py:53
  196.4 23.7 %collective-permute-start.25 = (bf16[2,64,4096]{2,1,0:T(8,128)(2,1)S(1)}, bf16[2,64,4096]{2,1,0:T(8,128)(2,1)S(1)}, u32[]{:S(2)}, u32[]{:S(2)}) collective-permute-start(bf16[2,64,4096]{2,1,0:T(8,128)(2,1)S(1)} %get-tuple-element.59.own), channel_id=1, source_target_pairs={{0,32},{16,112},{32,64},{48,16},{64,96},{80,48},{96,0},{112,80},{1... | collective-permute-start | bytes 3145736 | tf_op jit(solution)/shard_map/ppermute | solution.py:53
  198.0 26.2 %collective-permute-start.26 = (bf16[2,64,4096]{2,1,0:T(8,128)(2,1)S(1)}, bf16[2,64,4096]{2,1,0:T(8,128)(2,1)S(1)}, u32[]{:S(2)}, u32[]{:S(2)}) collective-permute-start(bf16[2,64,4096]{2,1,0:T(8,128)(2,1)S(1)} %get-tuple-element.59.own), channel_id=1, source_target_pairs={{0,96},{16,48},{32,0},{48,80},{64,32},{80,112},{96,64},{112,16},{1... | collective-permute-start | bytes 3145736 | tf_op jit(solution)/shard_map/ppermute | solution.py:53
  198.0 30.2 %collective-permute-start.27 = (bf16[64,4096]{1,0:T(8,128)(2,1)S(1)}, bf16[64,4096]{1,0:T(8,128)(2,1)S(1)}, u32[]{:S(2)}, u32[]{:S(2)}) collective-permute-start(bf16[64,4096]{1,0:T(8,128)(2,1)S(1)} %fusion.7), channel_id=1, source_target_pairs={{0,16},{16,0},{32,48},{48,32},{64,80},{80,64},{96,112},{112,96},{1... | collective-permute-start | bytes 1572872 | tf_op jit(solution)/shard_map/ppermute | solution.py:53
  224.4 15.7 %collective-permute-start.28 = (bf16[2,64,4096]{2,1,0:T(8,128)(2,1)S(1)}, bf16[2,64,4096]{2,1,0:T(8,128)(2,1)S(1)}, u32[]{:S(2)}, u32[]{:S(2)}) collective-permute-start(bf16[2,64,4096]{2,1,0:T(8,128)(2,1)S(1)} %pad_maximum_fusion.3), channel_id=1, source_target_pairs={{0,16},{16,0},{32,48},{48,32},{64,80},{80,64},{96,112},{112,96},{1... | collective-permute-start | bytes 3145736 | tf_op jit(solution)/shard_map/ppermute | solution.py:53
  226.6 13.5 %collective-permute-start.31 = (bf16[64,2048]{1,0:T(8,128)(2,1)S(1)}, bf16[64,2048]{1,0:T(8,128)(2,1)S(1)}, u32[]{:S(2)}, u32[]{:S(2)}) collective-permute-start(bf16[64,2048]{1,0:T(8,128)(2,1)S(1)} %get-tuple-element.75), channel_id=1, source_target_pairs={{0,48},{16,96},{32,80},{48,0},{64,112},{80,32},{96,16},{112,64},{1... | collective-permute-start | bytes 786440 | tf_op jit(solution)/shard_map/ppermute | solution.py:53
  (16 other events, 211.5 us)

commit v7 on v6

--- a/solution.py
+++ b/solution.py
@@ -73,8 +73,7 @@
     got = {(0, 0): own, (0, -1): join(x_prv, g_prv), (0, 1): join(x_nxt, g_nxt)}
     got[0, 2] = join(x_far, g_far)
     got[-1, 0], got[1, 0] = send(own, (1, 0)), send(own, (-1, 0))
-    got[-1, -1] = send(got[0, -1], (1, 0), x_far, g_far)
-    got[1, -1] = send(got[0, -1], (-1, 0), x_far, g_far)
+    got[-1, -1], got[1, -1] = send(got[0, -1], (1, 0)), send(got[0, -1], (-1, 0))
     hold = {3: compute(0, got)}
     ups = [(-1, 0), (-1, -1), (-1, 1), (-1, 2), (2, 0), (2, -1)]
     downs = [(1, 0), (1, -1), (1, 1), (1, 2), (2, 1), (2, 2)]

time: 243 us -> 237 us (0.975)
  waiting for transfers between devices: 118 us -> 108 us
  starting transfers between devices: 40.9 us -> 43.7 us
    ppermute x18, waiting for transfers between devices: 56.9 us -> 51.2 us  [send(): return lax.ppermute(a, ('path', 'fsdp'), plane_hop(*to))]
    ppermute x15, waiting for transfers between devices: 61.5 us -> 56.9 us  [on_path(): return lax.ppermute(a, 'path', path_hop(hop, flip))]
  transfers between devices with their start and end apart: 33 -> 33, of which waited for: 16 -> 22; matrix products, arithmetic and copies ran while one was open for 7% -> 8% of each run, Pallas kernels for 20% -> 20%
where the time goes in v7:
time: 237 us; the launch traced here: 235 us
  waiting for transfers between devices  108 us (46%)
  Pallas kernels  56.4 us (24%)
  starting transfers between devices  43.7 us (18%)
  local copies, waits for them, and re-layouts  12.3 us (5%)
  other arithmetic  7.93 us (3%)
  between operations  7.01 us (3%)
    ppermute x15, waiting for transfers between devices, on_path(): return lax.ppermute(a, 'path', path_hop(hop, flip))  56.9 us
    ppermute x18, waiting for transfers between devices, send(): return lax.ppermute(a, ('path', 'fsdp'), plane_hop(*to))  51.2 us
    pallas_call x4, Pallas kernels, accumulate(): pl.pallas_call(functools.partial(grads_kernel, n, first, features, hidden...  37.8 us
    ppermute x18, starting transfers between devices, send(): return lax.ppermute(a, ('path', 'fsdp'), plane_hop(*to))  26.8 us
    ppermute x15, starting transfers between devices, on_path(): return lax.ppermute(a, 'path', path_hop(hop, flip))  16.9 us
    pallas_call x3, Pallas kernels, tail_pseudo(): pl.pallas_call(functools.partial(pseudo_kernel, len(given), part, feature...  14.7 us
  transfers between devices with their start and end apart: 33, of which 22 were waited for; matrix products, arithmetic and copies ran while one was open for 8% of the time, Pallas kernels for 20%

profile of v7, /device:TPU:1, one launch (start us, length us, event | category | flops | bytes accessed | tf_op | source)
XLA Modules:
  0.0 235.4 jit_solution(9952411188323262149)
XLA Ops:
  28.2 11.2 %collective-permute-done.7 = bf16[192,2048]{1,0:T(8,128)(2,1)} collective-permute-done((bf16[192,2048]{1,0:T(8,128)(2,1)}, bf16[192,2048]{1,0:T(8,128)(2,1)}, u32[]{:S(2)}, u32[]{:S(2)}) %collective-permute-start.7) | collective-permute-done | bytes 786464 | tf_op jit(solution)/shard_map/ppermute | solution.py:64
  48.9 3.3 %collective-permute-start.6 = (bf16[192,4096]{1,0:T(8,128)(2,1)S(1)}, bf16[192,4096]{1,0:T(8,128)(2,1)S(1)}, u32[]{:S(2)}, u32[]{:S(2)}) collective-permute-start(bf16[192,4096]{1,0:T(8,128)(2,1)S(1)} %constant_dynamic-update-slice_fusion.refs_2_), channel_id=1, source_target_pairs={{0,12},{1,13},{2,14},{3,15},{4,0},{5,1},{6,2},{7,3},{8,4},{9,5},{1... | collective-permute-start | bytes 4718600 | tf_op jit(solution)/shard_map/ppermute | solution.py:64
  52.6 9.8 %grads.4.refs_5_ = f32[512,4096]{1,0:T(8,128)S(1)} custom-call(bf16[192,4096]{1,0:T(8,128)(2,1)S(1)} %pad_maximum_fusion.refs_0_, bf16[192,4096]{1,0:T(8,128)(2,1)S(1)} %constant_dynamic-update-slice_fusion.2.refs_1_, bf16[192,4096]{1,0:T(8,128)(2,1)S(1)} %constant_dynamic-update-slice_fusion.refs_2_, ...), custom_call_target="tpu_custom_call" | custom-call | flops 6442450944 | bytes 6291456 | tf_op jit(solution)/shard_map/grads/pallas_call | solution.py:164
  62.4 3.3 %collective-permute-done.8.refs_2_ = bf16[192,4096]{1,0:T(8,128)(2,1)S(1)} collective-permute-done((bf16[192,4096]{1,0:T(8,128)(2,1)S(1)}, bf16[192,4096]{1,0:T(8,128)(2,1)S(1)}, u32[]{:S(2)}, u32[]{:S(2)}) %collective-permute-start.8) | collective-permute-done | bytes 1572896 | tf_op jit(solution)/shard_map/ppermute | solution.py:64
  65.7 3.9 %collective-permute-done.9.refs_3_ = bf16[192,4096]{1,0:T(8,128)(2,1)S(1)} collective-permute-done((bf16[192,4096]{1,0:T(8,128)(2,1)S(1)}, bf16[192,4096]{1,0:T(8,128)(2,1)S(1)}, u32[]{:S(2)}, u32[]{:S(2)}) %collective-permute-start.9) | collective-permute-done | bytes 1572896 | tf_op jit(solution)/shard_map/ppermute | solution.py:64
  72.3 11.3 %grads.5.refs_5_ = f32[512,4096]{1,0:T(8,128)S(1)} custom-call(bf16[192,4096]{1,0:T(8,128)(2,1)S(1)} %collective-permute-done.refs_0_, bf16[192,4096]{1,0:T(8,128)(2,1)} %collective-permute-done.4.refs_1_, bf16[192,4096]{1,0:T(8,128)(2,1)S(1)} %collective-permute-done.8.refs_2_, ...), custom_call_target="tpu_custom_call", output_to_operand_aliasing={{}: (5, {})} | custom-call | flops 6442450944 | bytes 6291456 | tf_op jit(solution)/shard_map/grads/pallas_call | solution.py:164
  83.5 2.9 %collective-permute-done.6.refs_1_ = bf16[192,4096]{1,0:T(8,128)(2,1)S(1)} collective-permute-done((bf16[192,4096]{1,0:T(8,128)(2,1)S(1)}, bf16[192,4096]{1,0:T(8,128)(2,1)S(1)}, u32[]{:S(2)}, u32[]{:S(2)}) %collective-permute-start.6) | collective-permute-done | bytes 1572896 | tf_op jit(solution)/shard_map/ppermute | solution.py:64
  89.1 10.3 %collective-permute-done.14.refs_2_ = bf16[192,4096]{1,0:T(8,128)(2,1)S(1)} collective-permute-done((bf16[192,4096]{1,0:T(8,128)(2,1)S(1)}, bf16[192,4096]{1,0:T(8,128)(2,1)S(1)}, u32[]{:S(2)}, u32[]{:S(2)}) %collective-permute-start.14) | collective-permute-done | bytes 1572896 | tf_op jit(solution)/shard_map/ppermute | solution.py:64
  99.4 3.9 %collective-permute-done.15.refs_3_ = bf16[192,4096]{1,0:T(8,128)(2,1)S(1)} collective-permute-done((bf16[192,4096]{1,0:T(8,128)(2,1)S(1)}, bf16[192,4096]{1,0:T(8,128)(2,1)S(1)}, u32[]{:S(2)}, u32[]{:S(2)}) %collective-permute-start.15) | collective-permute-done | bytes 1572896 | tf_op jit(solution)/shard_map/ppermute | solution.py:64
  106.0 10.2 %grads.6.refs_3_ = f32[512,4096]{1,0:T(8,128)S(1)} custom-call(bf16[192,4096]{1,0:T(8,128)(2,1)S(1)} %collective-permute-done.5.refs_0_, bf16[192,4096]{1,0:T(8,128)(2,1)S(1)} %collective-permute-done.6.refs_1_, bf16[192,4096]{1,0:T(8,128)(2,1)S(1)} %collective-permute-done.14.refs_2_, ...), custom_call_target="tpu_custom_call", output_to_operand_aliasing={{}: (5, {})} | custom-call | flops 6442450944 | bytes 6291456 | tf_op jit(solution)/shard_map/grads/pallas_call | solution.py:164
  116.3 3.9 %collective-permute-done.13.refs_1_ = bf16[192,4096]{1,0:T(8,128)(2,1)S(1)} collective-permute-done((bf16[192,4096]{1,0:T(8,128)(2,1)S(1)}, bf16[192,4096]{1,0:T(8,128)(2,1)S(1)}, u32[]{:S(2)}, u32[]{:S(2)}) %collective-permute-start.13) | collective-permute-done | bytes 1572896 | tf_op jit(solution)/shard_map/ppermute | solution.py:64
  120.2 6.6 %grads.7.refs_4_.refs_2_ = f32[512,4096]{1,0:T(8,128)S(1)} custom-call(bf16[192,4096]{1,0:T(8,128)(2,1)S(1)} %collective-permute-done.12.refs_0_, bf16[192,4096]{1,0:T(8,128)(2,1)S(1)} %collective-permute-done.13.refs_1_, bf16[512,4096]{1,0:T(8,128)(2,1)S(1)} %bitcast.162, f32[512,4096]{1,0:T(8,128)S(1)} %grads.6.refs_3_), custom_call_target="tpu_custom_call", output_to_operand_aliasing={{}: (3, {})} | custom-call | flops 3221225472 | bytes 3145728 | tf_op jit(solution)/shard_map/grads/pallas_call | solution.py:164
  126.8 6.3 %collective-permute-done.16.refs_1_ = bf16[192,4096]{1,0:T(8,128)(2,1)S(1)} collective-permute-done((bf16[192,4096]{1,0:T(8,128)(2,1)S(1)}, bf16[192,4096]{1,0:T(8,128)(2,1)S(1)}, u32[]{:S(2)}, u32[]{:S(2)}) %collective-permute-start.16) | collective-permute-done | bytes 1572896 | tf_op jit(solution)/shard_map/ppermute | solution.py:64
  133.1 3.6 %collective-permute-done.17.refs_2_ = bf16[192,4096]{1,0:T(8,128)(2,1)S(1)} collective-permute-done((bf16[192,4096]{1,0:T(8,128)(2,1)S(1)}, bf16[192,4096]{1,0:T(8,128)(2,1)S(1)}, u32[]{:S(2)}, u32[]{:S(2)}) %collective-permute-start.17) | collective-permute-done | bytes 1572896 | tf_op jit(solution)/shard_map/ppermute | solution.py:64
  136.7 6.2 %tail_0.1 = (bf16[2,64,4096]{2,1,0:T(8,128)(2,1)S(1)}, bf16[384,4096]{1,0:T(8,128)(2,1)S(1)}, bf16[512,384]{1,0:T(8,128)(2,1)S(1)}, bf16[512,384]{1,0:T(8,128)(2,1)S(1)}) custom-call(s32[2]{0:T(128)S(1)} %pad_add_fusion.refs_0_, bf16[192,4096]{1,0:T(8,128)(2,1)S(1)} %collective-permute-done.16.refs_1_, ...), custom_call_target="tpu_custom_call" | custom-call | flops 2013265920 | bytes 6291456 | tf_op jit(solution)/shard_map/tail_0/pallas_call | solution.py:251
  143.0 2.9 %collective-permute-start.18 = (bf16[64,2048]{1,0:T(8,128)(2,1)S(1)}, bf16[64,2048]{1,0:T(8,128)(2,1)S(1)}, u32[]{:S(2)}, u32[]{:S(2)}) collective-permute-start(bf16[64,2048]{1,0:T(8,128)(2,1)S(1)} %get-tuple-element.78), channel_id=1, source_target_pairs={{0,32},{16,112},{32,64},{48,16},{64,96},{80,48},{96,0},{112,80},{1... | collective-permute-start | bytes 786440 | tf_op jit(solution)/shard_map/ppermute | solution.py:53
  145.9 4.3 %tail_1.1 = bf16[3,64,4096]{2,1,0:T(8,128)(2,1)S(1)} custom-call(s32[2]{0:T(128)S(1)} %pad_add_fusion.refs_0_, bf16[512,4096]{1,0:T(8,128)(2,1)S(1)} %bitcast.164, f32[512,4096]{1,0:T(8,128)S(1)} %grads.7.refs_4_.refs_2_, bf16[512,4096]{1,0:T(8,128)(2,1)S(1)} %bitcast.167, bf16[512,4096]{1,0:T(8,128)(2,1)S(1)} %bitcast.170, ...), custom_call_target="tpu_custom_call" | custom-call | flops 603979776 | bytes 9437184 | tf_op jit(solution)/shard_map/tail_1/pallas_call | solution.py:251
  154.9 4.3 %tail_2.1 = bf16[3,64,4096]{2,1,0:T(8,128)(2,1)S(1)} custom-call(s32[2]{0:T(128)S(1)} %pad_add_fusion.refs_0_, bf16[512,4096]{1,0:T(8,128)(2,1)S(1)} %bitcast.165, f32[512,4096]{1,0:T(8,128)S(1)} %grads.7.refs_4_.refs_2_, bf16[512,4096]{1,0:T(8,128)(2,1)S(1)} %bitcast.168, bf16[512,4096]{1,0:T(8,128)(2,1)S(1)} %bitcast.171, ...), custom_call_target="tpu_custom_call" | custom-call | flops 603979776 | bytes 9437184 | tf_op jit(solution)/shard_map/tail_2/pallas_call | solution.py:251
  163.7 2.9 %collective-permute-start.22 = (bf16[2,64,4096]{2,1,0:T(8,128)(2,1)S(1)}, bf16[2,64,4096]{2,1,0:T(8,128)(2,1)S(1)}, u32[]{:S(2)}, u32[]{:S(2)}) collective-permute-start(bf16[2,64,4096]{2,1,0:T(8,128)(2,1)S(1)} %pad_maximum_fusion.1), channel_id=1, source_target_pairs={{0,32},{16,112},{32,64},{48,16},{64,96},{80,48},{96,0},{112,80},{1... | collective-permute-start | bytes 3145736 | tf_op jit(solution)/shard_map/ppermute | solution.py:53
  166.8 19.2 %collective-permute-done.24 = bf16[2,64,4096]{2,1,0:T(8,128)(2,1)S(1)} collective-permute-done((bf16[2,64,4096]{2,1,0:T(8,128)(2,1)S(1)}, bf16[2,64,4096]{2,1,0:T(8,128)(2,1)S(1)}, u32[]{:S(2)}, u32[]{:S(2)}) %collective-permute-start.24) | collective-permute-done | bytes 1048608 | tf_op jit(solution)/shard_map/ppermute | solution.py:53
  186.0 2.9 %collective-permute-done.22 = bf16[2,64,4096]{2,1,0:T(8,128)(2,1)S(1)} collective-permute-done((bf16[2,64,4096]{2,1,0:T(8,128)(2,1)S(1)}, bf16[2,64,4096]{2,1,0:T(8,128)(2,1)S(1)}, u32[]{:S(2)}, u32[]{:S(2)}) %collective-permute-start.22) | collective-permute-done | bytes 1048608 | tf_op jit(solution)/shard_map/ppermute | solution.py:53
  194.5 19.4 %collective-permute-done.25.prv = bf16[2,64,4096]{2,1,0:T(8,128)(2,1)S(1)} collective-permute-done((bf16[2,64,4096]{2,1,0:T(8,128)(2,1)S(1)}, bf16[2,64,4096]{2,1,0:T(8,128)(2,1)S(1)}, u32[]{:S(2)}, u32[]{:S(2)}) %collective-permute-start.25) | collective-permute-done | bytes 1048608 | tf_op jit(solution)/shard_map/ppermute | solution.py:53
  213.9 3.7 %collective-permute-done.26.nxt = bf16[2,64,4096]{2,1,0:T(8,128)(2,1)S(1)} collective-permute-done((bf16[2,64,4096]{2,1,0:T(8,128)(2,1)S(1)}, bf16[2,64,4096]{2,1,0:T(8,128)(2,1)S(1)}, u32[]{:S(2)}, u32[]{:S(2)}) %collective-permute-start.26) | collective-permute-done | bytes 1048608 | tf_op jit(solution)/shard_map/ppermute | solution.py:53
  229.3 3.8 %collective-permute-done.31.other_l = bf16[64,2048]{1,0:T(8,128)(2,1)S(1)} collective-permute-done((bf16[64,2048]{1,0:T(8,128)(2,1)S(1)}, bf16[64,2048]{1,0:T(8,128)(2,1)S(1)}, u32[]{:S(2)}, u32[]{:S(2)}) %collective-permute-start.31) | collective-permute-done | bytes 262176 | tf_op jit(solution)/shard_map/ppermute | solution.py:53
  (113 shorter events, 68.4 us)
Async XLA Ops:
  0.7 17.6 %collective-permute-start.1 = (bf16[192,2048]{1,0:T(8,128)(2,1)}, bf16[192,2048]{1,0:T(8,128)(2,1)}, u32[]{:S(2)}, u32[]{:S(2)}) collective-permute-start(bf16[192,2048]{1,0:T(8,128)(2,1)} %bitcast.176), channel_id=1, source_target_pairs={{0,1},{1,2},{2,3},{3,0},{4,5},{5,6},{6,7},{7,4},{8,9},{9,10},{10,1... | collective-permute-start | bytes 2359304 | tf_op jit(solution)/shard_map/ppermute | solution.py:64
  3.2 15.1 %collective-permute-start.2 = (bf16[192,2048]{1,0:T(8,128)(2,1)}, bf16[192,2048]{1,0:T(8,128)(2,1)}, u32[]{:S(2)}, u32[]{:S(2)}) collective-permute-start(bf16[192,2048]{1,0:T(8,128)(2,1)} %bitcast.173), channel_id=1, source_target_pairs={{0,3},{1,0},{2,1},{3,2},{4,7},{5,4},{6,5},{7,6},{8,11},{9,8},{10,9... | collective-permute-start | bytes 2359304 | tf_op jit(solution)/shard_map/ppermute | solution.py:64
  6.9 37.5 %collective-permute-start = (bf16[192,4096]{1,0:T(8,128)(2,1)S(1)}, bf16[192,4096]{1,0:T(8,128)(2,1)S(1)}, u32[]{:S(2)}, u32[]{:S(2)}) collective-permute-start(bf16[192,4096]{1,0:T(8,128)(2,1)S(1)} %pad_maximum_fusion.refs_0_), channel_id=1, source_target_pairs={{0,4},{1,5},{2,6},{3,7},{4,8},{5,9},{6,10},{7,11},{8,12},{9,13},{1... | collective-permute-start | bytes 4718600 | tf_op jit(solution)/shard_map/ppermute | solution.py:64
  8.1 39.0 %collective-permute-start.4 = (bf16[192,4096]{1,0:T(8,128)(2,1)S(1)}, bf16[192,4096]{1,0:T(8,128)(2,1)}, u32[]{:S(2)}, u32[]{:S(2)}) collective-permute-start(bf16[192,4096]{1,0:T(8,128)(2,1)S(1)} %pad_maximum_fusion.refs_0_), channel_id=1, source_target_pairs={{0,12},{1,13},{2,14},{3,15},{4,0},{5,1},{6,2},{7,3},{8,4},{9,5},{1... | collective-permute-start | bytes 4718600 | tf_op jit(solution)/shard_map/ppermute | solution.py:64
  18.2 21.2 %collective-permute-start.7 = (bf16[192,2048]{1,0:T(8,128)(2,1)}, bf16[192,2048]{1,0:T(8,128)(2,1)}, u32[]{:S(2)}, u32[]{:S(2)}) collective-permute-start(bf16[192,2048]{1,0:T(8,128)(2,1)} %bitcast.175), channel_id=1, source_target_pairs={{0,1},{1,2},{2,3},{3,0},{4,5},{5,6},{6,7},{7,4},{8,9},{9,10},{10,1... | collective-permute-start | bytes 2359304 | tf_op jit(solution)/shard_map/ppermute | solution.py:64
  24.6 17.3 %collective-permute-start.3 = (bf16[192,2048]{1,0:T(8,128)(2,1)}, bf16[192,2048]{1,0:T(8,128)(2,1)S(1)}, u32[]{:S(2)}, u32[]{:S(2)}) collective-permute-start(bf16[192,2048]{1,0:T(8,128)(2,1)} %bitcast.178), channel_id=1, source_target_pairs={{0,3},{1,0},{2,1},{3,2},{4,7},{5,4},{6,5},{7,6},{8,11},{9,8},{10,9... | collective-permute-start | bytes 2359304 | tf_op jit(solution)/shard_map/ppermute | solution.py:64
  26.9 22.0 %collective-permute-start.10 = (bf16[192,2048]{1,0:T(8,128)(2,1)}, bf16[192,2048]{1,0:T(8,128)(2,1)S(1)}, u32[]{:S(2)}, u32[]{:S(2)}) collective-permute-start(bf16[192,2048]{1,0:T(8,128)(2,1)} %collective-permute-done.1), channel_id=1, source_target_pairs={{0,1},{1,2},{2,3},{3,0},{4,5},{5,6},{6,7},{7,4},{8,9},{9,10},{10,1... | collective-permute-start | bytes 2359304 | tf_op jit(solution)/shard_map/ppermute | solution.py:64
  39.4 13.1 %collective-permute-start.11 = (bf16[192,2048]{1,0:T(8,128)(2,1)}, bf16[192,2048]{1,0:T(8,128)(2,1)S(1)}, u32[]{:S(2)}, u32[]{:S(2)}) collective-permute-start(bf16[192,2048]{1,0:T(8,128)(2,1)} %collective-permute-done.2), channel_id=1, source_target_pairs={{0,3},{1,0},{2,1},{3,2},{4,7},{5,4},{6,5},{7,6},{8,11},{9,8},{10,9... | collective-permute-start | bytes 2359304 | tf_op jit(solution)/shard_map/ppermute | solution.py:64
  41.9 23.9 %collective-permute-start.8 = (bf16[192,4096]{1,0:T(8,128)(2,1)S(1)}, bf16[192,4096]{1,0:T(8,128)(2,1)S(1)}, u32[]{:S(2)}, u32[]{:S(2)}) collective-permute-start(bf16[192,4096]{1,0:T(8,128)(2,1)S(1)} %constant_dynamic-update-slice_fusion.2.refs_1_), channel_id=1, source_target_pairs={{0,4},{1,5},{2,6},{3,7},{4,8},{5,9},{6,10},{7,11},{8,12},{9,13},{1... | collective-permute-start | bytes 4718600 | tf_op jit(solution)/shard_map/ppermute | solution.py:64
  44.4 25.2 %collective-permute-start.9 = (bf16[192,4096]{1,0:T(8,128)(2,1)S(1)}, bf16[192,4096]{1,0:T(8,128)(2,1)S(1)}, u32[]{:S(2)}, u32[]{:S(2)}) collective-permute-start(bf16[192,4096]{1,0:T(8,128)(2,1)S(1)} %constant_dynamic-update-slice_fusion.2.refs_1_), channel_id=1, source_target_pairs={{0,12},{1,13},{2,14},{3,15},{4,0},{5,1},{6,2},{7,3},{8,4},{9,5},{1... | collective-permute-start | bytes 4718600 | tf_op jit(solution)/shard_map/ppermute | solution.py:64
  47.2 36.4 %collective-permute-start.5 = (bf16[192,4096]{1,0:T(8,128)(2,1)S(1)}, bf16[192,4096]{1,0:T(8,128)(2,1)S(1)}, u32[]{:S(2)}, u32[]{:S(2)}) collective-permute-start(bf16[192,4096]{1,0:T(8,128)(2,1)S(1)} %constant_dynamic-update-slice_fusion.refs_2_), channel_id=1, source_target_pairs={{0,4},{1,5},{2,6},{3,7},{4,8},{5,9},{6,10},{7,11},{8,12},{9,13},{1... | collective-permute-start | bytes 4718600 | tf_op jit(solution)/shard_map/ppermute | solution.py:64
  48.9 37.5 %collective-permute-start.6 = (bf16[192,4096]{1,0:T(8,128)(2,1)S(1)}, bf16[192,4096]{1,0:T(8,128)(2,1)S(1)}, u32[]{:S(2)}, u32[]{:S(2)}) collective-permute-start(bf16[192,4096]{1,0:T(8,128)(2,1)S(1)} %constant_dynamic-update-slice_fusion.refs_2_), channel_id=1, source_target_pairs={{0,12},{1,13},{2,14},{3,15},{4,0},{5,1},{6,2},{7,3},{8,4},{9,5},{1... | collective-permute-start | bytes 4718600 | tf_op jit(solution)/shard_map/ppermute | solution.py:64
  69.6 29.8 %collective-permute-start.14 = (bf16[192,4096]{1,0:T(8,128)(2,1)S(1)}, bf16[192,4096]{1,0:T(8,128)(2,1)S(1)}, u32[]{:S(2)}, u32[]{:S(2)}) collective-permute-start(bf16[192,4096]{1,0:T(8,128)(2,1)S(1)} %constant_dynamic-update-slice_fusion.4.refs_3_), channel_id=1, source_target_pairs={{0,4},{1,5},{2,6},{3,7},{4,8},{5,9},{6,10},{7,11},{8,12},{9,13},{1... | collective-permute-start | bytes 4718600 | tf_op jit(solution)/shard_map/ppermute | solution.py:64
  69.7 33.6 %collective-permute-start.15 = (bf16[192,4096]{1,0:T(8,128)(2,1)S(1)}, bf16[192,4096]{1,0:T(8,128)(2,1)S(1)}, u32[]{:S(2)}, u32[]{:S(2)}) collective-permute-start(bf16[192,4096]{1,0:T(8,128)(2,1)S(1)} %constant_dynamic-update-slice_fusion.4.refs_3_), channel_id=1, source_target_pairs={{0,12},{1,13},{2,14},{3,15},{4,0},{5,1},{6,2},{7,3},{8,4},{9,5},{1... | collective-permute-start | bytes 4718600 | tf_op jit(solution)/shard_map/ppermute | solution.py:64
  86.4 29.8 %collective-permute-start.12 = (bf16[192,4096]{1,0:T(8,128)(2,1)S(1)}, bf16[192,4096]{1,0:T(8,128)(2,1)S(1)}, u32[]{:S(2)}, u32[]{:S(2)}) collective-permute-start(bf16[192,4096]{1,0:T(8,128)(2,1)S(1)} %collective-permute-done.refs_0_), channel_id=1, source_target_pairs={{0,4},{1,5},{2,6},{3,7},{4,8},{5,9},{6,10},{7,11},{8,12},{9,13},{1... | collective-permute-start | bytes 4718600 | tf_op jit(solution)/shard_map/ppermute | solution.py:64
  86.5 33.6 %collective-permute-start.13 = (bf16[192,4096]{1,0:T(8,128)(2,1)S(1)}, bf16[192,4096]{1,0:T(8,128)(2,1)S(1)}, u32[]{:S(2)}, u32[]{:S(2)}) collective-permute-start(bf16[192,4096]{1,0:T(8,128)(2,1)S(1)} %collective-permute-done.6.refs_1_), channel_id=1, source_target_pairs={{0,12},{1,13},{2,14},{3,15},{4,0},{5,1},{6,2},{7,3},{8,4},{9,5},{1... | collective-permute-start | bytes 4718600 | tf_op jit(solution)/shard_map/ppermute | solution.py:64
  103.3 29.8 %collective-permute-start.16 = (bf16[192,4096]{1,0:T(8,128)(2,1)S(1)}, bf16[192,4096]{1,0:T(8,128)(2,1)S(1)}, u32[]{:S(2)}, u32[]{:S(2)}) collective-permute-start(bf16[192,4096]{1,0:T(8,128)(2,1)S(1)} %collective-permute-done.8.refs_2_), channel_id=1, source_target_pairs={{0,4},{1,5},{2,6},{3,7},{4,8},{5,9},{6,10},{7,11},{8,12},{9,13},{1... | collective-permute-start | bytes 4718600 | tf_op jit(solution)/shard_map/ppermute | solution.py:64
  103.4 33.3 %collective-permute-start.17 = (bf16[192,4096]{1,0:T(8,128)(2,1)S(1)}, bf16[192,4096]{1,0:T(8,128)(2,1)S(1)}, u32[]{:S(2)}, u32[]{:S(2)}) collective-permute-start(bf16[192,4096]{1,0:T(8,128)(2,1)S(1)} %collective-permute-done.15.refs_3_), channel_id=1, source_target_pairs={{0,12},{1,13},{2,14},{3,15},{4,0},{5,1},{6,2},{7,3},{8,4},{9,5},{1... | collective-permute-start | bytes 4718600 | tf_op jit(solution)/shard_map/ppermute | solution.py:64
  163.1 22.9 %collective-permute-start.24 = (bf16[2,64,4096]{2,1,0:T(8,128)(2,1)S(1)}, bf16[2,64,4096]{2,1,0:T(8,128)(2,1)S(1)}, u32[]{:S(2)}, u32[]{:S(2)}) collective-permute-start(bf16[2,64,4096]{2,1,0:T(8,128)(2,1)S(1)} %pad_maximum_fusion.2), channel_id=1, source_target_pairs={{0,96},{16,48},{32,0},{48,80},{64,32},{80,112},{96,64},{112,16},{1... | collective-permute-start | bytes 3145736 | tf_op jit(solution)/shard_map/ppermute | solution.py:53
  163.7 25.1 %collective-permute-start.22 = (bf16[2,64,4096]{2,1,0:T(8,128)(2,1)S(1)}, bf16[2,64,4096]{2,1,0:T(8,128)(2,1)S(1)}, u32[]{:S(2)}, u32[]{:S(2)}) collective-permute-start(bf16[2,64,4096]{2,1,0:T(8,128)(2,1)S(1)} %pad_maximum_fusion.1), channel_id=1, source_target_pairs={{0,32},{16,112},{32,64},{48,16},{64,96},{80,48},{96,0},{112,80},{1... | collective-permute-start | bytes 3145736 | tf_op jit(solution)/shard_map/ppermute | solution.py:53
  190.0 24.0 %collective-permute-start.25 = (bf16[2,64,4096]{2,1,0:T(8,128)(2,1)S(1)}, bf16[2,64,4096]{2,1,0:T(8,128)(2,1)S(1)}, u32[]{:S(2)}, u32[]{:S(2)}) collective-permute-start(bf16[2,64,4096]{2,1,0:T(8,128)(2,1)S(1)} %get-tuple-element.57.own), channel_id=1, source_target_pairs={{0,32},{16,112},{32,64},{48,16},{64,96},{80,48},{96,0},{112,80},{1... | collective-permute-start | bytes 3145736 | tf_op jit(solution)/shard_map/ppermute | solution.py:53
  192.8 24.9 %collective-permute-start.26 = (bf16[2,64,4096]{2,1,0:T(8,128)(2,1)S(1)}, bf16[2,64,4096]{2,1,0:T(8,128)(2,1)S(1)}, u32[]{:S(2)}, u32[]{:S(2)}) collective-permute-start(bf16[2,64,4096]{2,1,0:T(8,128)(2,1)S(1)} %get-tuple-element.57.own), channel_id=1, source_target_pairs={{0,96},{16,48},{32,0},{48,80},{64,32},{80,112},{96,64},{112,16},{1... | collective-permute-start | bytes 3145736 | tf_op jit(solution)/shard_map/ppermute | solution.py:53
  192.8 29.2 %collective-permute-start.27 = (bf16[64,4096]{1,0:T(8,128)(2,1)S(1)}, bf16[64,4096]{1,0:T(8,128)(2,1)S(1)}, u32[]{:S(2)}, u32[]{:S(2)}) collective-permute-start(bf16[64,4096]{1,0:T(8,128)(2,1)S(1)} %fusion.7), channel_id=1, source_target_pairs={{0,16},{16,0},{32,48},{48,32},{64,80},{80,64},{96,112},{112,96},{1... | collective-permute-start | bytes 1572872 | tf_op jit(solution)/shard_map/ppermute | solution.py:53
  217.9 15.3 %collective-permute-start.28 = (bf16[2,64,4096]{2,1,0:T(8,128)(2,1)S(1)}, bf16[2,64,4096]{2,1,0:T(8,128)(2,1)S(1)}, u32[]{:S(2)}, u32[]{:S(2)}) collective-permute-start(bf16[2,64,4096]{2,1,0:T(8,128)(2,1)S(1)} %pad_maximum_fusion.3), channel_id=1, source_target_pairs={{0,16},{16,0},{32,48},{48,32},{64,80},{80,64},{96,112},{112,96},{1... | collective-permute-start | bytes 3145736 | tf_op jit(solution)/shard_map/ppermute | solution.py:53
  (16 other events, 201.0 us)
